TPU v7x, 128 devices: a whole 4x4x4 slice. The times are simulated.
128 devices in a mesh: group: 4 (over z_hi, core), blk: 32 (over x, y, z_lo).
Axes of the slice: x: 4, y: 4, z: 4 (z_hi: 2, z_lo: 2; z = z_hi * 2 + z_lo), core: 2. Of those that a mesh axis runs over, the one named last changes fastest.
Arguments:
- vertex: float32 [131072, 256], P(('group', 'blk')), may hold values from -1.5 to 1.5
- vertex_state: float32 [131072], P(('group', 'blk')), may hold values from 0.1 to 1
- context: float32 [65536, 256], P(('group', 'blk')), may hold values from -1.5 to 1.5
- context_state: float32 [65536], P(('group', 'blk')), may hold values from 0.1 to 1
- tile_weights: bfloat16 [4, 32, 4, 6, 3, 128, 128], P('group', 'blk'), may hold values from 0.049804688 to 2
- tile_rows: int32 [4, 32, 4, 6, 3], P('group', 'blk'), may hold values from 0 to 7
- tile_cols: int32 [4, 32, 4, 6, 3], P('group', 'blk'), may hold values from 0 to 3
- tile_counts: int32 [4, 32, 4, 6], P('group', 'blk'), may hold values from 1 to 3, as said below
- negatives: int32 [4, 32, 6, 8, 2], P('group', 'blk'), may hold values from 0 to 3
Outputs:
- vertex_out: float32 [131072, 256], P(('group', 'blk'))
- vertex_state_out: float32 [131072], P(('group', 'blk'))
- context_out: float32 [65536, 256], P(('group', 'blk'))
- context_state_out: float32 [65536], P(('group', 'blk'))
Inputs may be any that keep to these rules, and one draw needn't show every extreme that they name: `tile_counts`: at each stop and each index of blk some destination of the group receives 3 used slots from every walk owner.
All inputs are finite; a program needn't handle non-finite values.
Results may differ from a plain program's by a relative error of at most 0.0049.
Values may be sent and summed in bfloat16 or wider, within the bound.
No kernel may reach another device: no remote copies, remote signals or barrier semaphores. Data moves between devices by JAX's collectives and lax.ppermute only.
A program may use at most 64 MiB of HBM per device.

v0:
```python
import functools

import jax
import jax.numpy as jnp
from jax import lax
from jax.experimental import pallas as pl
from jax.experimental.pallas import tpu as pltpu
from jax.sharding import PartitionSpec as P

LEARNING = 0.1
TILE = 128
F32 = jnp.float32
BF16 = jnp.bfloat16
NT = (((1,), (1,)), ((), ()))
NN = (((1,), (0,)), ((), ()))
TN = (((0,), (0,)), ((), ()))


def dot(a, b, dims):
    return lax.dot_general(a, b, dims, preferred_element_type=F32)


def eye_mask():
    return lax.broadcasted_iota(jnp.int32, (TILE, TILE), 0) == lax.broadcasted_iota(
        jnp.int32, (TILE, TILE), 1
    )


def to_column(eye, row):
    return jnp.sum(jnp.where(eye, row, 0.0), axis=1, keepdims=True)


def to_row(eye, column):
    return jnp.sum(jnp.where(eye, column, 0.0), axis=0, keepdims=True)


def adagrad(eye, rows, state_row, grad):
    width = grad.shape[1]
    state = to_column(eye, state_row) + jnp.sum(grad * grad, axis=1, keepdims=True) * (1.0 / width)
    return rows - (LEARNING * grad) * lax.rsqrt(state), to_row(eye, state)


def stack_rows(rows, height):
    which = lax.broadcasted_iota(jnp.int32, (height, TILE), 0)
    out = jnp.zeros((height, TILE), F32)
    for t, row in enumerate(rows):
        out = jnp.where(which == t, row, out)
    return out


def context_kernel(first, last, stop, *refs):
    ids_ref, neg_ref, v_ref, *refs = refs
    if first:
        c_ref, cs_ref, *refs = refs
    else:
        msg_ref, *refs = refs
    w_refs, refs = refs[:4], refs[4:]
    p_ref, *outs = refs
    *outs, wsum = outs

    rt = v_ref.shape[0] // TILE
    ctx = p_ref.shape[1]
    ct = ctx // TILE
    cap = w_refs[0].shape[0]

    wsum[...] = jnp.zeros_like(wsum)
    for src in range(4):
        for slot in range(cap):
            pair = ids_ref[src, stop, slot]
            wsum[pair] += w_refs[src][slot].astype(F32)

    if first:
        c_now = c_ref[...]
        c_bf = c_now.astype(BF16)
        states = cs_ref[...]
    else:
        c_bf = msg_ref[:ctx, :]
        c_now = c_bf.astype(F32)
        tail = msg_ref[ctx:, :].astype(F32)
        states = tail[:, :TILE] + tail[:, TILE:]

    for r in range(rt):
        rows = pl.ds(r * TILE, TILE)
        v_tile = v_ref[rows, :].astype(BF16)
        t_val = jnp.tanh(0.5 * dot(v_tile, c_bf, NT))
        for c in range(ct):
            cols = slice(c * TILE, (c + 1) * TILE)
            count = jnp.int32(0)
            for k in range(neg_ref.shape[2]):
                count += (neg_ref[stop, r, k] == c).astype(jnp.int32)
            q = 0.25 * count.astype(F32)
            half = 0.5 * wsum[r * ct + c]
            tt = t_val[:, cols]
            p_ref[rows, cols] = (half * (tt - 1.0) + q * (tt + 1.0)).astype(BF16)

    grad = dot(p_ref[...], v_ref[...].astype(BF16), TN)
    eye = eye_mask()
    new_states = []
    for c in range(ct):
        rows = slice(c * TILE, (c + 1) * TILE)
        new_rows, new_state = adagrad(eye, c_now[rows], states[c : c + 1], grad[rows])
        new_states.append(new_state)
        if last:
            outs[0][rows, :] = new_rows
            outs[1][c : c + 1, :] = new_state
        else:
            outs[0][rows, :] = new_rows.astype(BF16)
    if not last:
        block = stack_rows(new_states, outs[0].shape[0] - ctx)
        hi = block.astype(BF16)
        outs[0][ctx:, :TILE] = hi
        outs[0][ctx:, TILE:] = (block - hi.astype(F32)).astype(BF16)


def vertex_kernel(last, p_ref, c_ref, v_ref, vs_ref, vout_ref, vsout_ref, *more):
    ctx = p_ref.shape[1]
    c_bf = c_ref[:ctx, :].astype(BF16)
    eye = eye_mask()
    for r in range(v_ref.shape[0] // TILE):
        rows = pl.ds(r * TILE, TILE)
        grad = dot(p_ref[rows, :], c_bf, NN)
        new_rows, new_state = adagrad(eye, v_ref[rows, :], vs_ref[r : r + 1, :], grad)
        vout_ref[rows, :] = new_rows
        vsout_ref[r : r + 1, :] = new_state
        if not last:
            more[0][rows, :] = new_rows.astype(BF16)


VM = pl.BlockSpec(memory_space=pltpu.VMEM)
SM = pl.BlockSpec(memory_space=pltpu.SMEM)


def context_call(stop, first, last, ids, neg, v, context, weights):
    rt = v.shape[0] // TILE
    ctx = context[0].shape[0] if first else context[0].shape[0] - 16
    width = v.shape[1]
    pairs = rt * (ctx // TILE)
    if last:
        outs = [((ctx, width), F32), ((ctx // TILE, TILE), F32)]
    else:
        outs = [((ctx + 16, width), BF16)]
    outs = [((v.shape[0], ctx), BF16)] + outs
    args = (ids, neg, v, *context, *weights)
    return pl.pallas_call(
        functools.partial(context_kernel, first, last, stop),
        out_shape=[jax.ShapeDtypeStruct(s, d) for s, d in outs],
        in_specs=[SM, SM] + [VM] * (len(args) - 2),
        out_specs=[VM] * len(outs),
        scratch_shapes=[pltpu.VMEM((pairs + 1, TILE, TILE), F32)],
        compiler_params=pltpu.CompilerParams(vmem_limit_bytes=24 << 20),
        cost_estimate=pl.CostEstimate(
            flops=4 * v.shape[0] * ctx * width, bytes_accessed=4 << 20, transcendentals=v.shape[0] * ctx
        ),
        name="context_%d" % stop,
    )(*args)


def vertex_call(stop, last, p, c, v, vs):
    outs = [(v.shape, F32), (vs.shape, F32)]
    if not last:
        outs.append((v.shape, BF16))
    return pl.pallas_call(
        functools.partial(vertex_kernel, last),
        out_shape=[jax.ShapeDtypeStruct(s, d) for s, d in outs],
        in_specs=[VM] * 4,
        out_specs=[VM] * len(outs),
        compiler_params=pltpu.CompilerParams(vmem_limit_bytes=24 << 20),
        cost_estimate=pl.CostEstimate(
            flops=2 * v.shape[0] * c.shape[0] * v.shape[1], bytes_accessed=4 << 20, transcendentals=v.shape[0]
        ),
        name="vertex_%d" % stop,
    )(p, c, v, vs)


def shifted(value, axis, by):
    peers = lax.axis_size(axis)
    return lax.ppermute(value, axis, [(i, (i + by) % peers) for i in range(peers)])


def swapped(value, by):
    peers = lax.axis_size("group")
    return lax.ppermute(value, "group", [(i, i ^ by) for i in range(peers)])


def body(vertex, vertex_state, context, context_state, tile_weights, tile_rows, tile_cols, tile_counts, negatives):
    weights = tile_weights[0, 0]
    groups, stops, cap = weights.shape[:3]
    rt, ct = vertex.shape[0] // TILE, context.shape[0] // TILE
    me = lax.axis_index("group")

    valid = jnp.arange(cap)[None, None, :] < tile_counts[0, 0][..., None]
    codes = jnp.where(valid, tile_rows[0, 0] * ct + tile_cols[0, 0], rt * ct).astype(jnp.int32)

    def mine(array, by):
        return lax.dynamic_index_in_dim(array, me ^ by, 0, keepdims=False)

    ids = [mine(codes, 0)] + [swapped(mine(codes, by), by) for by in range(1, groups)]
    ids = jnp.stack(ids)
    neg = negatives[0, 0]

    def exchanged(stop):
        out = []
        for by in range(groups):
            piece = lax.dynamic_slice(
                weights, (me ^ by, stop, 0, 0, 0), (1, 1, cap, TILE, TILE)
            ).reshape(cap, TILE, TILE)
            out.append(swapped(piece, by) if by else piece)
        return out

    arrived = [exchanged(stop) for stop in range(stops)]
    v, vs = vertex, vertex_state.reshape(rt, TILE)
    v_bf = vertex
    held = (context, context_state.reshape(ct, TILE))
    for stop in range(stops):
        first, last = stop == 0, stop == stops - 1
        p, *new = context_call(stop, first, last, ids, neg, v_bf, held, arrived[stop])
        if not last:
            sent = shifted(new[0], "blk", 1)
        v, vs, *rest = vertex_call(stop, last, p, held[0], v, vs)
        if not last:
            v_bf = rest[0]
            held = (sent,)
    return v, vs.reshape(-1), new[0], new[1].reshape(-1)


def solution(mesh):
    in_specs = (
        P(("group", "blk"), None),
        P(("group", "blk")),
        P(("group", "blk"), None),
        P(("group", "blk")),
        P("group", "blk", None, None, None, None, None),
        P("group", "blk", None, None, None),
        P("group", "blk", None, None, None),
        P("group", "blk", None, None),
        P("group", "blk", None, None, None),
    )
    out_specs = (
        P(("group", "blk"), None),
        P(("group", "blk")),
        P(("group", "blk"), None),
        P(("group", "blk")),
    )
    return jax.shard_map(body, mesh=mesh, in_specs=in_specs, out_specs=out_specs, check_vma=False)
```

profile of v0, /device:TPU:0, one launch (start us, length us, event | category | flops | bytes accessed | tf_op | source)
XLA Modules:
  0.0 112.1 jit_solution(16238082400777611813)
XLA Ops:
  2.4 4.0 %collective-permute-start.1 = (s32[6,3]{0,1:T(4,128)S(1)}, s32[6,3]{0,1:T(4,128)S(1)}, u32[]{:S(2)}, u32[]{:S(2)}) collective-permute-start(s32[6,3]{0,1:T(4,128)S(1)} %bitcast.67), channel_id=1, source_target_pairs={{0,64},{32,96},{64,0},{96,32},{1,65},{33,97},{65,1},{97,33},{2,66}... | collective-permute-start | bytes 224 | tf_op jit(solution)/shard_map/ppermute | solution.py:182
  6.7 2.8 %dynamic-slice_bitcast_fusion = (bf16[3,128,128]{2,1,0:T(8,128)(2,1)S(1)}, bf16[3,128,128]{2,1,0:T(8,128)(2,1)S(1)}, bf16[3,128,128]{2,1,0:T(8,128)(2,1)S(1)}, b...) fusion(bf16[1,1,4,6,3,128,128]{6,5,4,3,2,1,0:T(8,128)(2,1)} %pa, ...), kind=kLoop, calls=%fused_computation | loop fusion | bytes 4718608 | tf_op jit(solution)/shard_map/reshape | solution.py:206
  9.5 3.1 %collective-permute-start.5 = (bf16[3,128,128]{2,1,0:T(8,128)(2,1)}, bf16[3,128,128]{2,1,0:T(8,128)(2,1)S(1)}, u32[]{:S(2)}, u32[]{:S(2)}) collective-permute-start(bf16[3,128,128]{2,1,0:T(8,128)(2,1)} %get-tuple-element.83), channel_id=1, source_target_pairs={{0,96},{32,64},{64,32},{96,0},{1,97},{33,65},{65,33},{97,1},{2,98}... | collective-permute-start | bytes 294920 | tf_op jit(solution)/shard_map/ppermute | solution.py:182
  13.4 2.7 %collective-permute-done.5.refs_8_ = bf16[3,128,128]{2,1,0:T(8,128)(2,1)S(1)} collective-permute-done((bf16[3,128,128]{2,1,0:T(8,128)(2,1)}, bf16[3,128,128]{2,1,0:T(8,128)(2,1)S(1)}, u32[]{:S(2)}, u32[]{:S(2)}) %collective-permute-start.5) | collective-permute-done | bytes 98336 | tf_op jit(solution)/shard_map/ppermute | solution.py:182
  16.0 3.2 %collective-permute-done.4.refs_7_ = bf16[3,128,128]{2,1,0:T(8,128)(2,1)S(1)} collective-permute-done((bf16[3,128,128]{2,1,0:T(8,128)(2,1)}, bf16[3,128,128]{2,1,0:T(8,128)(2,1)S(1)}, u32[]{:S(2)}, u32[]{:S(2)}) %collective-permute-start.4) | collective-permute-done | bytes 98336 | tf_op jit(solution)/shard_map/ppermute | solution.py:182
  19.2 2.8 %context_0.1 = (bf16[1024,512]{1,0:T(8,128)(2,1)S(1)}, bf16[528,256]{1,0:T(8,128)(2,1)S(1)}) custom-call(s32[4,6,3]{2,1,0:T(8,128)S(1)} %pad_add_fusion.refs_0_, s32[6,8,2]{2,1,0:T(8,128)S(1)} %copy.53.refs_1_, f32[1024,256]{1,0:T(8,128)S(1)} %copy-done, f32[512,256]{1,0:T(8,128)S(1)} %copy-done.1, f32[4,128]{1,0:T(4,128)S(1)} %bitcast.63, ...), custom_call_target="tpu_custom_call" | custom-call | flops 536870912 | bytes 4194304 | tf_op jit(solution)/shard_map/context_0/pallas_call | solution.py:144
  23.1 2.0 %collective-permute-start.9 = (bf16[3,128,128]{2,1,0:T(8,128)(2,1)}, bf16[3,128,128]{2,1,0:T(8,128)(2,1)S(1)}, u32[]{:S(2)}, u32[]{:S(2)}) collective-permute-start(bf16[3,128,128]{2,1,0:T(8,128)(2,1)} %get-tuple-element.79), channel_id=1, source_target_pairs={{0,96},{32,64},{64,32},{96,0},{1,97},{33,65},{65,33},{97,1},{2,98}... | collective-permute-start | bytes 294920 | tf_op jit(solution)/shard_map/ppermute | solution.py:182
  27.1 5.9 %collective-permute-done.9.refs_7_ = bf16[3,128,128]{2,1,0:T(8,128)(2,1)S(1)} collective-permute-done((bf16[3,128,128]{2,1,0:T(8,128)(2,1)}, bf16[3,128,128]{2,1,0:T(8,128)(2,1)S(1)}, u32[]{:S(2)}, u32[]{:S(2)}) %collective-permute-start.9) | collective-permute-done | bytes 98336 | tf_op jit(solution)/shard_map/ppermute | solution.py:182
  33.0 3.4 %collective-permute-done.8.refs_6_ = bf16[3,128,128]{2,1,0:T(8,128)(2,1)S(1)} collective-permute-done((bf16[3,128,128]{2,1,0:T(8,128)(2,1)}, bf16[3,128,128]{2,1,0:T(8,128)(2,1)S(1)}, u32[]{:S(2)}, u32[]{:S(2)}) %collective-permute-start.8) | collective-permute-done | bytes 98336 | tf_op jit(solution)/shard_map/ppermute | solution.py:182
  36.4 2.7 %context_1.1 = (bf16[1024,512]{1,0:T(8,128)(2,1)S(1)}, bf16[528,256]{1,0:T(8,128)(2,1)S(1)}) custom-call(s32[4,6,3]{2,1,0:T(8,128)S(1)} %pad_add_fusion.refs_0_, s32[6,8,2]{2,1,0:T(8,128)S(1)} %copy.53.refs_1_, bf16[1024,256]{1,0:T(8,128)(2,1)S(1)} %get-tuple-element.35.refs_2_, bf16[528,256]{1,0:T(8,128)(2,1)S(1)} %collective-permute-done.6.refs_3_.c_ref, ...), custom_call_target="tpu_custom_call" | custom-call | flops 536870912 | bytes 4194304 | tf_op jit(solution)/shard_map/context_1/pallas_call | solution.py:144
  39.1 2.4 %collective-permute-start.10 = (bf16[528,256]{1,0:T(8,128)(2,1)S(1)}, bf16[528,256]{1,0:T(8,128)(2,1)S(1)}, u32[]{:S(2)}, u32[]{:S(2)}) collective-permute-start(bf16[528,256]{1,0:T(8,128)(2,1)S(1)} %get-tuple-element.41), channel_id=1, source_target_pairs={{0,1},{1,2},{2,3},{3,4},{4,5},{5,6},{6,7},{7,8},{8,9},{9,10},{10,1... | collective-permute-start | bytes 811016 | tf_op jit(solution)/shard_map/ppermute | solution.py:177
  41.6 2.2 %collective-permute-start.13 = (bf16[3,128,128]{2,1,0:T(8,128)(2,1)S(1)}, bf16[3,128,128]{2,1,0:T(8,128)(2,1)S(1)}, u32[]{:S(2)}, u32[]{:S(2)}) collective-permute-start(bf16[3,128,128]{2,1,0:T(8,128)(2,1)S(1)} %copy-done.5), channel_id=1, source_target_pairs={{0,96},{32,64},{64,32},{96,0},{1,97},{33,65},{65,33},{97,1},{2,98}... | collective-permute-start | bytes 294920 | tf_op jit(solution)/shard_map/ppermute | solution.py:182
  45.6 6.5 %collective-permute-done.13.refs_7_ = bf16[3,128,128]{2,1,0:T(8,128)(2,1)S(1)} collective-permute-done((bf16[3,128,128]{2,1,0:T(8,128)(2,1)S(1)}, bf16[3,128,128]{2,1,0:T(8,128)(2,1)S(1)}, u32[]{:S(2)}, u32[]{:S(2)}) %collective-permute-start.13) | collective-permute-done | bytes 98336 | tf_op jit(solution)/shard_map/ppermute | solution.py:182
  52.1 2.9 %collective-permute-done.12.refs_6_ = bf16[3,128,128]{2,1,0:T(8,128)(2,1)S(1)} collective-permute-done((bf16[3,128,128]{2,1,0:T(8,128)(2,1)S(1)}, bf16[3,128,128]{2,1,0:T(8,128)(2,1)S(1)}, u32[]{:S(2)}, u32[]{:S(2)}) %collective-permute-start.12) | collective-permute-done | bytes 98336 | tf_op jit(solution)/shard_map/ppermute | solution.py:182
  55.1 2.7 %context_2.1 = (bf16[1024,512]{1,0:T(8,128)(2,1)S(1)}, bf16[528,256]{1,0:T(8,128)(2,1)S(1)}) custom-call(s32[4,6,3]{2,1,0:T(8,128)S(1)} %pad_add_fusion.refs_0_, s32[6,8,2]{2,1,0:T(8,128)S(1)} %copy.53.refs_1_, bf16[1024,256]{1,0:T(8,128)(2,1)S(1)} %get-tuple-element.40.refs_2_, bf16[528,256]{1,0:T(8,128)(2,1)S(1)} %collective-permute-done.10.refs_3_.c_ref, ...), custom_call_target="tpu_custom_call" | custom-call | flops 536870912 | bytes 4194304 | tf_op jit(solution)/shard_map/context_2/pallas_call | solution.py:144
  63.2 5.7 %collective-permute-done.17.refs_7_ = bf16[3,128,128]{2,1,0:T(8,128)(2,1)S(1)} collective-permute-done((bf16[3,128,128]{2,1,0:T(8,128)(2,1)S(1)}, bf16[3,128,128]{2,1,0:T(8,128)(2,1)S(1)}, u32[]{:S(2)}, u32[]{:S(2)}) %collective-permute-start.17) | collective-permute-done | bytes 98336 | tf_op jit(solution)/shard_map/ppermute | solution.py:182
  68.9 3.3 %collective-permute-done.16.refs_6_ = bf16[3,128,128]{2,1,0:T(8,128)(2,1)S(1)} collective-permute-done((bf16[3,128,128]{2,1,0:T(8,128)(2,1)S(1)}, bf16[3,128,128]{2,1,0:T(8,128)(2,1)S(1)}, u32[]{:S(2)}, u32[]{:S(2)}) %collective-permute-start.16) | collective-permute-done | bytes 98336 | tf_op jit(solution)/shard_map/ppermute | solution.py:182
  72.2 2.7 %context_3.1 = (bf16[1024,512]{1,0:T(8,128)(2,1)S(1)}, bf16[528,256]{1,0:T(8,128)(2,1)S(1)}) custom-call(s32[4,6,3]{2,1,0:T(8,128)S(1)} %pad_add_fusion.refs_0_, s32[6,8,2]{2,1,0:T(8,128)S(1)} %copy.53.refs_1_, bf16[1024,256]{1,0:T(8,128)(2,1)S(1)} %get-tuple-element.45.refs_2_, bf16[528,256]{1,0:T(8,128)(2,1)S(1)} %collective-permute-done.14.refs_3_.c_ref, ...), custom_call_target="tpu_custom_call" | custom-call | flops 536870912 | bytes 4194304 | tf_op jit(solution)/shard_map/context_3/pallas_call | solution.py:144
  80.6 6.4 %collective-permute-done.21.refs_7_ = bf16[3,128,128]{2,1,0:T(8,128)(2,1)S(1)} collective-permute-done((bf16[3,128,128]{2,1,0:T(8,128)(2,1)S(1)}, bf16[3,128,128]{2,1,0:T(8,128)(2,1)S(1)}, u32[]{:S(2)}, u32[]{:S(2)}) %collective-permute-start.21) | collective-permute-done | bytes 98336 | tf_op jit(solution)/shard_map/ppermute | solution.py:182
  86.9 2.9 %collective-permute-done.20.refs_6_ = bf16[3,128,128]{2,1,0:T(8,128)(2,1)S(1)} collective-permute-done((bf16[3,128,128]{2,1,0:T(8,128)(2,1)S(1)}, bf16[3,128,128]{2,1,0:T(8,128)(2,1)S(1)}, u32[]{:S(2)}, u32[]{:S(2)}) %collective-permute-start.20) | collective-permute-done | bytes 98336 | tf_op jit(solution)/shard_map/ppermute | solution.py:182
  89.9 2.7 %context_4.1 = (bf16[1024,512]{1,0:T(8,128)(2,1)S(1)}, bf16[528,256]{1,0:T(8,128)(2,1)S(1)}) custom-call(s32[4,6,3]{2,1,0:T(8,128)S(1)} %pad_add_fusion.refs_0_, s32[6,8,2]{2,1,0:T(8,128)S(1)} %copy.53.refs_1_, bf16[1024,256]{1,0:T(8,128)(2,1)S(1)} %get-tuple-element.50.refs_2_, bf16[528,256]{1,0:T(8,128)(2,1)S(1)} %collective-permute-done.18.refs_3_.c_ref, ...), custom_call_target="tpu_custom_call" | custom-call | flops 536870912 | bytes 4194304 | tf_op jit(solution)/shard_map/context_4/pallas_call | solution.py:144
  98.3 5.4 %collective-permute-done.25.refs_7_ = bf16[3,128,128]{2,1,0:T(8,128)(2,1)S(1)} collective-permute-done((bf16[3,128,128]{2,1,0:T(8,128)(2,1)S(1)}, bf16[3,128,128]{2,1,0:T(8,128)(2,1)S(1)}, u32[]{:S(2)}, u32[]{:S(2)}) %collective-permute-start.25) | collective-permute-done | bytes 98336 | tf_op jit(solution)/shard_map/ppermute | solution.py:182
  103.7 3.3 %collective-permute-done.24.refs_6_ = bf16[3,128,128]{2,1,0:T(8,128)(2,1)S(1)} collective-permute-done((bf16[3,128,128]{2,1,0:T(8,128)(2,1)S(1)}, bf16[3,128,128]{2,1,0:T(8,128)(2,1)S(1)}, u32[]{:S(2)}, u32[]{:S(2)}) %collective-permute-start.24) | collective-permute-done | bytes 98336 | tf_op jit(solution)/shard_map/ppermute | solution.py:182
  107.0 3.5 %context_5.1 = (bf16[1024,512]{1,0:T(8,128)(2,1)S(1)}, f32[512,256]{1,0:T(8,128)}, f32[4,128]{1,0:T(4,128)}) custom-call(s32[4,6,3]{2,1,0:T(8,128)S(1)} %pad_add_fusion.refs_0_, s32[6,8,2]{2,1,0:T(8,128)S(1)} %copy.53.refs_1_, bf16[1024,256]{1,0:T(8,128)(2,1)S(1)} %get-tuple-element.55.refs_2_, bf16[528,256]{1,0:T(8,128)(2,1)S(1)} %collective-permute-done.22.refs_3_.c_ref, ...), custom_call_target="tpu_custom_call" | custom-call | flops 536870912 | bytes 4194304 | tf_op jit(solution)/shard_map/context_5/pallas_call | solution.py:144
  (67 shorter events, 25.9 us)
Async XLA Ops:
  2.3 10.6 %collective-permute-start = (s32[6,3]{0,1:T(4,128)S(1)}, s32[6,3]{0,1:T(4,128)S(1)}, u32[]{:S(2)}, u32[]{:S(2)}) collective-permute-start(s32[6,3]{0,1:T(4,128)S(1)} %bitcast.71), channel_id=1, source_target_pairs={{0,32},{32,0},{64,96},{96,64},{1,33},{33,1},{65,97},{97,65},{2,34}... | collective-permute-start | bytes 224 | tf_op jit(solution)/shard_map/ppermute | solution.py:182
  2.4 10.7 %collective-permute-start.1 = (s32[6,3]{0,1:T(4,128)S(1)}, s32[6,3]{0,1:T(4,128)S(1)}, u32[]{:S(2)}, u32[]{:S(2)}) collective-permute-start(s32[6,3]{0,1:T(4,128)S(1)} %bitcast.67), channel_id=1, source_target_pairs={{0,64},{32,96},{64,0},{96,32},{1,65},{33,97},{65,1},{97,33},{2,66}... | collective-permute-start | bytes 224 | tf_op jit(solution)/shard_map/ppermute | solution.py:182
  6.5 6.8 %collective-permute-start.2 = (s32[6,3]{0,1:T(4,128)S(1)}, s32[6,3]{0,1:T(4,128)S(1)}, u32[]{:S(2)}, u32[]{:S(2)}) collective-permute-start(s32[6,3]{0,1:T(4,128)S(1)} %bitcast.69), channel_id=1, source_target_pairs={{0,96},{32,64},{64,32},{96,0},{1,97},{33,65},{65,33},{97,1},{2,98}... | collective-permute-start | bytes 224 | tf_op jit(solution)/shard_map/ppermute | solution.py:182
  12.6 6.6 %collective-permute-start.4 = (bf16[3,128,128]{2,1,0:T(8,128)(2,1)}, bf16[3,128,128]{2,1,0:T(8,128)(2,1)S(1)}, u32[]{:S(2)}, u32[]{:S(2)}) collective-permute-start(bf16[3,128,128]{2,1,0:T(8,128)(2,1)} %get-tuple-element.84), channel_id=1, source_target_pairs={{0,64},{32,96},{64,0},{96,32},{1,65},{33,97},{65,1},{97,33},{2,66}... | collective-permute-start | bytes 294920 | tf_op jit(solution)/shard_map/ppermute | solution.py:182
  22.0 14.4 %collective-permute-start.6 = (bf16[528,256]{1,0:T(8,128)(2,1)S(1)}, bf16[528,256]{1,0:T(8,128)(2,1)S(1)}, u32[]{:S(2)}, u32[]{:S(2)}) collective-permute-start(bf16[528,256]{1,0:T(8,128)(2,1)S(1)} %get-tuple-element.36), channel_id=1, source_target_pairs={{0,1},{1,2},{2,3},{3,4},{4,5},{5,6},{6,7},{7,8},{8,9},{9,10},{10,1... | collective-permute-start | bytes 811016 | tf_op jit(solution)/shard_map/ppermute | solution.py:177
  23.1 9.9 %collective-permute-start.9 = (bf16[3,128,128]{2,1,0:T(8,128)(2,1)}, bf16[3,128,128]{2,1,0:T(8,128)(2,1)S(1)}, u32[]{:S(2)}, u32[]{:S(2)}) collective-permute-start(bf16[3,128,128]{2,1,0:T(8,128)(2,1)} %get-tuple-element.79), channel_id=1, source_target_pairs={{0,96},{32,64},{64,32},{96,0},{1,97},{33,65},{65,33},{97,1},{2,98}... | collective-permute-start | bytes 294920 | tf_op jit(solution)/shard_map/ppermute | solution.py:182
  25.2 11.2 %collective-permute-start.8 = (bf16[3,128,128]{2,1,0:T(8,128)(2,1)}, bf16[3,128,128]{2,1,0:T(8,128)(2,1)S(1)}, u32[]{:S(2)}, u32[]{:S(2)}) collective-permute-start(bf16[3,128,128]{2,1,0:T(8,128)(2,1)} %get-tuple-element.80), channel_id=1, source_target_pairs={{0,64},{32,96},{64,0},{96,32},{1,65},{33,97},{65,1},{97,33},{2,66}... | collective-permute-start | bytes 294920 | tf_op jit(solution)/shard_map/ppermute | solution.py:182
  26.1 10.3 %collective-permute-start.7 = (bf16[3,128,128]{2,1,0:T(8,128)(2,1)}, bf16[3,128,128]{2,1,0:T(8,128)(2,1)S(1)}, u32[]{:S(2)}, u32[]{:S(2)}) collective-permute-start(bf16[3,128,128]{2,1,0:T(8,128)(2,1)} %get-tuple-element.81), channel_id=1, source_target_pairs={{0,32},{32,0},{64,96},{96,64},{1,33},{33,1},{65,97},{97,65},{2,34}... | collective-permute-start | bytes 294920 | tf_op jit(solution)/shard_map/ppermute | solution.py:182
  39.1 15.9 %collective-permute-start.10 = (bf16[528,256]{1,0:T(8,128)(2,1)S(1)}, bf16[528,256]{1,0:T(8,128)(2,1)S(1)}, u32[]{:S(2)}, u32[]{:S(2)}) collective-permute-start(bf16[528,256]{1,0:T(8,128)(2,1)S(1)} %get-tuple-element.41), channel_id=1, source_target_pairs={{0,1},{1,2},{2,3},{3,4},{4,5},{5,6},{6,7},{7,8},{8,9},{9,10},{10,1... | collective-permute-start | bytes 811016 | tf_op jit(solution)/shard_map/ppermute | solution.py:177
  41.6 10.5 %collective-permute-start.13 = (bf16[3,128,128]{2,1,0:T(8,128)(2,1)S(1)}, bf16[3,128,128]{2,1,0:T(8,128)(2,1)S(1)}, u32[]{:S(2)}, u32[]{:S(2)}) collective-permute-start(bf16[3,128,128]{2,1,0:T(8,128)(2,1)S(1)} %copy-done.5), channel_id=1, source_target_pairs={{0,96},{32,64},{64,32},{96,0},{1,97},{33,65},{65,33},{97,1},{2,98}... | collective-permute-start | bytes 294920 | tf_op jit(solution)/shard_map/ppermute | solution.py:182
  43.8 11.2 %collective-permute-start.12 = (bf16[3,128,128]{2,1,0:T(8,128)(2,1)S(1)}, bf16[3,128,128]{2,1,0:T(8,128)(2,1)S(1)}, u32[]{:S(2)}, u32[]{:S(2)}) collective-permute-start(bf16[3,128,128]{2,1,0:T(8,128)(2,1)S(1)} %copy-done.4), channel_id=1, source_target_pairs={{0,64},{32,96},{64,0},{96,32},{1,65},{33,97},{65,1},{97,33},{2,66}... | collective-permute-start | bytes 294920 | tf_op jit(solution)/shard_map/ppermute | solution.py:182
  44.6 10.4 %collective-permute-start.11 = (bf16[3,128,128]{2,1,0:T(8,128)(2,1)S(1)}, bf16[3,128,128]{2,1,0:T(8,128)(2,1)S(1)}, u32[]{:S(2)}, u32[]{:S(2)}) collective-permute-start(bf16[3,128,128]{2,1,0:T(8,128)(2,1)S(1)} %get-tuple-element.77), channel_id=1, source_target_pairs={{0,32},{32,0},{64,96},{96,64},{1,33},{33,1},{65,97},{97,65},{2,34}... | collective-permute-start | bytes 294920 | tf_op jit(solution)/shard_map/ppermute | solution.py:182
  57.8 14.4 %collective-permute-start.14 = (bf16[528,256]{1,0:T(8,128)(2,1)S(1)}, bf16[528,256]{1,0:T(8,128)(2,1)S(1)}, u32[]{:S(2)}, u32[]{:S(2)}) collective-permute-start(bf16[528,256]{1,0:T(8,128)(2,1)S(1)} %get-tuple-element.46), channel_id=1, source_target_pairs={{0,1},{1,2},{2,3},{3,4},{4,5},{5,6},{6,7},{7,8},{8,9},{9,10},{10,1... | collective-permute-start | bytes 811016 | tf_op jit(solution)/shard_map/ppermute | solution.py:177
  59.2 9.7 %collective-permute-start.17 = (bf16[3,128,128]{2,1,0:T(8,128)(2,1)S(1)}, bf16[3,128,128]{2,1,0:T(8,128)(2,1)S(1)}, u32[]{:S(2)}, u32[]{:S(2)}) collective-permute-start(bf16[3,128,128]{2,1,0:T(8,128)(2,1)S(1)} %get-tuple-element.71), channel_id=1, source_target_pairs={{0,96},{32,64},{64,32},{96,0},{1,97},{33,65},{65,33},{97,1},{2,98}... | collective-permute-start | bytes 294920 | tf_op jit(solution)/shard_map/ppermute | solution.py:182
  60.9 11.2 %collective-permute-start.16 = (bf16[3,128,128]{2,1,0:T(8,128)(2,1)S(1)}, bf16[3,128,128]{2,1,0:T(8,128)(2,1)S(1)}, u32[]{:S(2)}, u32[]{:S(2)}) collective-permute-start(bf16[3,128,128]{2,1,0:T(8,128)(2,1)S(1)} %get-tuple-element.72), channel_id=1, source_target_pairs={{0,64},{32,96},{64,0},{96,32},{1,65},{33,97},{65,1},{97,33},{2,66}... | collective-permute-start | bytes 294920 | tf_op jit(solution)/shard_map/ppermute | solution.py:182
  62.2 10.0 %collective-permute-start.15 = (bf16[3,128,128]{2,1,0:T(8,128)(2,1)S(1)}, bf16[3,128,128]{2,1,0:T(8,128)(2,1)S(1)}, u32[]{:S(2)}, u32[]{:S(2)}) collective-permute-start(bf16[3,128,128]{2,1,0:T(8,128)(2,1)S(1)} %get-tuple-element.73), channel_id=1, source_target_pairs={{0,32},{32,0},{64,96},{96,64},{1,33},{33,1},{65,97},{97,65},{2,34}... | collective-permute-start | bytes 294920 | tf_op jit(solution)/shard_map/ppermute | solution.py:182
  74.9 15.0 %collective-permute-start.18 = (bf16[528,256]{1,0:T(8,128)(2,1)S(1)}, bf16[528,256]{1,0:T(8,128)(2,1)S(1)}, u32[]{:S(2)}, u32[]{:S(2)}) collective-permute-start(bf16[528,256]{1,0:T(8,128)(2,1)S(1)} %get-tuple-element.51), channel_id=1, source_target_pairs={{0,1},{1,2},{2,3},{3,4},{4,5},{5,6},{6,7},{7,8},{8,9},{9,10},{10,1... | collective-permute-start | bytes 811016 | tf_op jit(solution)/shard_map/ppermute | solution.py:177
  76.6 10.3 %collective-permute-start.21 = (bf16[3,128,128]{2,1,0:T(8,128)(2,1)S(1)}, bf16[3,128,128]{2,1,0:T(8,128)(2,1)S(1)}, u32[]{:S(2)}, u32[]{:S(2)}) collective-permute-start(bf16[3,128,128]{2,1,0:T(8,128)(2,1)S(1)} %get-tuple-element.67), channel_id=1, source_target_pairs={{0,96},{32,64},{64,32},{96,0},{1,97},{33,65},{65,33},{97,1},{2,98}... | collective-permute-start | bytes 294920 | tf_op jit(solution)/shard_map/ppermute | solution.py:182
  78.6 11.2 %collective-permute-start.20 = (bf16[3,128,128]{2,1,0:T(8,128)(2,1)S(1)}, bf16[3,128,128]{2,1,0:T(8,128)(2,1)S(1)}, u32[]{:S(2)}, u32[]{:S(2)}) collective-permute-start(bf16[3,128,128]{2,1,0:T(8,128)(2,1)S(1)} %get-tuple-element.68), channel_id=1, source_target_pairs={{0,64},{32,96},{64,0},{96,32},{1,65},{33,97},{65,1},{97,33},{2,66}... | collective-permute-start | bytes 294920 | tf_op jit(solution)/shard_map/ppermute | solution.py:182
  79.3 10.6 %collective-permute-start.19 = (bf16[3,128,128]{2,1,0:T(8,128)(2,1)S(1)}, bf16[3,128,128]{2,1,0:T(8,128)(2,1)S(1)}, u32[]{:S(2)}, u32[]{:S(2)}) collective-permute-start(bf16[3,128,128]{2,1,0:T(8,128)(2,1)S(1)} %get-tuple-element.69), channel_id=1, source_target_pairs={{0,32},{32,0},{64,96},{96,64},{1,33},{33,1},{65,97},{97,65},{2,34}... | collective-permute-start | bytes 294920 | tf_op jit(solution)/shard_map/ppermute | solution.py:182
  92.6 14.4 %collective-permute-start.22 = (bf16[528,256]{1,0:T(8,128)(2,1)S(1)}, bf16[528,256]{1,0:T(8,128)(2,1)S(1)}, u32[]{:S(2)}, u32[]{:S(2)}) collective-permute-start(bf16[528,256]{1,0:T(8,128)(2,1)S(1)} %get-tuple-element.56), channel_id=1, source_target_pairs={{0,1},{1,2},{2,3},{3,4},{4,5},{5,6},{6,7},{7,8},{8,9},{9,10},{10,1... | collective-permute-start | bytes 811016 | tf_op jit(solution)/shard_map/ppermute | solution.py:177
  94.0 9.7 %collective-permute-start.25 = (bf16[3,128,128]{2,1,0:T(8,128)(2,1)S(1)}, bf16[3,128,128]{2,1,0:T(8,128)(2,1)S(1)}, u32[]{:S(2)}, u32[]{:S(2)}) collective-permute-start(bf16[3,128,128]{2,1,0:T(8,128)(2,1)S(1)} %get-tuple-element.64), channel_id=1, source_target_pairs={{0,96},{32,64},{64,32},{96,0},{1,97},{33,65},{65,33},{97,1},{2,98}... | collective-permute-start | bytes 294920 | tf_op jit(solution)/shard_map/ppermute | solution.py:182
  95.8 8.0 %collective-permute-start.23 = (bf16[3,128,128]{2,1,0:T(8,128)(2,1)S(1)}, bf16[3,128,128]{2,1,0:T(8,128)(2,1)S(1)}, u32[]{:S(2)}, u32[]{:S(2)}) collective-permute-start(bf16[3,128,128]{2,1,0:T(8,128)(2,1)S(1)} %get-tuple-element.65), channel_id=1, source_target_pairs={{0,32},{32,0},{64,96},{96,64},{1,33},{33,1},{65,97},{97,65},{2,34}... | collective-permute-start | bytes 294920 | tf_op jit(solution)/shard_map/ppermute | solution.py:182
  96.7 10.3 %collective-permute-start.24 = (bf16[3,128,128]{2,1,0:T(8,128)(2,1)S(1)}, bf16[3,128,128]{2,1,0:T(8,128)(2,1)S(1)}, u32[]{:S(2)}, u32[]{:S(2)}) collective-permute-start(bf16[3,128,128]{2,1,0:T(8,128)(2,1)S(1)} %get-tuple-element.87), channel_id=1, source_target_pairs={{0,64},{32,96},{64,0},{96,32},{1,65},{33,97},{65,1},{97,33},{2,66}... | collective-permute-start | bytes 294920 | tf_op jit(solution)/shard_map/ppermute | solution.py:182
  (9 other events, 118.8 us)
where the time goes:
time: 112 us
  waiting for transfers between devices  51.7 us (46%)
  starting transfers between devices  32.7 us (29%)
  Pallas kernels  21.9 us (20%)
  local copies, waits for them, and re-layouts  3.58 us (3%)
  other arithmetic  1.47 us (1%)
    ppermute x21, waiting for transfers between devices, swapped(): return lax.ppermute(value, 'group', [(i, i ^ by) for i in range(peers)])  51.7 us
    ppermute x21, starting transfers between devices, swapped(): return lax.ppermute(value, 'group', [(i, i ^ by) for i in range(peers)])  24.8 us
    pallas_call x6, Pallas kernels, context_call(): pl.pallas_call(functools.partial(context_kernel, first, last, stop), out_...  17.2 us
    ppermute x5, starting transfers between devices, shifted(): lax.ppermute(value, axis, [(i, (i + by) % peers) for i in range(peers)])  7.93 us
    pallas_call x6, Pallas kernels, vertex_call(): pl.pallas_call(functools.partial(vertex_kernel, last), out_shape=[jax.Sha...  4.63 us
    reshape x1, local copies, waits for them, and re-layouts, exchanged(): piece = lax.dynamic_slice(weights, (me ^ by, stop, 0, 0, 0), (1, 1, cap,...  2.76 us
  transfers between devices with their start and end apart: 26, of which 12 were waited for; matrix products, arithmetic and copies ran while one was open for 3% of the time, Pallas kernels for 3%

commit v1 on v0

v1 whole, which is shorter than its diff:
```python
import functools

import jax
import jax.numpy as jnp
from jax import lax
from jax.experimental import pallas as pl
from jax.experimental.pallas import tpu as pltpu
from jax.sharding import PartitionSpec as P

LEARNING = 0.1
TILE = 128
BLOCK = 256
F32 = jnp.float32
BF16 = jnp.bfloat16
NT = (((1,), (1,)), ((), ()))
NN = (((1,), (0,)), ((), ()))
TN = (((0,), (0,)), ((), ()))
VM = pl.BlockSpec(memory_space=pltpu.VMEM)
SM = pl.BlockSpec(memory_space=pltpu.SMEM)
HBM = pl.BlockSpec(memory_space=pltpu.HBM)
FREE = pl.CostEstimate(flops=0, bytes_accessed=0, transcendentals=0)
ROOM = 24 << 20
PACK_ROOM = 60 << 20
ROW_TILES = 8
PAIRS = 32
CHUNKS = 2
TAIL = 16
ID_ROWS = 8


def dot(a, b, dims):
    return lax.dot_general(a, b, dims, preferred_element_type=F32)


def eye_mask():
    return lax.broadcasted_iota(jnp.int32, (TILE, TILE), 0) == lax.broadcasted_iota(
        jnp.int32, (TILE, TILE), 1
    )


def to_column(eye, row):
    return jnp.sum(jnp.where(eye, row, 0.0), axis=1, keepdims=True)


def to_row(eye, column):
    return jnp.sum(jnp.where(eye, column, 0.0), axis=0, keepdims=True)


def adagrad(eye, rows, state_row, grad):
    width = grad.shape[1]
    state = to_column(eye, state_row) + jnp.sum(grad * grad, axis=1, keepdims=True) * (1.0 / width)
    return rows - (LEARNING * grad) * lax.rsqrt(state), to_row(eye, state)


def stack_rows(rows, height):
    which = lax.broadcasted_iota(jnp.int32, (height, TILE), 0)
    out = jnp.zeros((height, TILE), F32)
    for t, row in enumerate(rows):
        out = jnp.where(which == t, row, out)
    return out


def context_kernel(first, last, stop, base, *refs):
    neg_ref, v_ref, w_ref, *refs = refs
    if first:
        c_ref, cs_ref, pt_ref, *outs = refs
        height = pt_ref.shape[0]
        tiles = slice(base, base + height // TILE)
        c_now = c_ref[base * TILE : base * TILE + height, :]
        c_bf = c_now.astype(BF16)
        states = cs_ref[tiles, :]
    else:
        parts = len(refs) - (3 if last else 2)
        msgs, (pt_ref, *outs) = refs[:parts], refs[parts:]
        part = msgs[0].shape[0] - TAIL
        height = part * parts
        c_bf = jnp.concatenate([msg[:part, :] for msg in msgs], axis=0)
        c_now = c_bf.astype(F32)
        tails = [msg[part:, :].astype(F32) for msg in msgs]
        states = jnp.concatenate(
            [(tail[:, :TILE] + tail[:, TILE:])[: part // TILE] for tail in tails], axis=0
        )

    rows_v = v_ref.shape[0]
    rt, ct = rows_v // TILE, height // TILE
    for block in range(rows_v // BLOCK):
        v_block = v_ref[block * BLOCK : (block + 1) * BLOCK, :].astype(BF16)
        t_val = jnp.tanh(0.5 * dot(c_bf, v_block, NT))
        for c in range(ct):
            for k in range(BLOCK // TILE):
                r = block * (BLOCK // TILE) + k
                count = jnp.int32(0)
                for n in range(neg_ref.shape[1]):
                    count += (neg_ref[stop, n, r] == base + c).astype(jnp.int32)
                q = 0.25 * count.astype(F32)
                half = w_ref[(base + c) * rt + r]
                tt = t_val[c * TILE : (c + 1) * TILE, k * TILE : (k + 1) * TILE]
                pt_ref[c * TILE : (c + 1) * TILE, r * TILE : (r + 1) * TILE] = (
                    half * (tt - 1.0) + q * (tt + 1.0)
                ).astype(BF16)

    grad = dot(pt_ref[...], v_ref[...].astype(BF16), NN)
    eye = eye_mask()
    new_states = []
    for c in range(ct):
        rows = slice(c * TILE, (c + 1) * TILE)
        new_rows, new_state = adagrad(eye, c_now[rows], states[c : c + 1], grad[rows])
        new_states.append(new_state)
        if last:
            outs[0][rows, :] = new_rows
            outs[1][c : c + 1, :] = new_state
        else:
            outs[0][rows, :] = new_rows.astype(BF16)
    if not last:
        block = stack_rows(new_states, TAIL)
        hi = block.astype(BF16)
        outs[0][height:, :TILE] = hi
        outs[0][height:, TILE:] = (block - hi.astype(F32)).astype(BF16)


def vertex_kernel(last, n_pt, n_c, *refs):
    pt_refs, c_refs, refs = refs[:n_pt], refs[n_pt : n_pt + n_c], refs[n_pt + n_c :]
    v_ref, vs_ref, vout_ref, vsout_ref, *more = refs
    ctx = sum(ref.shape[0] for ref in pt_refs)
    c_bf = jnp.concatenate([ref[: ctx // n_c, :] for ref in c_refs], axis=0).astype(BF16)
    eye = eye_mask()
    for r in range(v_ref.shape[0] // TILE):
        rows = slice(r * TILE, (r + 1) * TILE)
        pt = jnp.concatenate([ref[:, rows] for ref in pt_refs], axis=0)
        grad = dot(pt, c_bf, TN)
        new_rows, new_state = adagrad(eye, v_ref[rows, :], vs_ref[r : r + 1, :], grad)
        vout_ref[rows, :] = new_rows
        vsout_ref[r : r + 1, :] = new_state
        if not last:
            more[0][rows, :] = new_rows.astype(BF16)


def add_tiles(out_ref, tiles):
    for pair, tile in tiles:
        out_ref[pair] += 0.5 * tile.astype(F32).T


def near_kernel(own_ref, one_ref, near_ref, out_ref):
    out_ref[...] = jnp.zeros_like(out_ref)
    cap = near_ref.shape[0] // 2
    add_tiles(
        out_ref,
        [(ref[slot, 0], near_ref[k * cap + slot]) for k, ref in enumerate((own_ref, one_ref)) for slot in range(cap)],
    )


def first_weights_kernel(own_ref, one_ref, part_ref, two_ref, three_ref, out_ref, ids_ref, scalars, sem):
    msgs = two_ref, three_ref
    cap = (two_ref.shape[0] - TAIL) // TILE
    for at, msg in enumerate(msgs):
        ids_ref[at + 2] = msg[cap * TILE :, :].astype(F32)[:ID_ROWS].astype(jnp.int32)
    copy = pltpu.make_async_copy(ids_ref.at[pl.ds(2, 2)], scalars, sem)
    copy.start()
    ids_ref[0] = own_ref[...]
    ids_ref[1] = one_ref[...]
    copy.wait()
    add_tiles(
        out_ref,
        [
            (scalars[at, slot, 0], msg[slot * TILE : (slot + 1) * TILE, :])
            for at, msg in enumerate(msgs)
            for slot in range(cap)
        ],
    )


def weights_kernel(stop, ids_ref, near_ref, far_ref, out_ref):
    out_ref[...] = jnp.zeros_like(out_ref)
    cap = far_ref.shape[0] // 2
    tiles = [ref[t] for ref in (near_ref, far_ref) for t in range(2 * cap)]
    add_tiles(out_ref, [(ids_ref[at // cap, at % cap, stop], tile) for at, tile in enumerate(tiles)])


def pack_kernel(me_ref, w_ref, rows_ref, cols_ref, counts_ref, *refs):
    groups, _, cap = w_ref.shape[:3]
    outs, (given, counts, ids, sem) = refs[:4], refs[4:]
    msgs = outs[2:]
    me = me_ref[0]
    fetches = [
        pltpu.make_async_copy(rows_ref, given.at[0], sem.at[0]),
        pltpu.make_async_copy(cols_ref, given.at[1], sem.at[1]),
        pltpu.make_async_copy(counts_ref, counts, sem.at[2]),
    ]
    for copy in fetches:
        copy.start()
    copies = [
        pltpu.make_async_copy(
            w_ref.at[me ^ (at + 2), 0, slot], msg.at[pl.ds(slot * TILE, TILE)], sem.at[3 + at * cap + slot]
        )
        for at, msg in enumerate(msgs)
        for slot in range(cap)
    ]
    for copy in copies:
        copy.start()
    ids[...] = jnp.zeros_like(ids)
    for copy in fetches:
        copy.wait()
    stops = counts.shape[1]
    for slot in range(cap):
        code = jnp.where(slot < counts[...], given[1, slot] * ROW_TILES + given[0, slot], PAIRS)
        which = lax.broadcasted_iota(jnp.int32, code.shape, 0)
        for by in range(groups):
            kept = jnp.sum(jnp.where(which == (me ^ by), code, 0), axis=0, keepdims=True)
            ids[by, slot : slot + 1, :stops] = kept
    outs[0][...] = ids[0, :ID_ROWS]
    outs[1][...] = ids[1, :ID_ROWS]
    for at, msg in enumerate(msgs):
        msg[cap * TILE :, :] = ids[at + 2].astype(F32).astype(BF16)
    for copy in copies:
        copy.wait()


def relay_kernel(stop, me_ref, w_ref, sib_ref, after_ref, *refs):
    *out_refs, sem = refs
    me = me_ref[0]
    cap = w_ref.shape[2]
    copies = []
    for n, (dst, by, at) in enumerate(zip(out_refs, (2, 0, 0), (stop, stop, 0))):
        for half, src in enumerate((w_ref, sib_ref)):
            copies.append(
                pltpu.make_async_copy(
                    src.at[me ^ by, at], dst.at[pl.ds(half * cap, cap)], sem.at[2 * n + half]
                )
            )
    for copy in copies:
        copy.start()
    for copy in copies:
        copy.wait()


def params(room=ROOM):
    return pltpu.CompilerParams(vmem_limit_bytes=room)


def context_call(stop, first, last, chunk, neg, v, context, w):
    width = v.shape[1]
    if first:
        height = context[0].shape[0] // CHUNKS
    else:
        height = len(context) * (context[0].shape[0] - TAIL)
    if last:
        outs = [((height, width), F32), ((height // TILE, TILE), F32)]
    else:
        outs = [((height + TAIL, width), BF16)]
    outs = [((height, v.shape[0]), BF16)] + outs
    args = (neg, v, w, *context)
    return pl.pallas_call(
        functools.partial(context_kernel, first, last, stop, chunk * height // TILE),
        out_shape=[jax.ShapeDtypeStruct(s, d) for s, d in outs],
        in_specs=[SM] + [VM] * (len(args) - 1),
        out_specs=[VM] * len(outs),
        compiler_params=params(),
        cost_estimate=FREE,
        name="context_%d_%d" % (stop, chunk),
    )(*args)


def vertex_call(stop, last, pts, cs, v, vs):
    outs = [(v.shape, F32), (vs.shape, F32)]
    if not last:
        outs.append((v.shape, BF16))
    return pl.pallas_call(
        functools.partial(vertex_kernel, last, len(pts), len(cs)),
        out_shape=[jax.ShapeDtypeStruct(s, d) for s, d in outs],
        in_specs=[VM] * (len(pts) + len(cs) + 2),
        out_specs=[VM] * len(outs),
        compiler_params=params(),
        cost_estimate=FREE,
        name="vertex_%d" % stop,
    )(*pts, *cs, v, vs)


def weights_call(stop, ids, near, far):
    return pl.pallas_call(
        functools.partial(weights_kernel, stop),
        out_shape=shape(PAIRS + 1, TILE, TILE, dtype=F32),
        in_specs=[SM] + [VM] * 2,
        out_specs=VM,
        compiler_params=params(),
        cost_estimate=FREE,
        name="weights_%d" % stop,
    )(ids, near, far)


def relay_call(stop, me, weights, sibling, after):
    cap = weights.shape[2]
    count = 3 if stop == 1 else 2
    return pl.pallas_call(
        functools.partial(relay_kernel, stop),
        out_shape=[shape(2 * cap, TILE, TILE)] * count,
        in_specs=[SM, HBM, HBM, HBM],
        out_specs=[VM] * count,
        scratch_shapes=[pltpu.SemaphoreType.DMA((2 * count,))],
        compiler_params=params(),
        cost_estimate=FREE,
        name="relay_%d" % stop,
    )(me, weights, sibling, after)


def shifted(value, axis, by):
    peers = lax.axis_size(axis)
    return lax.ppermute(value, axis, [(i, (i + by) % peers) for i in range(peers)])


def swapped(value, by):
    peers = lax.axis_size("group")
    return lax.ppermute(value, "group", [(i, i ^ by) for i in range(peers)])


def shape(*dims, dtype=BF16):
    return jax.ShapeDtypeStruct(dims, dtype)


def body(vertex, vertex_state, context, context_state, tile_weights, tile_rows, tile_cols, tile_counts, negatives):
    weights = tile_weights[0, 0]
    groups, stops, cap = weights.shape[:3]
    rt, ct = vertex.shape[0] // TILE, context.shape[0] // TILE
    assert (groups, rt, rt * ct) == (4, ROW_TILES, PAIRS)
    me = lax.axis_index("group").astype(jnp.int32).reshape(1)
    neg = jnp.transpose(negatives[0, 0], (0, 2, 1))

    outs = [shape(ID_ROWS, TILE, dtype=jnp.int32)] * 2 + [shape(cap * TILE + TAIL, TILE)] * 2
    own_ids, one_ids, *msgs = pl.pallas_call(
        pack_kernel,
        out_shape=outs,
        in_specs=[SM, HBM, HBM, HBM, HBM],
        out_specs=[VM] * len(outs),
        scratch_shapes=[
            pltpu.VMEM((2, cap, groups, stops), jnp.int32),
            pltpu.VMEM((groups, stops), jnp.int32),
            pltpu.VMEM((groups, TAIL, TILE), jnp.int32),
            pltpu.SemaphoreType.DMA((3 + 2 * cap,)),
        ],
        compiler_params=params(PACK_ROOM),
        cost_estimate=FREE,
        name="pack",
    )(
        me,
        weights,
        jnp.transpose(tile_rows[0, 0], (2, 0, 1)),
        jnp.transpose(tile_cols[0, 0], (2, 0, 1)),
        tile_counts[0, 0],
    )
    later, _ = lax.optimization_barrier((weights, msgs[0]))
    sibling = swapped(later, 1)
    two, three, one_ids = swapped(msgs[0], 2), swapped(msgs[1], 3), swapped(one_ids, 1)

    def relay(stop, after):
        far, *near = relay_call(stop, me, weights, sibling, after)
        return near, swapped(far, 2)

    (near, near_first), far = relay(1, one_ids)
    arrived = {1: ((near,), far)}
    part = pl.pallas_call(
        near_kernel,
        out_shape=shape(PAIRS + 1, TILE, TILE, dtype=F32),
        in_specs=[SM, SM, VM],
        out_specs=VM,
        compiler_params=params(),
        cost_estimate=FREE,
        name="near_0",
    )(own_ids, one_ids, near_first)
    w_sum, ids = pl.pallas_call(
        first_weights_kernel,
        out_shape=[shape(PAIRS + 1, TILE, TILE, dtype=F32), shape(groups, ID_ROWS, TILE, dtype=jnp.int32)],
        in_specs=[VM] * 5,
        out_specs=[VM] * 2,
        scratch_shapes=[pltpu.SMEM((2, ID_ROWS, TILE), jnp.int32), pltpu.SemaphoreType.DMA],
        input_output_aliases={2: 0},
        compiler_params=params(),
        cost_estimate=FREE,
        name="weights_0",
    )(own_ids, one_ids, part, two, three)

    v, vs = vertex, vertex_state.reshape(rt, TILE)
    v_bf = vertex
    full = (context, context_state.reshape(ct, TILE))
    held = None
    for stop in range(stops - 1):
        pts, sent = [], []
        for chunk in range(CHUNKS):
            given = full if stop == 0 else (held[chunk],)
            pt, new = context_call(stop, stop == 0, False, chunk, neg, v_bf, given, w_sum)
            pts.append(pt)
            sent.append(shifted(new, "blk", 1))
        (near,), far = arrived[stop + 1]
        w_sum = weights_call(stop + 1, ids, near, far)
        v, vs, v_bf = vertex_call(stop, False, pts, [context] if stop == 0 else held, v, vs)
        if stop + 2 < stops:
            arrived[stop + 2] = relay(stop + 2, vs)
        held = sent
    pt, c_out, cs_out = context_call(stops - 1, False, True, 0, neg, v_bf, held, w_sum)
    v, vs = vertex_call(stops - 1, True, [pt], held, v, vs)
    return v, vs.reshape(-1), c_out, cs_out.reshape(-1)


def solution(mesh):
    in_specs = (
        P(("group", "blk"), None),
        P(("group", "blk")),
        P(("group", "blk"), None),
        P(("group", "blk")),
        P("group", "blk", None, None, None, None, None),
        P("group", "blk", None, None, None),
        P("group", "blk", None, None, None),
        P("group", "blk", None, None),
        P("group", "blk", None, None, None),
    )
    out_specs = (
        P(("group", "blk"), None),
        P(("group", "blk")),
        P(("group", "blk"), None),
        P(("group", "blk")),
    )
    return jax.shard_map(body, mesh=mesh, in_specs=in_specs, out_specs=out_specs, check_vma=False)
```

time: 112 us -> 78.7 us (0.70)
  waiting for transfers between devices: 51.7 us -> 23.3 us
  starting transfers between devices: 32.7 us -> 20.2 us
  Pallas kernels: 21.9 us -> 34.1 us
  local copies, waits for them, and re-layouts: 3.58 us -> 0.03 us
  other arithmetic: 1.47 us -> 0 us
    ppermute x21 -> x9, waiting for transfers between devices: 51.7 us -> 1.28 us  [swapped(): return lax.ppermute(value, 'group', [(i, i ^ by) for i in range(peers)])]
    ppermute x5 -> x10, waiting for transfers between devices: 0.01 us -> 22 us  [shifted(): lax.ppermute(value, axis, [(i, (i + by) % peers) for i in range(peers)])]
    pallas_call x12 -> x30, Pallas kernels: 21.9 us -> 34.1 us  [the longest x11 16.7 us: context_call(): pl.pallas_call(functools.partial(context_kernel, first, last, stop, chunk...]
    ppermute x21 -> x9, starting transfers between devices: 24.8 us -> 15.9 us  [swapped(): return lax.ppermute(value, 'group', [(i, i ^ by) for i in range(peers)])]
    ppermute x5 -> x10, starting transfers between devices: 7.93 us -> 4.34 us  [shifted(): lax.ppermute(value, axis, [(i, (i + by) % peers) for i in range(peers)])]
    reshape x1 -> x0, local copies, waits for them, and re-layouts: 2.76 us -> none  [exchanged(): piece = lax.dynamic_slice(weights, (me ^ by, stop, 0, 0, 0), (1, 1, cap,...]
  transfers between devices with their start and end apart: 26 -> 19, of which waited for: 12 -> 10; matrix products, arithmetic and copies ran while one was open for 3% -> 0% of each run, Pallas kernels for 3% -> 36%
where the time goes in v1:
time: 78.7 us; the launch traced here: 78.6 us
  Pallas kernels  34.1 us (43%)
  waiting for transfers between devices  23.3 us (30%)
  starting transfers between devices  20.2 us (26%)
  between operations  0.99 us (1%)
    ppermute x10, waiting for transfers between devices, shifted(): lax.ppermute(value, axis, [(i, (i + by) % peers) for i in range(peers)])  22 us
    pallas_call x11, Pallas kernels, context_call(): pl.pallas_call(functools.partial(context_kernel, first, last, stop, chunk...  16.7 us
    ppermute x9, starting transfers between devices, swapped(): return lax.ppermute(value, 'group', [(i, i ^ by) for i in range(peers)])  15.9 us
    pallas_call x5, Pallas kernels, weights_call(): pl.pallas_call(functools.partial(weights_kernel, stop), out_shape=shape(P...  5.52 us
    pallas_call x6, Pallas kernels, vertex_call(): pl.pallas_call(functools.partial(vertex_kernel, last, len(pts), len(cs)),...  5.23 us
    ppermute x10, starting transfers between devices, shifted(): lax.ppermute(value, axis, [(i, (i + by) % peers) for i in range(peers)])  4.34 us
    pallas_call x5, Pallas kernels, relay_call(): pl.pallas_call(functools.partial(relay_kernel, stop), out_shape=[shape(2...  3.04 us
    pallas_call x1, Pallas kernels, body(): pl.pallas_call(pack_kernel, out_shape=outs, in_specs=[SM, HBM, HBM, HBM,...  1.8 us
  transfers between devices with their start and end apart: 19, of which 10 were waited for; matrix products, arithmetic and copies ran while one was open for 0% of the time, Pallas kernels for 36%

profile of v1, /device:TPU:0, one launch (start us, length us, event | category | flops | bytes accessed | tf_op | source)
XLA Modules:
  0.0 78.6 jit_solution(430729297251277998)
XLA Ops:
  0.6 1.8 %pack.1 = (s32[8,128]{1,0:T(8,128)}, s32[8,128]{1,0:T(8,128)}, bf16[400,128]{1,0:T(8,128)(2,1)}, bf16[400,128]{1,0:T(8,128)(2,1)}) custom-call(s32[1]{0:T(128)} %bitcast.3.me_ref, bf16[4,6,3,128,128]{4,3,2,1,0:T(8,128)(2,1)} %bitcast.16, s32[3,4,6]{2,1,0:T(4,128)} %bitcast.37, s32[3,4,6]{2,1,0:T(4,128)} %bitcast.38, s32[4,6]{1,0:T(4,128)} %bitcast.39), custom_call_target="tpu_custom_call" | custom-call | tf_op jit(solution)/shard_map/pack/pallas_call | solution.py:328
  2.6 4.0 %collective-permute-start.2 = (bf16[400,128]{1,0:T(8,128)(2,1)}, bf16[400,128]{1,0:T(8,128)(2,1)S(1)}, u32[]{:S(2)}, u32[]{:S(2)}) collective-permute-start(bf16[400,128]{1,0:T(8,128)(2,1)} %get-tuple-element.64), channel_id=1, source_target_pairs={{0,64},{32,96},{64,0},{96,32},{1,65},{33,97},{65,1},{97,33},{2,66}... | collective-permute-start | bytes 307208 | tf_op jit(solution)/shard_map/ppermute | solution.py:312
  8.8 3.3 %collective-permute-start.4 = (bf16[6,128,128]{2,1,0:T(8,128)(2,1)S(1)}, bf16[6,128,128]{2,1,0:T(8,128)(2,1)S(1)}, u32[]{:S(2)}, u32[]{:S(2)}) collective-permute-start(bf16[6,128,128]{2,1,0:T(8,128)(2,1)S(1)} %get-tuple-element.74), channel_id=1, source_target_pairs={{0,64},{32,96},{64,0},{96,32},{1,65},{33,97},{65,1},{97,33},{2,66}... | collective-permute-start | bytes 589832 | tf_op jit(solution)/shard_map/ppermute | solution.py:312
  14.0 1.4 %context_0_0.1 = (bf16[256,1024]{1,0:T(8,128)(2,1)S(1)}, bf16[272,256]{1,0:T(8,128)(2,1)S(1)}) custom-call(s32[6,2,8]{2,1,0:T(2,128)S(1)} %bitcast.23, f32[1024,256]{1,0:T(8,128)S(1)} %copy-done.1, f32[33,128,128]{2,1,0:T(8,128)S(1)} %get-tuple-element.68.refs_2_, f32[512,256]{1,0:T(8,128)S(1)} %copy-done.2, f32[4,128]{1,0:T(4,128)S(1)} %bitcast.34), custom_call_target="tpu_custom_call" | custom-call | tf_op jit(solution)/shard_map/context_0_0/pallas_call | solution.py:252
  16.6 1.4 %context_0_1.1 = (bf16[256,1024]{1,0:T(8,128)(2,1)S(1)}, bf16[272,256]{1,0:T(8,128)(2,1)S(1)}) custom-call(s32[6,2,8]{2,1,0:T(2,128)S(1)} %bitcast.24, f32[1024,256]{1,0:T(8,128)S(1)} %copy-done.1, f32[33,128,128]{2,1,0:T(8,128)S(1)} %get-tuple-element.68.refs_2_, f32[512,256]{1,0:T(8,128)S(1)} %copy-done.2, f32[4,128]{1,0:T(4,128)S(1)} %bitcast.35), custom_call_target="tpu_custom_call" | custom-call | tf_op jit(solution)/shard_map/context_0_1/pallas_call | solution.py:252
  18.0 2.1 %collective-permute-start.6 = (bf16[272,256]{1,0:T(8,128)(2,1)S(1)}, bf16[272,256]{1,0:T(8,128)(2,1)S(1)}, u32[]{:S(2)}, u32[]{:S(2)}) collective-permute-start(bf16[272,256]{1,0:T(8,128)(2,1)S(1)} %get-tuple-element.77), channel_id=1, source_target_pairs={{0,1},{1,2},{2,3},{3,4},{4,5},{5,6},{6,7},{7,8},{8,9},{9,10},{10,1... | collective-permute-start | bytes 417800 | tf_op jit(solution)/shard_map/ppermute | solution.py:307
  21.4 2.2 %collective-permute-start.7 = (bf16[6,128,128]{2,1,0:T(8,128)(2,1)S(1)}, bf16[6,128,128]{2,1,0:T(8,128)(2,1)S(1)}, u32[]{:S(2)}, u32[]{:S(2)}) collective-permute-start(bf16[6,128,128]{2,1,0:T(8,128)(2,1)S(1)} %get-tuple-element.83), channel_id=1, source_target_pairs={{0,64},{32,96},{64,0},{96,32},{1,65},{33,97},{65,1},{97,33},{2,66}... | collective-permute-start | bytes 589832 | tf_op jit(solution)/shard_map/ppermute | solution.py:312
  24.7 1.7 %collective-permute-done.5.refs_3_.refs_2_ = bf16[272,256]{1,0:T(8,128)(2,1)S(1)} collective-permute-done((bf16[272,256]{1,0:T(8,128)(2,1)S(1)}, bf16[272,256]{1,0:T(8,128)(2,1)S(1)}, u32[]{:S(2)}, u32[]{:S(2)}) %collective-permute-start.5) | collective-permute-done | bytes 139296 | tf_op jit(solution)/shard_map/ppermute | solution.py:307
  28.6 1.4 %context_1_1.1 = (bf16[256,1024]{1,0:T(8,128)(2,1)S(1)}, bf16[272,256]{1,0:T(8,128)(2,1)S(1)}) custom-call(s32[6,2,8]{2,1,0:T(2,128)S(1)} %bitcast.26, bf16[1024,256]{1,0:T(8,128)(2,1)S(1)} %get-tuple-element.71.refs_1_, f32[33,128,128]{2,1,0:T(8,128)S(1)} %weights_1.1.refs_2_, bf16[272,256]{1,0:T(8,128)(2,1)S(1)} %collective-permute-done.6.refs_3_), custom_call_target="tpu_custom_call" | custom-call | tf_op jit(solution)/shard_map/context_1_1/pallas_call | solution.py:252
  32.0 2.0 %collective-permute-start.10 = (bf16[6,128,128]{2,1,0:T(8,128)(2,1)S(1)}, bf16[6,128,128]{2,1,0:T(8,128)(2,1)S(1)}, u32[]{:S(2)}, u32[]{:S(2)}) collective-permute-start(bf16[6,128,128]{2,1,0:T(8,128)(2,1)S(1)} %get-tuple-element.92), channel_id=1, source_target_pairs={{0,64},{32,96},{64,0},{96,32},{1,65},{33,97},{65,1},{97,33},{2,66}... | collective-permute-start | bytes 589832 | tf_op jit(solution)/shard_map/ppermute | solution.py:312
  35.1 3.1 %collective-permute-done.8.refs_3_.refs_2_ = bf16[272,256]{1,0:T(8,128)(2,1)S(1)} collective-permute-done((bf16[272,256]{1,0:T(8,128)(2,1)S(1)}, bf16[272,256]{1,0:T(8,128)(2,1)S(1)}, u32[]{:S(2)}, u32[]{:S(2)}) %collective-permute-start.8) | collective-permute-done | bytes 139296 | tf_op jit(solution)/shard_map/ppermute | solution.py:307
  40.2 1.4 %context_2_1.1 = (bf16[256,1024]{1,0:T(8,128)(2,1)S(1)}, bf16[272,256]{1,0:T(8,128)(2,1)S(1)}) custom-call(s32[6,2,8]{2,1,0:T(2,128)S(1)} %bitcast.28, bf16[1024,256]{1,0:T(8,128)(2,1)S(1)} %get-tuple-element.81.refs_1_, f32[33,128,128]{2,1,0:T(8,128)S(1)} %weights_2.1.refs_2_, bf16[272,256]{1,0:T(8,128)(2,1)S(1)} %collective-permute-done.9.refs_3_), custom_call_target="tpu_custom_call" | custom-call | tf_op jit(solution)/shard_map/context_2_1/pallas_call | solution.py:252
  43.0 2.3 %collective-permute-start.13 = (bf16[6,128,128]{2,1,0:T(8,128)(2,1)S(1)}, bf16[6,128,128]{2,1,0:T(8,128)(2,1)S(1)}, u32[]{:S(2)}, u32[]{:S(2)}) collective-permute-start(bf16[6,128,128]{2,1,0:T(8,128)(2,1)S(1)} %get-tuple-element.101), channel_id=1, source_target_pairs={{0,64},{32,96},{64,0},{96,32},{1,65},{33,97},{65,1},{97,33},{2,66}... | collective-permute-start | bytes 589832 | tf_op jit(solution)/shard_map/ppermute | solution.py:312
  46.4 4.0 %collective-permute-done.11.refs_3_.refs_2_ = bf16[272,256]{1,0:T(8,128)(2,1)S(1)} collective-permute-done((bf16[272,256]{1,0:T(8,128)(2,1)S(1)}, bf16[272,256]{1,0:T(8,128)(2,1)S(1)}, u32[]{:S(2)}, u32[]{:S(2)}) %collective-permute-start.11) | collective-permute-done | bytes 139296 | tf_op jit(solution)/shard_map/ppermute | solution.py:307
  50.4 1.4 %context_3_0.1 = (bf16[256,1024]{1,0:T(8,128)(2,1)S(1)}, bf16[272,256]{1,0:T(8,128)(2,1)S(1)}) custom-call(s32[6,2,8]{2,1,0:T(2,128)S(1)} %bitcast.29, bf16[1024,256]{1,0:T(8,128)(2,1)S(1)} %get-tuple-element.90.refs_1_, f32[33,128,128]{2,1,0:T(8,128)S(1)} %weights_3.1.refs_2_, bf16[272,256]{1,0:T(8,128)(2,1)S(1)} %collective-permute-done.11.refs_3_.refs_2_), custom_call_target="tpu_custom_call" | custom-call | tf_op jit(solution)/shard_map/context_3_0/pallas_call | solution.py:252
  52.0 1.4 %context_3_1.1 = (bf16[256,1024]{1,0:T(8,128)(2,1)S(1)}, bf16[272,256]{1,0:T(8,128)(2,1)S(1)}) custom-call(s32[6,2,8]{2,1,0:T(2,128)S(1)} %bitcast.30, bf16[1024,256]{1,0:T(8,128)(2,1)S(1)} %get-tuple-element.90.refs_1_, f32[33,128,128]{2,1,0:T(8,128)S(1)} %weights_3.1.refs_2_, bf16[272,256]{1,0:T(8,128)(2,1)S(1)} %collective-permute-done.12.refs_3_), custom_call_target="tpu_custom_call" | custom-call | tf_op jit(solution)/shard_map/context_3_1/pallas_call | solution.py:252
  54.8 1.8 %collective-permute-start.16 = (bf16[6,128,128]{2,1,0:T(8,128)(2,1)S(1)}, bf16[6,128,128]{2,1,0:T(8,128)(2,1)S(1)}, u32[]{:S(2)}, u32[]{:S(2)}) collective-permute-start(bf16[6,128,128]{2,1,0:T(8,128)(2,1)S(1)} %get-tuple-element.110), channel_id=1, source_target_pairs={{0,64},{32,96},{64,0},{96,32},{1,65},{33,97},{65,1},{97,33},{2,66}... | collective-permute-start | bytes 589832 | tf_op jit(solution)/shard_map/ppermute | solution.py:312
  57.7 4.3 %collective-permute-done.14.refs_3_.refs_2_ = bf16[272,256]{1,0:T(8,128)(2,1)S(1)} collective-permute-done((bf16[272,256]{1,0:T(8,128)(2,1)S(1)}, bf16[272,256]{1,0:T(8,128)(2,1)S(1)}, u32[]{:S(2)}, u32[]{:S(2)}) %collective-permute-start.14) | collective-permute-done | bytes 139296 | tf_op jit(solution)/shard_map/ppermute | solution.py:307
  62.1 1.4 %context_4_0.1 = (bf16[256,1024]{1,0:T(8,128)(2,1)S(1)}, bf16[272,256]{1,0:T(8,128)(2,1)S(1)}) custom-call(s32[6,2,8]{2,1,0:T(2,128)S(1)} %bitcast.31, bf16[1024,256]{1,0:T(8,128)(2,1)S(1)} %get-tuple-element.99.refs_1_, f32[33,128,128]{2,1,0:T(8,128)S(1)} %weights_4.1.refs_2_, bf16[272,256]{1,0:T(8,128)(2,1)S(1)} %collective-permute-done.14.refs_3_.refs_2_), custom_call_target="tpu_custom_call" | custom-call | tf_op jit(solution)/shard_map/context_4_0/pallas_call | solution.py:252
  63.6 1.4 %context_4_1.1 = (bf16[256,1024]{1,0:T(8,128)(2,1)S(1)}, bf16[272,256]{1,0:T(8,128)(2,1)S(1)}) custom-call(s32[6,2,8]{2,1,0:T(2,128)S(1)} %bitcast.32, bf16[1024,256]{1,0:T(8,128)(2,1)S(1)} %get-tuple-element.99.refs_1_, f32[33,128,128]{2,1,0:T(8,128)S(1)} %weights_4.1.refs_2_, bf16[272,256]{1,0:T(8,128)(2,1)S(1)} %collective-permute-done.15.refs_3_), custom_call_target="tpu_custom_call" | custom-call | tf_op jit(solution)/shard_map/context_4_1/pallas_call | solution.py:252
  66.9 5.9 %collective-permute-done.17.refs_3_.refs_1_ = bf16[272,256]{1,0:T(8,128)(2,1)S(1)} collective-permute-done((bf16[272,256]{1,0:T(8,128)(2,1)S(1)}, bf16[272,256]{1,0:T(8,128)(2,1)S(1)}, u32[]{:S(2)}, u32[]{:S(2)}) %collective-permute-start.17) | collective-permute-done | bytes 139296 | tf_op jit(solution)/shard_map/ppermute | solution.py:307
  72.8 1.5 %collective-permute-done.18.refs_4_.refs_2_ = bf16[272,256]{1,0:T(8,128)(2,1)S(1)} collective-permute-done((bf16[272,256]{1,0:T(8,128)(2,1)S(1)}, bf16[272,256]{1,0:T(8,128)(2,1)S(1)}, u32[]{:S(2)}, u32[]{:S(2)}) %collective-permute-start.18) | collective-permute-done | bytes 139296 | tf_op jit(solution)/shard_map/ppermute | solution.py:307
  74.3 2.6 %context_5_0.1 = (bf16[512,1024]{1,0:T(8,128)(2,1)S(1)}, f32[512,256]{1,0:T(8,128)}, f32[4,128]{1,0:T(4,128)}) custom-call(s32[6,2,8]{2,1,0:T(2,128)S(1)} %bitcast.33, bf16[1024,256]{1,0:T(8,128)(2,1)S(1)} %get-tuple-element.108.refs_1_, f32[33,128,128]{2,1,0:T(8,128)S(1)} %weights_5.1.refs_2_, bf16[272,256]{1,0:T(8,128)(2,1)S(1)} %collective-permute-done.17.refs_3_.refs_1_, ...), custom_call_target="tpu_custom_call" | custom-call | tf_op jit(solution)/shard_map/context_5_0/pallas_call | solution.py:252
  76.9 1.7 %vertex_5.1 = (f32[1024,256]{1,0:T(8,128)}, f32[8,128]{1,0:T(8,128)}) custom-call(bf16[512,1024]{1,0:T(8,128)(2,1)S(1)} %get-tuple-element.113.refs_0_, bf16[272,256]{1,0:T(8,128)(2,1)S(1)} %collective-permute-done.17.refs_3_.refs_1_, bf16[272,256]{1,0:T(8,128)(2,1)S(1)} %collective-permute-done.18.refs_4_.refs_2_, ...), custom_call_target="tpu_custom_call" | custom-call | tf_op jit(solution)/shard_map/vertex_5/pallas_call | solution.py:267
  (58 shorter events, 22.0 us)
Async XLA Ops:
  2.5 5.6 %collective-permute-start.1 = (bf16[4,6,3,128,128]{4,3,2,1,0:T(8,128)(2,1)S(1)}, bf16[4,6,3,128,128]{4,3,2,1,0:T(8,128)(2,1)S(1)}, u32[]{:S(2)}, u32[]{:S(2)}) collective-permute-start(bf16[4,6,3,128,128]{4,3,2,1,0:T(8,128)(2,1)S(1)} %bitcast.17), channel_id=1, source_target_pairs={{0,32},{32,0},{64,96},{96,64},{1,33},{33,1},{65,97},{97,65},{2,34}... | collective-permute-start | bytes 7077896 | tf_op jit(solution)/shard_map/ppermute | solution.py:312
  2.6 10.6 %collective-permute-start.2 = (bf16[400,128]{1,0:T(8,128)(2,1)}, bf16[400,128]{1,0:T(8,128)(2,1)S(1)}, u32[]{:S(2)}, u32[]{:S(2)}) collective-permute-start(bf16[400,128]{1,0:T(8,128)(2,1)} %get-tuple-element.64), channel_id=1, source_target_pairs={{0,64},{32,96},{64,0},{96,32},{1,65},{33,97},{65,1},{97,33},{2,66}... | collective-permute-start | bytes 307208 | tf_op jit(solution)/shard_map/ppermute | solution.py:312
  6.6 6.6 %collective-permute-start.3 = (bf16[400,128]{1,0:T(8,128)(2,1)}, bf16[400,128]{1,0:T(8,128)(2,1)S(1)}, u32[]{:S(2)}, u32[]{:S(2)}) collective-permute-start(bf16[400,128]{1,0:T(8,128)(2,1)} %get-tuple-element.67), channel_id=1, source_target_pairs={{0,96},{32,64},{64,32},{96,0},{1,97},{33,65},{65,33},{97,1},{2,98}... | collective-permute-start | bytes 307208 | tf_op jit(solution)/shard_map/ppermute | solution.py:312
  6.7 5.5 %copy-start.4 = (s32[8,128]{1,0:T(8,128)S(1)}, s32[8,128]{1,0:T(8,128)}, u32[]{:S(2)}) copy-start(s32[8,128]{1,0:T(8,128)} %get-tuple-element.62.own_ref) | copy-start | bytes 12292
  6.7 1.4 %collective-permute-start = (s32[8,128]{1,0:T(8,128)}, s32[8,128]{1,0:T(8,128)S(1)}, u32[]{:S(2)}, u32[]{:S(2)}) collective-permute-start(s32[8,128]{1,0:T(8,128)} %get-tuple-element.63), channel_id=1, source_target_pairs={{0,32},{32,0},{64,96},{96,64},{1,33},{33,1},{65,97},{97,65},{2,34}... | collective-permute-start | bytes 12296 | tf_op jit(solution)/shard_map/ppermute | solution.py:312
  8.8 14.7 %collective-permute-start.4 = (bf16[6,128,128]{2,1,0:T(8,128)(2,1)S(1)}, bf16[6,128,128]{2,1,0:T(8,128)(2,1)S(1)}, u32[]{:S(2)}, u32[]{:S(2)}) collective-permute-start(bf16[6,128,128]{2,1,0:T(8,128)(2,1)S(1)} %get-tuple-element.74), channel_id=1, source_target_pairs={{0,64},{32,96},{64,0},{96,32},{1,65},{33,97},{65,1},{97,33},{2,66}... | collective-permute-start | bytes 589832 | tf_op jit(solution)/shard_map/ppermute | solution.py:312
  12.2 1.8 %copy-start.2 = (f32[512,256]{1,0:T(8,128)S(1)}, f32[512,256]{1,0:T(8,128)}, u32[]{:S(2)}) copy-start(f32[512,256]{1,0:T(8,128)} %refs_2_.1) | copy-start | bytes 1572868
  12.2 1.8 %copy-start.3 = (s32[1,1,6,8,2]{3,4,2,1,0:T(2,128)S(1)}, s32[1,1,6,8,2]{3,4,2,1,0:T(2,128)}, u32[]{:S(2)}) copy-start(s32[1,1,6,8,2]{3,4,2,1,0:T(2,128)} %param.17) | copy-start | bytes 1156
  12.2 1.8 %copy-start.5 = (f32[512]{0:T(512)S(1)}, f32[512]{0:T(512)}, u32[]{:S(2)}) copy-start(f32[512]{0:T(512)} %param.12) | copy-start | bytes 6148
  15.5 4.6 %copy-start.6 = (f32[1024]{0:T(1024)S(1)}, f32[1024]{0:T(1024)}, u32[]{:S(2)}) copy-start(f32[1024]{0:T(1024)} %param.10) | copy-start | bytes 12292
  15.5 10.9 %collective-permute-start.5 = (bf16[272,256]{1,0:T(8,128)(2,1)S(1)}, bf16[272,256]{1,0:T(8,128)(2,1)S(1)}, u32[]{:S(2)}, u32[]{:S(2)}) collective-permute-start(bf16[272,256]{1,0:T(8,128)(2,1)S(1)} %get-tuple-element.75), channel_id=1, source_target_pairs={{0,1},{1,2},{2,3},{3,4},{4,5},{5,6},{6,7},{7,8},{8,9},{9,10},{10,1... | collective-permute-start | bytes 417800 | tf_op jit(solution)/shard_map/ppermute | solution.py:307
  18.0 10.6 %collective-permute-start.6 = (bf16[272,256]{1,0:T(8,128)(2,1)S(1)}, bf16[272,256]{1,0:T(8,128)(2,1)S(1)}, u32[]{:S(2)}, u32[]{:S(2)}) collective-permute-start(bf16[272,256]{1,0:T(8,128)(2,1)S(1)} %get-tuple-element.77), channel_id=1, source_target_pairs={{0,1},{1,2},{2,3},{3,4},{4,5},{5,6},{6,7},{7,8},{8,9},{9,10},{10,1... | collective-permute-start | bytes 417800 | tf_op jit(solution)/shard_map/ppermute | solution.py:307
  21.4 12.6 %collective-permute-start.7 = (bf16[6,128,128]{2,1,0:T(8,128)(2,1)S(1)}, bf16[6,128,128]{2,1,0:T(8,128)(2,1)S(1)}, u32[]{:S(2)}, u32[]{:S(2)}) collective-permute-start(bf16[6,128,128]{2,1,0:T(8,128)(2,1)S(1)} %get-tuple-element.83), channel_id=1, source_target_pairs={{0,64},{32,96},{64,0},{96,32},{1,65},{33,97},{65,1},{97,33},{2,66}... | collective-permute-start | bytes 589832 | tf_op jit(solution)/shard_map/ppermute | solution.py:312
  27.8 10.4 %collective-permute-start.8 = (bf16[272,256]{1,0:T(8,128)(2,1)S(1)}, bf16[272,256]{1,0:T(8,128)(2,1)S(1)}, u32[]{:S(2)}, u32[]{:S(2)}) collective-permute-start(bf16[272,256]{1,0:T(8,128)(2,1)S(1)} %get-tuple-element.84), channel_id=1, source_target_pairs={{0,1},{1,2},{2,3},{3,4},{4,5},{5,6},{6,7},{7,8},{8,9},{9,10},{10,1... | collective-permute-start | bytes 417800 | tf_op jit(solution)/shard_map/ppermute | solution.py:307
  30.1 10.2 %collective-permute-start.9 = (bf16[272,256]{1,0:T(8,128)(2,1)S(1)}, bf16[272,256]{1,0:T(8,128)(2,1)S(1)}, u32[]{:S(2)}, u32[]{:S(2)}) collective-permute-start(bf16[272,256]{1,0:T(8,128)(2,1)S(1)} %get-tuple-element.86), channel_id=1, source_target_pairs={{0,1},{1,2},{2,3},{3,4},{4,5},{5,6},{6,7},{7,8},{8,9},{9,10},{10,1... | collective-permute-start | bytes 417800 | tf_op jit(solution)/shard_map/ppermute | solution.py:307
  32.0 13.3 %collective-permute-start.10 = (bf16[6,128,128]{2,1,0:T(8,128)(2,1)S(1)}, bf16[6,128,128]{2,1,0:T(8,128)(2,1)S(1)}, u32[]{:S(2)}, u32[]{:S(2)}) collective-permute-start(bf16[6,128,128]{2,1,0:T(8,128)(2,1)S(1)} %get-tuple-element.92), channel_id=1, source_target_pairs={{0,64},{32,96},{64,0},{96,32},{1,65},{33,97},{65,1},{97,33},{2,66}... | collective-permute-start | bytes 589832 | tf_op jit(solution)/shard_map/ppermute | solution.py:312
  39.6 10.8 %collective-permute-start.11 = (bf16[272,256]{1,0:T(8,128)(2,1)S(1)}, bf16[272,256]{1,0:T(8,128)(2,1)S(1)}, u32[]{:S(2)}, u32[]{:S(2)}) collective-permute-start(bf16[272,256]{1,0:T(8,128)(2,1)S(1)} %get-tuple-element.93), channel_id=1, source_target_pairs={{0,1},{1,2},{2,3},{3,4},{4,5},{5,6},{6,7},{7,8},{8,9},{9,10},{10,1... | collective-permute-start | bytes 417800 | tf_op jit(solution)/shard_map/ppermute | solution.py:307
  41.6 10.4 %collective-permute-start.12 = (bf16[272,256]{1,0:T(8,128)(2,1)S(1)}, bf16[272,256]{1,0:T(8,128)(2,1)S(1)}, u32[]{:S(2)}, u32[]{:S(2)}) collective-permute-start(bf16[272,256]{1,0:T(8,128)(2,1)S(1)} %get-tuple-element.95), channel_id=1, source_target_pairs={{0,1},{1,2},{2,3},{3,4},{4,5},{5,6},{6,7},{7,8},{8,9},{9,10},{10,1... | collective-permute-start | bytes 417800 | tf_op jit(solution)/shard_map/ppermute | solution.py:307
  43.0 13.6 %collective-permute-start.13 = (bf16[6,128,128]{2,1,0:T(8,128)(2,1)S(1)}, bf16[6,128,128]{2,1,0:T(8,128)(2,1)S(1)}, u32[]{:S(2)}, u32[]{:S(2)}) collective-permute-start(bf16[6,128,128]{2,1,0:T(8,128)(2,1)S(1)} %get-tuple-element.101), channel_id=1, source_target_pairs={{0,64},{32,96},{64,0},{96,32},{1,65},{33,97},{65,1},{97,33},{2,66}... | collective-permute-start | bytes 589832 | tf_op jit(solution)/shard_map/ppermute | solution.py:312
  51.8 10.2 %collective-permute-start.14 = (bf16[272,256]{1,0:T(8,128)(2,1)S(1)}, bf16[272,256]{1,0:T(8,128)(2,1)S(1)}, u32[]{:S(2)}, u32[]{:S(2)}) collective-permute-start(bf16[272,256]{1,0:T(8,128)(2,1)S(1)} %get-tuple-element.102), channel_id=1, source_target_pairs={{0,1},{1,2},{2,3},{3,4},{4,5},{5,6},{6,7},{7,8},{8,9},{9,10},{10,1... | collective-permute-start | bytes 417800 | tf_op jit(solution)/shard_map/ppermute | solution.py:307
  53.5 10.1 %collective-permute-start.15 = (bf16[272,256]{1,0:T(8,128)(2,1)S(1)}, bf16[272,256]{1,0:T(8,128)(2,1)S(1)}, u32[]{:S(2)}, u32[]{:S(2)}) collective-permute-start(bf16[272,256]{1,0:T(8,128)(2,1)S(1)} %get-tuple-element.104), channel_id=1, source_target_pairs={{0,1},{1,2},{2,3},{3,4},{4,5},{5,6},{6,7},{7,8},{8,9},{9,10},{10,1... | collective-permute-start | bytes 417800 | tf_op jit(solution)/shard_map/ppermute | solution.py:307
  54.8 11.0 %collective-permute-start.16 = (bf16[6,128,128]{2,1,0:T(8,128)(2,1)S(1)}, bf16[6,128,128]{2,1,0:T(8,128)(2,1)S(1)}, u32[]{:S(2)}, u32[]{:S(2)}) collective-permute-start(bf16[6,128,128]{2,1,0:T(8,128)(2,1)S(1)} %get-tuple-element.110), channel_id=1, source_target_pairs={{0,64},{32,96},{64,0},{96,32},{1,65},{33,97},{65,1},{97,33},{2,66}... | collective-permute-start | bytes 589832 | tf_op jit(solution)/shard_map/ppermute | solution.py:312
  63.5 9.3 %collective-permute-start.17 = (bf16[272,256]{1,0:T(8,128)(2,1)S(1)}, bf16[272,256]{1,0:T(8,128)(2,1)S(1)}, u32[]{:S(2)}, u32[]{:S(2)}) collective-permute-start(bf16[272,256]{1,0:T(8,128)(2,1)S(1)} %get-tuple-element.111), channel_id=1, source_target_pairs={{0,1},{1,2},{2,3},{3,4},{4,5},{5,6},{6,7},{7,8},{8,9},{9,10},{10,1... | collective-permute-start | bytes 417800 | tf_op jit(solution)/shard_map/ppermute | solution.py:307
  65.0 9.3 %collective-permute-start.18 = (bf16[272,256]{1,0:T(8,128)(2,1)S(1)}, bf16[272,256]{1,0:T(8,128)(2,1)S(1)}, u32[]{:S(2)}, u32[]{:S(2)}) collective-permute-start(bf16[272,256]{1,0:T(8,128)(2,1)S(1)} %get-tuple-element.112), channel_id=1, source_target_pairs={{0,1},{1,2},{2,3},{3,4},{4,5},{5,6},{6,7},{7,8},{8,9},{9,10},{10,1... | collective-permute-start | bytes 417800 | tf_op jit(solution)/shard_map/ppermute | solution.py:307
  (2 other events, 3.6 us)

commit v2 on v1

--- a/solution.py
+++ b/solution.py
@@ -60,28 +60,15 @@
     return out
 
 
-def context_kernel(first, last, stop, base, *refs):
-    neg_ref, v_ref, w_ref, *refs = refs
-    if first:
-        c_ref, cs_ref, pt_ref, *outs = refs
-        height = pt_ref.shape[0]
-        tiles = slice(base, base + height // TILE)
-        c_now = c_ref[base * TILE : base * TILE + height, :]
-        c_bf = c_now.astype(BF16)
-        states = cs_ref[tiles, :]
-    else:
-        parts = len(refs) - (3 if last else 2)
-        msgs, (pt_ref, *outs) = refs[:parts], refs[parts:]
-        part = msgs[0].shape[0] - TAIL
-        height = part * parts
-        c_bf = jnp.concatenate([msg[:part, :] for msg in msgs], axis=0)
-        c_now = c_bf.astype(F32)
-        tails = [msg[part:, :].astype(F32) for msg in msgs]
-        states = jnp.concatenate(
-            [(tail[:, :TILE] + tail[:, TILE:])[: part // TILE] for tail in tails], axis=0
-        )
-
-    rows_v = v_ref.shape[0]
+def unpack_message(msg_ref):
+    height = msg_ref.shape[0] - TAIL
+    tail = msg_ref[height:, :].astype(F32)
+    c_bf = msg_ref[:height, :]
+    return c_bf, c_bf.astype(F32), tail[:, :TILE] + tail[:, TILE:]
+
+
+def update_context(base, c_bf, c_now, states, v_ref, w_ref, q_ref, pt_ref):
+    rows_v, height = v_ref.shape[0], c_bf.shape[0]
     rt, ct = rows_v // TILE, height // TILE
     for block in range(rows_v // BLOCK):
         v_block = v_ref[block * BLOCK : (block + 1) * BLOCK, :].astype(BF16)
@@ -89,11 +76,9 @@
         for c in range(ct):
             for k in range(BLOCK // TILE):
                 r = block * (BLOCK // TILE) + k
-                count = jnp.int32(0)
-                for n in range(neg_ref.shape[1]):
-                    count += (neg_ref[stop, n, r] == base + c).astype(jnp.int32)
-                q = 0.25 * count.astype(F32)
-                half = w_ref[(base + c) * rt + r]
+                pair = (base + c) * rt + r
+                q = q_ref[pair : pair + 1, :]
+                half = w_ref[pair]
                 tt = t_val[c * TILE : (c + 1) * TILE, k * TILE : (k + 1) * TILE]
                 pt_ref[c * TILE : (c + 1) * TILE, r * TILE : (r + 1) * TILE] = (
                     half * (tt - 1.0) + q * (tt + 1.0)
@@ -101,38 +86,104 @@
 
     grad = dot(pt_ref[...], v_ref[...].astype(BF16), NN)
     eye = eye_mask()
-    new_states = []
+    result = []
     for c in range(ct):
         rows = slice(c * TILE, (c + 1) * TILE)
-        new_rows, new_state = adagrad(eye, c_now[rows], states[c : c + 1], grad[rows])
-        new_states.append(new_state)
+        result.append(adagrad(eye, c_now[rows], states[c : c + 1], grad[rows]))
+    return result
+
+
+def context_kernel(first, last, base, v_ref, w_ref, q_ref, *refs):
+    if first:
+        c_ref, cs_ref, pt_ref, *outs = refs
+        height = pt_ref.shape[0]
+        c_now = c_ref[base * TILE : base * TILE + height, :]
+        c_bf = c_now.astype(BF16)
+        states = cs_ref[base : base + height // TILE, :]
+    else:
+        msg_ref, pt_ref, *outs = refs
+        height = pt_ref.shape[0]
+        c_bf, c_now, states = unpack_message(msg_ref)
+    result = update_context(base, c_bf, c_now, states, v_ref, w_ref, q_ref, pt_ref)
+    for c, (new_rows, new_state) in enumerate(result):
+        rows = slice(c * TILE, (c + 1) * TILE)
+        outs[0][rows, :] = new_rows if last else new_rows.astype(BF16)
         if last:
-            outs[0][rows, :] = new_rows
             outs[1][c : c + 1, :] = new_state
-        else:
-            outs[0][rows, :] = new_rows.astype(BF16)
     if not last:
-        block = stack_rows(new_states, TAIL)
+        block = stack_rows([new_state for _, new_state in result], TAIL)
         hi = block.astype(BF16)
         outs[0][height:, :TILE] = hi
         outs[0][height:, TILE:] = (block - hi.astype(F32)).astype(BF16)
 
 
-def vertex_kernel(last, n_pt, n_c, *refs):
-    pt_refs, c_refs, refs = refs[:n_pt], refs[n_pt : n_pt + n_c], refs[n_pt + n_c :]
-    v_ref, vs_ref, vout_ref, vsout_ref, *more = refs
+def vertex_kernel(n, first, *refs):
+    pt_refs, refs = refs[:n], refs[n:]
+    n_c = 1 if first else n
+    c_refs, refs = refs[:n_c], refs[n_c:]
+    v_ref, vs_ref, vout_ref, vsout_ref, vbf_ref = refs
     ctx = sum(ref.shape[0] for ref in pt_refs)
     c_bf = jnp.concatenate([ref[: ctx // n_c, :] for ref in c_refs], axis=0).astype(BF16)
     eye = eye_mask()
     for r in range(v_ref.shape[0] // TILE):
         rows = slice(r * TILE, (r + 1) * TILE)
         pt = jnp.concatenate([ref[:, rows] for ref in pt_refs], axis=0)
-        grad = dot(pt, c_bf, TN)
-        new_rows, new_state = adagrad(eye, v_ref[rows, :], vs_ref[r : r + 1, :], grad)
+        new_rows, new_state = adagrad(eye, v_ref[rows, :], vs_ref[r : r + 1, :], dot(pt, c_bf, TN))
         vout_ref[rows, :] = new_rows
         vsout_ref[r : r + 1, :] = new_state
-        if not last:
-            more[0][rows, :] = new_rows.astype(BF16)
+        vbf_ref[rows, :] = new_rows.astype(BF16)
+
+
+def final_kernel(n, v_ref, w_ref, q_ref, *refs):
+    msgs, refs = refs[:n], refs[n:]
+    done, refs = refs[: 3 * (n - 1)], refs[3 * (n - 1) :]
+    v32_ref, vs_ref, *refs = refs
+    vout_ref, vsout_ref, cout_ref, csout_ref, *refs = refs
+    last_pt, c_new, cs_new, v_new, vs_new, sem = refs
+    height = last_pt.shape[0]
+    tiles = height // TILE
+    rt = v_ref.shape[0] // TILE
+    stores = []
+
+    def store(src, dst):
+        copy = pltpu.make_async_copy(src, dst, sem.at[len(stores)])
+        copy.start()
+        stores.append(copy)
+
+    for k in range(n - 1):
+        _, rows_ref, state_ref = done[3 * k : 3 * k + 3]
+        store(rows_ref, cout_ref.at[pl.ds(k * height, height)])
+        cs_new[k * tiles : (k + 1) * tiles, :] = state_ref[...]
+    base = (n - 1) * tiles
+    result = update_context(base, *unpack_message(msgs[-1]), v_ref, w_ref, q_ref, last_pt)
+    for c, (new_rows, new_state) in enumerate(result):
+        c_new[c * TILE : (c + 1) * TILE, :] = new_rows
+        cs_new[base + c : base + c + 1, :] = new_state
+    store(c_new, cout_ref.at[pl.ds((n - 1) * height, height)])
+    store(cs_new, csout_ref)
+    c_bf = jnp.concatenate([msg[:height, :] for msg in msgs], axis=0)
+    pt_refs = [done[3 * k] for k in range(n - 1)] + [last_pt]
+    eye = eye_mask()
+    for r in range(rt):
+        rows = slice(r * TILE, (r + 1) * TILE)
+        pt = jnp.concatenate([ref[:, rows] for ref in pt_refs], axis=0)
+        new_rows, new_state = adagrad(eye, v32_ref[rows, :], vs_ref[r : r + 1, :], dot(pt, c_bf, TN))
+        v_new[rows, :] = new_rows
+        vs_new[r : r + 1, :] = new_state
+        if r % 2:
+            store(v_new.at[pl.ds((r - 1) * TILE, 2 * TILE)], vout_ref.at[pl.ds((r - 1) * TILE, 2 * TILE)])
+    store(vs_new, vsout_ref)
+    for copy in stores:
+        copy.wait()
+
+
+def fill_counts(stop, neg_ref, q_ref):
+    per_stop, rt = neg_ref.shape[1:]
+    for pair in range(PAIRS):
+        count = jnp.int32(0)
+        for n in range(per_stop):
+            count += (neg_ref[stop, n, pair % rt] == pair // rt).astype(jnp.int32)
+        q_ref[pair : pair + 1, :] = jnp.full((1, TILE), 0.25 * count.astype(F32))
 
 
 def add_tiles(out_ref, tiles):
@@ -140,7 +191,8 @@
         out_ref[pair] += 0.5 * tile.astype(F32).T
 
 
-def near_kernel(own_ref, one_ref, near_ref, out_ref):
+def near_kernel(own_ref, one_ref, neg_ref, near_ref, out_ref, q_ref):
+    fill_counts(0, neg_ref, q_ref)
     out_ref[...] = jnp.zeros_like(out_ref)
     cap = near_ref.shape[0] // 2
     add_tiles(
@@ -169,7 +221,8 @@
     )
 
 
-def weights_kernel(stop, ids_ref, near_ref, far_ref, out_ref):
+def weights_kernel(stop, ids_ref, neg_ref, near_ref, far_ref, out_ref, q_ref):
+    fill_counts(stop, neg_ref, q_ref)
     out_ref[...] = jnp.zeros_like(out_ref)
     cap = far_ref.shape[0] // 2
     tiles = [ref[t] for ref in (near_ref, far_ref) for t in range(2 * cap)]
@@ -237,22 +290,19 @@
     return pltpu.CompilerParams(vmem_limit_bytes=room)
 
 
-def context_call(stop, first, last, chunk, neg, v, context, w):
+def context_call(stop, first, last, chunk, v, context, w, q):
     width = v.shape[1]
-    if first:
-        height = context[0].shape[0] // CHUNKS
+    height = context[0].shape[0] // CHUNKS if first else context[0].shape[0] - TAIL
+    if last:
+        outs = [shape(height, width, dtype=F32), shape(height // TILE, TILE, dtype=F32)]
     else:
-        height = len(context) * (context[0].shape[0] - TAIL)
-    if last:
-        outs = [((height, width), F32), ((height // TILE, TILE), F32)]
-    else:
-        outs = [((height + TAIL, width), BF16)]
-    outs = [((height, v.shape[0]), BF16)] + outs
-    args = (neg, v, w, *context)
+        outs = [shape(height + TAIL, width)]
+    outs = [shape(height, v.shape[0])] + outs
+    args = (v, w, q, *context)
     return pl.pallas_call(
-        functools.partial(context_kernel, first, last, stop, chunk * height // TILE),
-        out_shape=[jax.ShapeDtypeStruct(s, d) for s, d in outs],
-        in_specs=[SM] + [VM] * (len(args) - 1),
+        functools.partial(context_kernel, first, last, chunk * height // TILE),
+        out_shape=outs,
+        in_specs=[VM] * len(args),
         out_specs=[VM] * len(outs),
         compiler_params=params(),
         cost_estimate=FREE,
@@ -260,13 +310,11 @@
     )(*args)
 
 
-def vertex_call(stop, last, pts, cs, v, vs):
-    outs = [(v.shape, F32), (vs.shape, F32)]
-    if not last:
-        outs.append((v.shape, BF16))
+def vertex_call(stop, pts, cs, v, vs):
+    outs = [shape(*v.shape, dtype=F32), shape(*vs.shape, dtype=F32), shape(*v.shape)]
     return pl.pallas_call(
-        functools.partial(vertex_kernel, last, len(pts), len(cs)),
-        out_shape=[jax.ShapeDtypeStruct(s, d) for s, d in outs],
+        functools.partial(vertex_kernel, len(pts), len(cs) == 1),
+        out_shape=outs,
         in_specs=[VM] * (len(pts) + len(cs) + 2),
         out_specs=[VM] * len(outs),
         compiler_params=params(),
@@ -275,16 +323,45 @@
     )(*pts, *cs, v, vs)
 
 
-def weights_call(stop, ids, near, far):
+def final_call(v_bf, w, q, msgs, done, v, vs):
+    n = len(msgs)
+    height, width = msgs[0].shape[0] - TAIL, v.shape[1]
+    tiles = n * height // TILE
+    args = (v_bf, w, q, *msgs, *done, v, vs)
+    return pl.pallas_call(
+        functools.partial(final_kernel, n),
+        out_shape=[
+            shape(*v.shape, dtype=F32),
+            shape(*vs.shape, dtype=F32),
+            shape(n * height, width, dtype=F32),
+            shape(tiles, TILE, dtype=F32),
+        ],
+        in_specs=[VM] * len(args),
+        out_specs=[HBM] * 4,
+        scratch_shapes=[
+            pltpu.VMEM((height, v.shape[0]), BF16),
+            pltpu.VMEM((height, width), F32),
+            pltpu.VMEM((tiles, TILE), F32),
+            pltpu.VMEM(v.shape, F32),
+            pltpu.VMEM(vs.shape, F32),
+            pltpu.SemaphoreType.DMA((n + 2 + v.shape[0] // (2 * TILE),)),
+        ],
+        compiler_params=params(),
+        cost_estimate=FREE,
+        name="final",
+    )(*args)
+
+
+def weights_call(stop, ids, neg, near, far):
     return pl.pallas_call(
         functools.partial(weights_kernel, stop),
-        out_shape=shape(PAIRS + 1, TILE, TILE, dtype=F32),
-        in_specs=[SM] + [VM] * 2,
-        out_specs=VM,
+        out_shape=[shape(PAIRS + 1, TILE, TILE, dtype=F32), shape(PAIRS, TILE, dtype=F32)],
+        in_specs=[SM] * 2 + [VM] * 2,
+        out_specs=[VM] * 2,
         compiler_params=params(),
         cost_estimate=FREE,
         name="weights_%d" % stop,
-    )(ids, near, far)
+    )(ids, neg, near, far)
 
 
 def relay_call(stop, me, weights, sibling, after):
@@ -356,15 +433,15 @@
 
     (near, near_first), far = relay(1, one_ids)
     arrived = {1: ((near,), far)}
-    part = pl.pallas_call(
+    part, q = pl.pallas_call(
         near_kernel,
-        out_shape=shape(PAIRS + 1, TILE, TILE, dtype=F32),
-        in_specs=[SM, SM, VM],
-        out_specs=VM,
+        out_shape=[shape(PAIRS + 1, TILE, TILE, dtype=F32), shape(PAIRS, TILE, dtype=F32)],
+        in_specs=[SM, SM, SM, VM],
+        out_specs=[VM] * 2,
         compiler_params=params(),
         cost_estimate=FREE,
         name="near_0",
-    )(own_ids, one_ids, near_first)
+    )(own_ids, one_ids, neg, near_first)
     w_sum, ids = pl.pallas_call(
         first_weights_kernel,
         out_shape=[shape(PAIRS + 1, TILE, TILE, dtype=F32), shape(groups, ID_ROWS, TILE, dtype=jnp.int32)],
@@ -385,17 +462,19 @@
         pts, sent = [], []
         for chunk in range(CHUNKS):
             given = full if stop == 0 else (held[chunk],)
-            pt, new = context_call(stop, stop == 0, False, chunk, neg, v_bf, given, w_sum)
+            pt, new = context_call(stop, stop == 0, False, chunk, v_bf, given, w_sum, q)
             pts.append(pt)
             sent.append(shifted(new, "blk", 1))
         (near,), far = arrived[stop + 1]
-        w_sum = weights_call(stop + 1, ids, near, far)
-        v, vs, v_bf = vertex_call(stop, False, pts, [context] if stop == 0 else held, v, vs)
+        w_sum, q = weights_call(stop + 1, ids, neg, near, far)
+        v, vs, v_bf = vertex_call(stop, pts, [context] if stop == 0 else held, v, vs)
         if stop + 2 < stops:
             arrived[stop + 2] = relay(stop + 2, vs)
         held = sent
-    pt, c_out, cs_out = context_call(stops - 1, False, True, 0, neg, v_bf, held, w_sum)
-    v, vs = vertex_call(stops - 1, True, [pt], held, v, vs)
+    done = []
+    for chunk in range(CHUNKS - 1):
+        done += context_call(stops - 1, False, True, chunk, v_bf, (held[chunk],), w_sum, q)
+    v, vs, c_out, cs_out = final_call(v_bf, w_sum, q, held, done, v, vs)
     return v, vs.reshape(-1), c_out, cs_out.reshape(-1)
 
 

time: 78.7 us -> 74.6 us (0.948); the launches traced: 78.6 us -> 73.6 us
  Pallas kernels: 34.1 us -> 27.3 us
  waiting for transfers between devices: 23.3 us -> 24.4 us
    pallas_call x23, Pallas kernels: 28.4 us -> 21.6 us  [the longest x11 8.64 us: context_call(): pl.pallas_call(functools.partial(context_kernel, first, last, chunk * hei...]
    ppermute x10, waiting for transfers between devices: 22 us -> 23.1 us  [shifted(): lax.ppermute(value, axis, [(i, (i + by) % peers) for i in range(peers)])]
    ppermute x9, starting transfers between devices: 15.9 us -> 16.9 us  [swapped(): return lax.ppermute(value, 'group', [(i, i ^ by) for i in range(peers)])]
  transfers between devices with their start and end apart: 19 -> 19, of which waited for: 10 -> 11; matrix products, arithmetic and copies ran while one was open for 0% -> 0% of each run, Pallas kernels for 36% -> 32%
where the time goes in v2:
time: 74.6 us; the launch traced here: 73.6 us
  Pallas kernels  27.3 us (37%)
  waiting for transfers between devices  24.4 us (33%)
  starting transfers between devices  20.7 us (28%)
  between operations  1.17 us (2%)
    ppermute x10, waiting for transfers between devices, shifted(): lax.ppermute(value, axis, [(i, (i + by) % peers) for i in range(peers)])  23.1 us
    ppermute x9, starting transfers between devices, swapped(): return lax.ppermute(value, 'group', [(i, i ^ by) for i in range(peers)])  16.9 us
    pallas_call x11, Pallas kernels, context_call(): pl.pallas_call(functools.partial(context_kernel, first, last, chunk * hei...  8.64 us
    pallas_call x5, Pallas kernels, weights_call(): pl.pallas_call(functools.partial(weights_kernel, stop), out_shape=[shape(...  6.13 us
    ppermute x10, starting transfers between devices, shifted(): lax.ppermute(value, axis, [(i, (i + by) % peers) for i in range(peers)])  3.78 us
    pallas_call x5, Pallas kernels, vertex_call(): pl.pallas_call(functools.partial(vertex_kernel, len(pts), len(cs) == 1),...  3.57 us
    pallas_call x5, Pallas kernels, relay_call(): pl.pallas_call(functools.partial(relay_kernel, stop), out_shape=[shape(2...  3.04 us
    pallas_call x1, Pallas kernels, final_call(): pl.pallas_call(functools.partial(final_kernel, n), out_shape=[shape(*v.sh...  2.24 us
  transfers between devices with their start and end apart: 19, of which 11 were waited for; matrix products, arithmetic and copies ran while one was open for 0% of the time, Pallas kernels for 32%

profile of v2, /device:TPU:0, one launch (start us, length us, event | category | flops | bytes accessed | tf_op | source)
XLA Modules:
  0.0 73.6 jit_solution(9271073632429979036)
XLA Ops:
  0.6 1.8 %pack.1 = (s32[8,128]{1,0:T(8,128)}, s32[8,128]{1,0:T(8,128)}, bf16[400,128]{1,0:T(8,128)(2,1)}, bf16[400,128]{1,0:T(8,128)(2,1)}) custom-call(s32[1]{0:T(128)} %bitcast.me_ref, bf16[4,6,3,128,128]{4,3,2,1,0:T(8,128)(2,1)} %bitcast.16, s32[3,4,6]{2,1,0:T(4,128)} %bitcast.32, s32[3,4,6]{2,1,0:T(4,128)} %bitcast.33, s32[4,6]{1,0:T(4,128)} %bitcast.34), custom_call_target="tpu_custom_call" | custom-call | tf_op jit(solution)/shard_map/pack/pallas_call | solution.py:405
  2.6 4.0 %collective-permute-start.2 = (bf16[400,128]{1,0:T(8,128)(2,1)}, bf16[400,128]{1,0:T(8,128)(2,1)S(1)}, u32[]{:S(2)}, u32[]{:S(2)}) collective-permute-start(bf16[400,128]{1,0:T(8,128)(2,1)} %get-tuple-element.78), channel_id=1, source_target_pairs={{0,64},{32,96},{64,0},{96,32},{1,65},{33,97},{65,1},{97,33},{2,66}... | collective-permute-start | bytes 307208 | tf_op jit(solution)/shard_map/ppermute | solution.py:389
  6.8 1.2 %collective-permute-done.after_ref.one_ref = s32[8,128]{1,0:T(8,128)S(1)} collective-permute-done((s32[8,128]{1,0:T(8,128)}, s32[8,128]{1,0:T(8,128)S(1)}, u32[]{:S(2)}, u32[]{:S(2)}) %collective-permute-start) | collective-permute-done | bytes 4128 | tf_op jit(solution)/shard_map/ppermute | solution.py:389
  8.9 3.3 %collective-permute-start.4 = (bf16[6,128,128]{2,1,0:T(8,128)(2,1)S(1)}, bf16[6,128,128]{2,1,0:T(8,128)(2,1)S(1)}, u32[]{:S(2)}, u32[]{:S(2)}) collective-permute-start(bf16[6,128,128]{2,1,0:T(8,128)(2,1)S(1)} %get-tuple-element.90), channel_id=1, source_target_pairs={{0,64},{32,96},{64,0},{96,32},{1,65},{33,97},{65,1},{97,33},{2,66}... | collective-permute-start | bytes 589832 | tf_op jit(solution)/shard_map/ppermute | solution.py:389
  12.2 1.0 %near_0.1 = (f32[33,128,128]{2,1,0:T(8,128)S(1)}, f32[32,128]{1,0:T(8,128)S(1)}) custom-call(s32[8,128]{1,0:T(8,128)S(1)} %copy-done.4, s32[8,128]{1,0:T(8,128)S(1)} %collective-permute-done.after_ref.one_ref, s32[6,2,8]{2,1,0:T(2,128)S(1)} %bitcast.23, bf16[6,128,128]{2,1,0:T(8,128)(2,1)S(1)} %get-tuple-element.80.near_ref), custom_call_target="tpu_custom_call" | custom-call | tf_op jit(solution)/shard_map/near_0/pallas_call | solution.py:436
  15.0 1.1 %collective-permute-start.5 = (bf16[272,256]{1,0:T(8,128)(2,1)S(1)}, bf16[272,256]{1,0:T(8,128)(2,1)S(1)}, u32[]{:S(2)}, u32[]{:S(2)}) collective-permute-start(bf16[272,256]{1,0:T(8,128)(2,1)S(1)} %get-tuple-element.93), channel_id=1, source_target_pairs={{0,1},{1,2},{2,3},{3,4},{4,5},{5,6},{6,7},{7,8},{8,9},{9,10},{10,1... | collective-permute-start | bytes 417800 | tf_op jit(solution)/shard_map/ppermute | solution.py:384
  16.8 2.1 %collective-permute-start.6 = (bf16[272,256]{1,0:T(8,128)(2,1)S(1)}, bf16[272,256]{1,0:T(8,128)(2,1)S(1)}, u32[]{:S(2)}, u32[]{:S(2)}) collective-permute-start(bf16[272,256]{1,0:T(8,128)(2,1)S(1)} %get-tuple-element.95), channel_id=1, source_target_pairs={{0,1},{1,2},{2,3},{3,4},{4,5},{5,6},{6,7},{7,8},{8,9},{9,10},{10,1... | collective-permute-start | bytes 417800 | tf_op jit(solution)/shard_map/ppermute | solution.py:384
  20.2 2.1 %collective-permute-start.7 = (bf16[6,128,128]{2,1,0:T(8,128)(2,1)S(1)}, bf16[6,128,128]{2,1,0:T(8,128)(2,1)S(1)}, u32[]{:S(2)}, u32[]{:S(2)}) collective-permute-start(bf16[6,128,128]{2,1,0:T(8,128)(2,1)S(1)} %get-tuple-element.101), channel_id=1, source_target_pairs={{0,64},{32,96},{64,0},{96,32},{1,65},{33,97},{65,1},{97,33},{2,66}... | collective-permute-start | bytes 589832 | tf_op jit(solution)/shard_map/ppermute | solution.py:389
  22.3 1.2 %weights_1.1 = (f32[33,128,128]{2,1,0:T(8,128)S(1)}, f32[32,128]{1,0:T(8,128)S(1)}) custom-call(s32[4,8,128]{2,1,0:T(8,128)S(1)} %get-tuple-element.88.ids_ref, s32[6,2,8]{2,1,0:T(2,128)S(1)} %bitcast.24, bf16[6,128,128]{2,1,0:T(8,128)(2,1)S(1)} %get-tuple-element.89.near_ref, bf16[6,128,128]{2,1,0:T(8,128)(2,1)S(1)} %collective-permute-done.4.far_ref), custom_call_target="tpu_custom_call" | custom-call | tf_op jit(solution)/shard_map/weights_1/pallas_call | solution.py:356
  23.5 2.3 %collective-permute-done.5.refs_0_.refs_2_ = bf16[272,256]{1,0:T(8,128)(2,1)S(1)} collective-permute-done((bf16[272,256]{1,0:T(8,128)(2,1)S(1)}, bf16[272,256]{1,0:T(8,128)(2,1)S(1)}, u32[]{:S(2)}, u32[]{:S(2)}) %collective-permute-start.5) | collective-permute-done | bytes 139296 | tf_op jit(solution)/shard_map/ppermute | solution.py:384
  26.7 1.2 %collective-permute-done.6.refs_0_.refs_3_ = bf16[272,256]{1,0:T(8,128)(2,1)S(1)} collective-permute-done((bf16[272,256]{1,0:T(8,128)(2,1)S(1)}, bf16[272,256]{1,0:T(8,128)(2,1)S(1)}, u32[]{:S(2)}, u32[]{:S(2)}) %collective-permute-start.6) | collective-permute-done | bytes 139296 | tf_op jit(solution)/shard_map/ppermute | solution.py:384
  30.1 2.6 %collective-permute-start.10 = (bf16[6,128,128]{2,1,0:T(8,128)(2,1)S(1)}, bf16[6,128,128]{2,1,0:T(8,128)(2,1)S(1)}, u32[]{:S(2)}, u32[]{:S(2)}) collective-permute-start(bf16[6,128,128]{2,1,0:T(8,128)(2,1)S(1)} %get-tuple-element.112), channel_id=1, source_target_pairs={{0,64},{32,96},{64,0},{96,32},{1,65},{33,97},{65,1},{97,33},{2,66}... | collective-permute-start | bytes 589832 | tf_op jit(solution)/shard_map/ppermute | solution.py:389
  32.7 1.2 %weights_2.1 = (f32[33,128,128]{2,1,0:T(8,128)S(1)}, f32[32,128]{1,0:T(8,128)S(1)}) custom-call(s32[4,8,128]{2,1,0:T(8,128)S(1)} %get-tuple-element.88.ids_ref, s32[6,2,8]{2,1,0:T(2,128)S(1)} %bitcast.25, bf16[6,128,128]{2,1,0:T(8,128)(2,1)S(1)} %get-tuple-element.100.near_ref, bf16[6,128,128]{2,1,0:T(8,128)(2,1)S(1)} %collective-permute-done.7.far_ref), custom_call_target="tpu_custom_call" | custom-call | tf_op jit(solution)/shard_map/weights_2/pallas_call | solution.py:356
  34.0 3.4 %collective-permute-done.8.refs_0_.refs_2_ = bf16[272,256]{1,0:T(8,128)(2,1)S(1)} collective-permute-done((bf16[272,256]{1,0:T(8,128)(2,1)S(1)}, bf16[272,256]{1,0:T(8,128)(2,1)S(1)}, u32[]{:S(2)}, u32[]{:S(2)}) %collective-permute-start.8) | collective-permute-done | bytes 139296 | tf_op jit(solution)/shard_map/ppermute | solution.py:384
  38.2 0.9 %collective-permute-done.9.refs_0_.refs_3_ = bf16[272,256]{1,0:T(8,128)(2,1)S(1)} collective-permute-done((bf16[272,256]{1,0:T(8,128)(2,1)S(1)}, bf16[272,256]{1,0:T(8,128)(2,1)S(1)}, u32[]{:S(2)}, u32[]{:S(2)}) %collective-permute-start.9) | collective-permute-done | bytes 139296 | tf_op jit(solution)/shard_map/ppermute | solution.py:384
  41.2 2.1 %collective-permute-start.13 = (bf16[6,128,128]{2,1,0:T(8,128)(2,1)S(1)}, bf16[6,128,128]{2,1,0:T(8,128)(2,1)S(1)}, u32[]{:S(2)}, u32[]{:S(2)}) collective-permute-start(bf16[6,128,128]{2,1,0:T(8,128)(2,1)S(1)} %get-tuple-element.123), channel_id=1, source_target_pairs={{0,64},{32,96},{64,0},{96,32},{1,65},{33,97},{65,1},{97,33},{2,66}... | collective-permute-start | bytes 589832 | tf_op jit(solution)/shard_map/ppermute | solution.py:389
  43.4 1.2 %weights_3.1 = (f32[33,128,128]{2,1,0:T(8,128)S(1)}, f32[32,128]{1,0:T(8,128)S(1)}) custom-call(s32[4,8,128]{2,1,0:T(8,128)S(1)} %get-tuple-element.88.ids_ref, s32[6,2,8]{2,1,0:T(2,128)S(1)} %bitcast.26, bf16[6,128,128]{2,1,0:T(8,128)(2,1)S(1)} %get-tuple-element.111.near_ref, bf16[6,128,128]{2,1,0:T(8,128)(2,1)S(1)} %collective-permute-done.10.far_ref), custom_call_target="tpu_custom_call" | custom-call | tf_op jit(solution)/shard_map/weights_3/pallas_call | solution.py:356
  44.6 4.0 %collective-permute-done.11.refs_0_.refs_2_ = bf16[272,256]{1,0:T(8,128)(2,1)S(1)} collective-permute-done((bf16[272,256]{1,0:T(8,128)(2,1)S(1)}, bf16[272,256]{1,0:T(8,128)(2,1)S(1)}, u32[]{:S(2)}, u32[]{:S(2)}) %collective-permute-start.11) | collective-permute-done | bytes 139296 | tf_op jit(solution)/shard_map/ppermute | solution.py:384
  52.3 2.5 %collective-permute-start.16 = (bf16[6,128,128]{2,1,0:T(8,128)(2,1)S(1)}, bf16[6,128,128]{2,1,0:T(8,128)(2,1)S(1)}, u32[]{:S(2)}, u32[]{:S(2)}) collective-permute-start(bf16[6,128,128]{2,1,0:T(8,128)(2,1)S(1)} %get-tuple-element.134), channel_id=1, source_target_pairs={{0,64},{32,96},{64,0},{96,32},{1,65},{33,97},{65,1},{97,33},{2,66}... | collective-permute-start | bytes 589832 | tf_op jit(solution)/shard_map/ppermute | solution.py:389
  54.8 1.2 %weights_4.1 = (f32[33,128,128]{2,1,0:T(8,128)S(1)}, f32[32,128]{1,0:T(8,128)S(1)}) custom-call(s32[4,8,128]{2,1,0:T(8,128)S(1)} %get-tuple-element.88.ids_ref, s32[6,2,8]{2,1,0:T(2,128)S(1)} %bitcast.27, bf16[6,128,128]{2,1,0:T(8,128)(2,1)S(1)} %get-tuple-element.122.near_ref, bf16[6,128,128]{2,1,0:T(8,128)(2,1)S(1)} %collective-permute-done.13.far_ref), custom_call_target="tpu_custom_call" | custom-call | tf_op jit(solution)/shard_map/weights_4/pallas_call | solution.py:356
  56.0 3.0 %collective-permute-done.14.refs_0_.refs_2_ = bf16[272,256]{1,0:T(8,128)(2,1)S(1)} collective-permute-done((bf16[272,256]{1,0:T(8,128)(2,1)S(1)}, bf16[272,256]{1,0:T(8,128)(2,1)S(1)}, u32[]{:S(2)}, u32[]{:S(2)}) %collective-permute-start.14) | collective-permute-done | bytes 139296 | tf_op jit(solution)/shard_map/ppermute | solution.py:384
  62.1 1.2 %weights_5.1 = (f32[33,128,128]{2,1,0:T(8,128)S(1)}, f32[32,128]{1,0:T(8,128)S(1)}) custom-call(s32[4,8,128]{2,1,0:T(8,128)S(1)} %get-tuple-element.88.ids_ref, s32[6,2,8]{2,1,0:T(2,128)S(1)} %bitcast.28, bf16[6,128,128]{2,1,0:T(8,128)(2,1)S(1)} %get-tuple-element.133.near_ref, bf16[6,128,128]{2,1,0:T(8,128)(2,1)S(1)} %collective-permute-done.16.far_ref), custom_call_target="tpu_custom_call" | custom-call | tf_op jit(solution)/shard_map/weights_5/pallas_call | solution.py:356
  63.4 6.3 %collective-permute-done.17.refs_0_ = bf16[272,256]{1,0:T(8,128)(2,1)S(1)} collective-permute-done((bf16[272,256]{1,0:T(8,128)(2,1)S(1)}, bf16[272,256]{1,0:T(8,128)(2,1)S(1)}, u32[]{:S(2)}, u32[]{:S(2)}) %collective-permute-start.17) | collective-permute-done | bytes 139296 | tf_op jit(solution)/shard_map/ppermute | solution.py:384
  71.2 2.2 %final.1 = (f32[1024,256]{1,0:T(8,128)}, f32[8,128]{1,0:T(8,128)}, f32[512,256]{1,0:T(8,128)}, f32[4,128]{1,0:T(4,128)}) custom-call(bf16[1024,256]{1,0:T(8,128)(2,1)S(1)} %get-tuple-element.132.v_ref, f32[33,128,128]{2,1,0:T(8,128)S(1)} %get-tuple-element.135.w_ref, f32[32,128]{1,0:T(8,128)S(1)} %get-tuple-element.136.q_ref, ...), custom_call_target="tpu_custom_call" | custom-call | tf_op jit(solution)/shard_map/final/pallas_call | solution.py:331
  (58 shorter events, 19.0 us)
Async XLA Ops:
  2.5 5.6 %collective-permute-start.1 = (bf16[4,6,3,128,128]{4,3,2,1,0:T(8,128)(2,1)S(1)}, bf16[4,6,3,128,128]{4,3,2,1,0:T(8,128)(2,1)S(1)}, u32[]{:S(2)}, u32[]{:S(2)}) collective-permute-start(bf16[4,6,3,128,128]{4,3,2,1,0:T(8,128)(2,1)S(1)} %bitcast.17), channel_id=1, source_target_pairs={{0,32},{32,0},{64,96},{96,64},{1,33},{33,1},{65,97},{97,65},{2,34}... | collective-permute-start | bytes 7077896 | tf_op jit(solution)/shard_map/ppermute | solution.py:389
  2.6 10.7 %collective-permute-start.2 = (bf16[400,128]{1,0:T(8,128)(2,1)}, bf16[400,128]{1,0:T(8,128)(2,1)S(1)}, u32[]{:S(2)}, u32[]{:S(2)}) collective-permute-start(bf16[400,128]{1,0:T(8,128)(2,1)} %get-tuple-element.78), channel_id=1, source_target_pairs={{0,64},{32,96},{64,0},{96,32},{1,65},{33,97},{65,1},{97,33},{2,66}... | collective-permute-start | bytes 307208 | tf_op jit(solution)/shard_map/ppermute | solution.py:389
  6.6 6.7 %collective-permute-start.3 = (bf16[400,128]{1,0:T(8,128)(2,1)}, bf16[400,128]{1,0:T(8,128)(2,1)S(1)}, u32[]{:S(2)}, u32[]{:S(2)}) collective-permute-start(bf16[400,128]{1,0:T(8,128)(2,1)} %get-tuple-element.82), channel_id=1, source_target_pairs={{0,96},{32,64},{64,32},{96,0},{1,97},{33,65},{65,33},{97,1},{2,98}... | collective-permute-start | bytes 307208 | tf_op jit(solution)/shard_map/ppermute | solution.py:389
  6.7 5.6 %copy-start.3 = (s32[1,1,6,8,2]{3,4,2,1,0:T(2,128)S(1)}, s32[1,1,6,8,2]{3,4,2,1,0:T(2,128)}, u32[]{:S(2)}) copy-start(s32[1,1,6,8,2]{3,4,2,1,0:T(2,128)} %param.17) | copy-start | bytes 1156
  6.7 5.6 %copy-start.4 = (s32[8,128]{1,0:T(8,128)S(1)}, s32[8,128]{1,0:T(8,128)}, u32[]{:S(2)}) copy-start(s32[8,128]{1,0:T(8,128)} %get-tuple-element.76.own_ref) | copy-start | bytes 12292
  6.7 1.4 %collective-permute-start = (s32[8,128]{1,0:T(8,128)}, s32[8,128]{1,0:T(8,128)S(1)}, u32[]{:S(2)}, u32[]{:S(2)}) collective-permute-start(s32[8,128]{1,0:T(8,128)} %get-tuple-element.77), channel_id=1, source_target_pairs={{0,32},{32,0},{64,96},{96,64},{1,33},{33,1},{65,97},{97,65},{2,34}... | collective-permute-start | bytes 12296 | tf_op jit(solution)/shard_map/ppermute | solution.py:389
  8.9 5.3 %copy-start.1 = (f32[1024,256]{1,0:T(8,128)S(1)}, f32[1024,256]{1,0:T(8,128)}, u32[]{:S(2)}) copy-start(f32[1024,256]{1,0:T(8,128)} %refs_3_.1) | copy-start | bytes 3145732
  8.9 5.3 %copy-start.2 = (f32[512,256]{1,0:T(8,128)S(1)}, f32[512,256]{1,0:T(8,128)}, u32[]{:S(2)}) copy-start(f32[512,256]{1,0:T(8,128)} %refs_2_.1) | copy-start | bytes 1572868
  8.9 5.3 %copy-start.5 = (f32[512]{0:T(512)S(1)}, f32[512]{0:T(512)}, u32[]{:S(2)}) copy-start(f32[512]{0:T(512)} %param.12) | copy-start | bytes 6148
  8.9 13.4 %collective-permute-start.4 = (bf16[6,128,128]{2,1,0:T(8,128)(2,1)S(1)}, bf16[6,128,128]{2,1,0:T(8,128)(2,1)S(1)}, u32[]{:S(2)}, u32[]{:S(2)}) collective-permute-start(bf16[6,128,128]{2,1,0:T(8,128)(2,1)S(1)} %get-tuple-element.90), channel_id=1, source_target_pairs={{0,64},{32,96},{64,0},{96,32},{1,65},{33,97},{65,1},{97,33},{2,66}... | collective-permute-start | bytes 589832 | tf_op jit(solution)/shard_map/ppermute | solution.py:389
  15.0 10.9 %collective-permute-start.5 = (bf16[272,256]{1,0:T(8,128)(2,1)S(1)}, bf16[272,256]{1,0:T(8,128)(2,1)S(1)}, u32[]{:S(2)}, u32[]{:S(2)}) collective-permute-start(bf16[272,256]{1,0:T(8,128)(2,1)S(1)} %get-tuple-element.93), channel_id=1, source_target_pairs={{0,1},{1,2},{2,3},{3,4},{4,5},{5,6},{6,7},{7,8},{8,9},{9,10},{10,1... | collective-permute-start | bytes 417800 | tf_op jit(solution)/shard_map/ppermute | solution.py:384
  16.8 11.1 %collective-permute-start.6 = (bf16[272,256]{1,0:T(8,128)(2,1)S(1)}, bf16[272,256]{1,0:T(8,128)(2,1)S(1)}, u32[]{:S(2)}, u32[]{:S(2)}) collective-permute-start(bf16[272,256]{1,0:T(8,128)(2,1)S(1)} %get-tuple-element.95), channel_id=1, source_target_pairs={{0,1},{1,2},{2,3},{3,4},{4,5},{5,6},{6,7},{7,8},{8,9},{9,10},{10,1... | collective-permute-start | bytes 417800 | tf_op jit(solution)/shard_map/ppermute | solution.py:384
  20.2 12.5 %collective-permute-start.7 = (bf16[6,128,128]{2,1,0:T(8,128)(2,1)S(1)}, bf16[6,128,128]{2,1,0:T(8,128)(2,1)S(1)}, u32[]{:S(2)}, u32[]{:S(2)}) collective-permute-start(bf16[6,128,128]{2,1,0:T(8,128)(2,1)S(1)} %get-tuple-element.101), channel_id=1, source_target_pairs={{0,64},{32,96},{64,0},{96,32},{1,65},{33,97},{65,1},{97,33},{2,66}... | collective-permute-start | bytes 589832 | tf_op jit(solution)/shard_map/ppermute | solution.py:389
  26.7 10.7 %collective-permute-start.8 = (bf16[272,256]{1,0:T(8,128)(2,1)S(1)}, bf16[272,256]{1,0:T(8,128)(2,1)S(1)}, u32[]{:S(2)}, u32[]{:S(2)}) collective-permute-start(bf16[272,256]{1,0:T(8,128)(2,1)S(1)} %get-tuple-element.104), channel_id=1, source_target_pairs={{0,1},{1,2},{2,3},{3,4},{4,5},{5,6},{6,7},{7,8},{8,9},{9,10},{10,1... | collective-permute-start | bytes 417800 | tf_op jit(solution)/shard_map/ppermute | solution.py:384
  28.8 10.3 %collective-permute-start.9 = (bf16[272,256]{1,0:T(8,128)(2,1)S(1)}, bf16[272,256]{1,0:T(8,128)(2,1)S(1)}, u32[]{:S(2)}, u32[]{:S(2)}) collective-permute-start(bf16[272,256]{1,0:T(8,128)(2,1)S(1)} %get-tuple-element.106), channel_id=1, source_target_pairs={{0,1},{1,2},{2,3},{3,4},{4,5},{5,6},{6,7},{7,8},{8,9},{9,10},{10,1... | collective-permute-start | bytes 417800 | tf_op jit(solution)/shard_map/ppermute | solution.py:384
  30.1 13.2 %collective-permute-start.10 = (bf16[6,128,128]{2,1,0:T(8,128)(2,1)S(1)}, bf16[6,128,128]{2,1,0:T(8,128)(2,1)S(1)}, u32[]{:S(2)}, u32[]{:S(2)}) collective-permute-start(bf16[6,128,128]{2,1,0:T(8,128)(2,1)S(1)} %get-tuple-element.112), channel_id=1, source_target_pairs={{0,64},{32,96},{64,0},{96,32},{1,65},{33,97},{65,1},{97,33},{2,66}... | collective-permute-start | bytes 589832 | tf_op jit(solution)/shard_map/ppermute | solution.py:389
  38.1 10.5 %collective-permute-start.11 = (bf16[272,256]{1,0:T(8,128)(2,1)S(1)}, bf16[272,256]{1,0:T(8,128)(2,1)S(1)}, u32[]{:S(2)}, u32[]{:S(2)}) collective-permute-start(bf16[272,256]{1,0:T(8,128)(2,1)S(1)} %get-tuple-element.115), channel_id=1, source_target_pairs={{0,1},{1,2},{2,3},{3,4},{4,5},{5,6},{6,7},{7,8},{8,9},{9,10},{10,1... | collective-permute-start | bytes 417800 | tf_op jit(solution)/shard_map/ppermute | solution.py:384
  39.9 10.2 %collective-permute-start.12 = (bf16[272,256]{1,0:T(8,128)(2,1)S(1)}, bf16[272,256]{1,0:T(8,128)(2,1)S(1)}, u32[]{:S(2)}, u32[]{:S(2)}) collective-permute-start(bf16[272,256]{1,0:T(8,128)(2,1)S(1)} %get-tuple-element.117), channel_id=1, source_target_pairs={{0,1},{1,2},{2,3},{3,4},{4,5},{5,6},{6,7},{7,8},{8,9},{9,10},{10,1... | collective-permute-start | bytes 417800 | tf_op jit(solution)/shard_map/ppermute | solution.py:384
  41.2 13.5 %collective-permute-start.13 = (bf16[6,128,128]{2,1,0:T(8,128)(2,1)S(1)}, bf16[6,128,128]{2,1,0:T(8,128)(2,1)S(1)}, u32[]{:S(2)}, u32[]{:S(2)}) collective-permute-start(bf16[6,128,128]{2,1,0:T(8,128)(2,1)S(1)} %get-tuple-element.123), channel_id=1, source_target_pairs={{0,64},{32,96},{64,0},{96,32},{1,65},{33,97},{65,1},{97,33},{2,66}... | collective-permute-start | bytes 589832 | tf_op jit(solution)/shard_map/ppermute | solution.py:389
  49.4 9.6 %collective-permute-start.14 = (bf16[272,256]{1,0:T(8,128)(2,1)S(1)}, bf16[272,256]{1,0:T(8,128)(2,1)S(1)}, u32[]{:S(2)}, u32[]{:S(2)}) collective-permute-start(bf16[272,256]{1,0:T(8,128)(2,1)S(1)} %get-tuple-element.126), channel_id=1, source_target_pairs={{0,1},{1,2},{2,3},{3,4},{4,5},{5,6},{6,7},{7,8},{8,9},{9,10},{10,1... | collective-permute-start | bytes 417800 | tf_op jit(solution)/shard_map/ppermute | solution.py:384
  50.9 9.6 %collective-permute-start.15 = (bf16[272,256]{1,0:T(8,128)(2,1)S(1)}, bf16[272,256]{1,0:T(8,128)(2,1)S(1)}, u32[]{:S(2)}, u32[]{:S(2)}) collective-permute-start(bf16[272,256]{1,0:T(8,128)(2,1)S(1)} %get-tuple-element.128), channel_id=1, source_target_pairs={{0,1},{1,2},{2,3},{3,4},{4,5},{5,6},{6,7},{7,8},{8,9},{9,10},{10,1... | collective-permute-start | bytes 417800 | tf_op jit(solution)/shard_map/ppermute | solution.py:384
  52.3 9.9 %collective-permute-start.16 = (bf16[6,128,128]{2,1,0:T(8,128)(2,1)S(1)}, bf16[6,128,128]{2,1,0:T(8,128)(2,1)S(1)}, u32[]{:S(2)}, u32[]{:S(2)}) collective-permute-start(bf16[6,128,128]{2,1,0:T(8,128)(2,1)S(1)} %get-tuple-element.134), channel_id=1, source_target_pairs={{0,64},{32,96},{64,0},{96,32},{1,65},{33,97},{65,1},{97,33},{2,66}... | collective-permute-start | bytes 589832 | tf_op jit(solution)/shard_map/ppermute | solution.py:389
  59.8 9.9 %collective-permute-start.17 = (bf16[272,256]{1,0:T(8,128)(2,1)S(1)}, bf16[272,256]{1,0:T(8,128)(2,1)S(1)}, u32[]{:S(2)}, u32[]{:S(2)}) collective-permute-start(bf16[272,256]{1,0:T(8,128)(2,1)S(1)} %get-tuple-element.137), channel_id=1, source_target_pairs={{0,1},{1,2},{2,3},{3,4},{4,5},{5,6},{6,7},{7,8},{8,9},{9,10},{10,1... | collective-permute-start | bytes 417800 | tf_op jit(solution)/shard_map/ppermute | solution.py:384
  61.3 9.9 %collective-permute-start.18 = (bf16[272,256]{1,0:T(8,128)(2,1)S(1)}, bf16[272,256]{1,0:T(8,128)(2,1)S(1)}, u32[]{:S(2)}, u32[]{:S(2)}) collective-permute-start(bf16[272,256]{1,0:T(8,128)(2,1)S(1)} %get-tuple-element.138), channel_id=1, source_target_pairs={{0,1},{1,2},{2,3},{3,4},{4,5},{5,6},{6,7},{7,8},{8,9},{9,10},{10,1... | collective-permute-start | bytes 417800 | tf_op jit(solution)/shard_map/ppermute | solution.py:384
  (2 other events, 5.8 us)

commit v3 on v2

--- a/solution.py
+++ b/solution.py
@@ -70,18 +70,18 @@
 def update_context(base, c_bf, c_now, states, v_ref, w_ref, q_ref, pt_ref):
     rows_v, height = v_ref.shape[0], c_bf.shape[0]
     rt, ct = rows_v // TILE, height // TILE
+    c_half = c_bf * jnp.asarray(0.5, BF16)
     for block in range(rows_v // BLOCK):
         v_block = v_ref[block * BLOCK : (block + 1) * BLOCK, :].astype(BF16)
-        t_val = jnp.tanh(0.5 * dot(c_bf, v_block, NT))
+        t_val = jnp.tanh(dot(c_half, v_block, NT))
         for c in range(ct):
             for k in range(BLOCK // TILE):
                 r = block * (BLOCK // TILE) + k
                 pair = (base + c) * rt + r
-                q = q_ref[pair : pair + 1, :]
-                half = w_ref[pair]
+                both = 2.0 * q_ref[pair : pair + 1, :]
                 tt = t_val[c * TILE : (c + 1) * TILE, k * TILE : (k + 1) * TILE]
                 pt_ref[c * TILE : (c + 1) * TILE, r * TILE : (r + 1) * TILE] = (
-                    half * (tt - 1.0) + q * (tt + 1.0)
+                    w_ref[pair] * (tt - 1.0) + both
                 ).astype(BF16)
 
     grad = dot(pt_ref[...], v_ref[...].astype(BF16), NN)
@@ -177,13 +177,15 @@
         copy.wait()
 
 
-def fill_counts(stop, neg_ref, q_ref):
+def fill_counts(stop, neg_ref, out_ref, q_ref):
     per_stop, rt = neg_ref.shape[1:]
     for pair in range(PAIRS):
         count = jnp.int32(0)
         for n in range(per_stop):
             count += (neg_ref[stop, n, pair % rt] == pair // rt).astype(jnp.int32)
-        q_ref[pair : pair + 1, :] = jnp.full((1, TILE), 0.25 * count.astype(F32))
+        value = 0.25 * count.astype(F32)
+        q_ref[pair : pair + 1, :] = jnp.full((1, TILE), value)
+        out_ref[pair] = jnp.full((TILE, TILE), value)
 
 
 def add_tiles(out_ref, tiles):
@@ -192,8 +194,7 @@
 
 
 def near_kernel(own_ref, one_ref, neg_ref, near_ref, out_ref, q_ref):
-    fill_counts(0, neg_ref, q_ref)
-    out_ref[...] = jnp.zeros_like(out_ref)
+    fill_counts(0, neg_ref, out_ref, q_ref)
     cap = near_ref.shape[0] // 2
     add_tiles(
         out_ref,
@@ -222,8 +223,7 @@
 
 
 def weights_kernel(stop, ids_ref, neg_ref, near_ref, far_ref, out_ref, q_ref):
-    fill_counts(stop, neg_ref, q_ref)
-    out_ref[...] = jnp.zeros_like(out_ref)
+    fill_counts(stop, neg_ref, out_ref, q_ref)
     cap = far_ref.shape[0] // 2
     tiles = [ref[t] for ref in (near_ref, far_ref) for t in range(2 * cap)]
     add_tiles(out_ref, [(ids_ref[at // cap, at % cap, stop], tile) for at, tile in enumerate(tiles)])
@@ -268,16 +268,16 @@
         copy.wait()
 
 
-def relay_kernel(stop, me_ref, w_ref, sib_ref, after_ref, *refs):
+def relay_kernel(wanted, me_ref, w_ref, sib_ref, after_ref, *refs):
     *out_refs, sem = refs
     me = me_ref[0]
     cap = w_ref.shape[2]
     copies = []
-    for n, (dst, by, at) in enumerate(zip(out_refs, (2, 0, 0), (stop, stop, 0))):
+    for n, (dst, (by, stop)) in enumerate(zip(out_refs, wanted)):
         for half, src in enumerate((w_ref, sib_ref)):
             copies.append(
                 pltpu.make_async_copy(
-                    src.at[me ^ by, at], dst.at[pl.ds(half * cap, cap)], sem.at[2 * n + half]
+                    src.at[me ^ by, stop], dst.at[pl.ds(half * cap, cap)], sem.at[2 * n + half]
                 )
             )
     for copy in copies:
@@ -364,18 +364,17 @@
     )(ids, neg, near, far)
 
 
-def relay_call(stop, me, weights, sibling, after):
+def relay_call(wanted, me, weights, sibling, after):
     cap = weights.shape[2]
-    count = 3 if stop == 1 else 2
     return pl.pallas_call(
-        functools.partial(relay_kernel, stop),
-        out_shape=[shape(2 * cap, TILE, TILE)] * count,
+        functools.partial(relay_kernel, wanted),
+        out_shape=[shape(2 * cap, TILE, TILE)] * len(wanted),
         in_specs=[SM, HBM, HBM, HBM],
-        out_specs=[VM] * count,
-        scratch_shapes=[pltpu.SemaphoreType.DMA((2 * count,))],
-        compiler_params=params(),
-        cost_estimate=FREE,
-        name="relay_%d" % stop,
+        out_specs=[VM] * len(wanted),
+        scratch_shapes=[pltpu.SemaphoreType.DMA((2 * len(wanted),))],
+        compiler_params=params(),
+        cost_estimate=FREE,
+        name="relay_%d" % wanted[0][1],
     )(me, weights, sibling, after)
 
 
@@ -427,12 +426,8 @@
     sibling = swapped(later, 1)
     two, three, one_ids = swapped(msgs[0], 2), swapped(msgs[1], 3), swapped(one_ids, 1)
 
-    def relay(stop, after):
-        far, *near = relay_call(stop, me, weights, sibling, after)
-        return near, swapped(far, 2)
-
-    (near, near_first), far = relay(1, one_ids)
-    arrived = {1: ((near,), far)}
+    far, near, near_first = relay_call(((2, 1), (0, 1), (0, 0)), me, weights, sibling, one_ids)
+    arrived = {1: (near, swapped(far, 2))}
     part, q = pl.pallas_call(
         near_kernel,
         out_shape=[shape(PAIRS + 1, TILE, TILE, dtype=F32), shape(PAIRS, TILE, dtype=F32)],
@@ -465,11 +460,14 @@
             pt, new = context_call(stop, stop == 0, False, chunk, v_bf, given, w_sum, q)
             pts.append(pt)
             sent.append(shifted(new, "blk", 1))
-        (near,), far = arrived[stop + 1]
-        w_sum, q = weights_call(stop + 1, ids, neg, near, far)
+        w_sum, q = weights_call(stop + 1, ids, neg, *arrived[stop + 1])
         v, vs, v_bf = vertex_call(stop, pts, [context] if stop == 0 else held, v, vs)
         if stop + 2 < stops:
-            arrived[stop + 2] = relay(stop + 2, vs)
+            if stop == 0:
+                wanted = tuple((by, later) for later in range(2, stops) for by in (2, 0))
+                pieces = relay_call(wanted, me, weights, sibling, vs)
+            far, _ = lax.optimization_barrier((pieces[2 * stop], vs))
+            arrived[stop + 2] = (pieces[2 * stop + 1], swapped(far, 2))
         held = sent
     done = []
     for chunk in range(CHUNKS - 1):

time: 74.6 us -> 74.6 us (level); the launches traced: 73.6 us -> 74.4 us
  waiting for transfers between devices: 24.4 us -> 25.7 us
    ppermute x10, starting transfers between devices: 3.78 us -> 5.15 us  [shifted(): lax.ppermute(value, axis, [(i, (i + by) % peers) for i in range(peers)])]
    ppermute x9, starting transfers between devices: 16.9 us -> 15.8 us  [swapped(): return lax.ppermute(value, 'group', [(i, i ^ by) for i in range(peers)])]
    ppermute x9, waiting for transfers between devices: 1.25 us -> 2.37 us  [swapped(): return lax.ppermute(value, 'group', [(i, i ^ by) for i in range(peers)])]
    pallas_call x5 -> x2, Pallas kernels: 3.04 us -> 3.02 us  [relay_call(): pl.pallas_call(functools.partial(relay_kernel, wanted), out_shape=[shape(...]
  transfers between devices with their start and end apart: 19 -> 19, of which waited for: 11 -> 12; matrix products, arithmetic and copies ran while one was open for 0% -> 0% of each run, Pallas kernels for 32% -> 31%
where the time goes in v3:
time: 74.6 us; the launch traced here: 74.4 us
  Pallas kernels  26.7 us (36%)
  waiting for transfers between devices  25.7 us (34%)
  starting transfers between devices  20.9 us (28%)
  between operations  1.12 us (2%)
    ppermute x10, waiting for transfers between devices, shifted(): lax.ppermute(value, axis, [(i, (i + by) % peers) for i in range(peers)])  23.3 us
    ppermute x9, starting transfers between devices, swapped(): return lax.ppermute(value, 'group', [(i, i ^ by) for i in range(peers)])  15.8 us
    pallas_call x11, Pallas kernels, context_call(): pl.pallas_call(functools.partial(context_kernel, first, last, chunk * hei...  8.58 us
    pallas_call x5, Pallas kernels, weights_call(): pl.pallas_call(functools.partial(weights_kernel, stop), out_shape=[shape(...  5.83 us
    ppermute x10, starting transfers between devices, shifted(): lax.ppermute(value, axis, [(i, (i + by) % peers) for i in range(peers)])  5.15 us
    pallas_call x5, Pallas kernels, vertex_call(): pl.pallas_call(functools.partial(vertex_kernel, len(pts), len(cs) == 1),...  3.5 us
    pallas_call x2, Pallas kernels, relay_call(): pl.pallas_call(functools.partial(relay_kernel, wanted), out_shape=[shape(...  3.02 us
    ppermute x9, waiting for transfers between devices, swapped(): return lax.ppermute(value, 'group', [(i, i ^ by) for i in range(peers)])  2.37 us
  transfers between devices with their start and end apart: 19, of which 12 were waited for; matrix products, arithmetic and copies ran while one was open for 0% of the time, Pallas kernels for 31%

profile of v3, /device:TPU:0, one launch (start us, length us, event | category | flops | bytes accessed | tf_op | source)
XLA Modules:
  0.0 74.4 jit_solution(5139696704592817914)
XLA Ops:
  0.6 1.8 %pack.1 = (s32[8,128]{1,0:T(8,128)}, s32[8,128]{1,0:T(8,128)}, bf16[400,128]{1,0:T(8,128)(2,1)}, bf16[400,128]{1,0:T(8,128)(2,1)}) custom-call(s32[1]{0:T(128)} %bitcast.me_ref, bf16[4,6,3,128,128]{4,3,2,1,0:T(8,128)(2,1)} %bitcast.16, s32[3,4,6]{2,1,0:T(4,128)} %bitcast.29, s32[3,4,6]{2,1,0:T(4,128)} %bitcast.30, s32[4,6]{1,0:T(4,128)} %bitcast.31), custom_call_target="tpu_custom_call" | custom-call | tf_op jit(solution)/shard_map/pack/pallas_call | solution.py:404
  2.6 4.0 %collective-permute-start.2 = (bf16[400,128]{1,0:T(8,128)(2,1)}, bf16[400,128]{1,0:T(8,128)(2,1)S(1)}, u32[]{:S(2)}, u32[]{:S(2)}) collective-permute-start(bf16[400,128]{1,0:T(8,128)(2,1)} %get-tuple-element.82), channel_id=1, source_target_pairs={{0,64},{32,96},{64,0},{96,32},{1,65},{33,97},{65,1},{97,33},{2,66}... | collective-permute-start | bytes 307208 | tf_op jit(solution)/shard_map/ppermute | solution.py:388
  6.8 1.2 %collective-permute-done.after_ref.one_ref = s32[8,128]{1,0:T(8,128)S(1)} collective-permute-done((s32[8,128]{1,0:T(8,128)}, s32[8,128]{1,0:T(8,128)S(1)}, u32[]{:S(2)}, u32[]{:S(2)}) %collective-permute-start) | collective-permute-done | bytes 4128 | tf_op jit(solution)/shard_map/ppermute | solution.py:388
  8.9 3.3 %collective-permute-start.4 = (bf16[6,128,128]{2,1,0:T(8,128)(2,1)S(1)}, bf16[6,128,128]{2,1,0:T(8,128)(2,1)S(1)}, u32[]{:S(2)}, u32[]{:S(2)}) collective-permute-start(bf16[6,128,128]{2,1,0:T(8,128)(2,1)S(1)} %get-tuple-element.94), channel_id=1, source_target_pairs={{0,64},{32,96},{64,0},{96,32},{1,65},{33,97},{65,1},{97,33},{2,66}... | collective-permute-start | bytes 589832 | tf_op jit(solution)/shard_map/ppermute | solution.py:388
  14.9 1.1 %collective-permute-start.5 = (bf16[272,256]{1,0:T(8,128)(2,1)S(1)}, bf16[272,256]{1,0:T(8,128)(2,1)S(1)}, u32[]{:S(2)}, u32[]{:S(2)}) collective-permute-start(bf16[272,256]{1,0:T(8,128)(2,1)S(1)} %get-tuple-element.97), channel_id=1, source_target_pairs={{0,1},{1,2},{2,3},{3,4},{4,5},{5,6},{6,7},{7,8},{8,9},{9,10},{10,1... | collective-permute-start | bytes 417800 | tf_op jit(solution)/shard_map/ppermute | solution.py:383
  16.8 2.1 %collective-permute-start.6 = (bf16[272,256]{1,0:T(8,128)(2,1)S(1)}, bf16[272,256]{1,0:T(8,128)(2,1)S(1)}, u32[]{:S(2)}, u32[]{:S(2)}) collective-permute-start(bf16[272,256]{1,0:T(8,128)(2,1)S(1)} %get-tuple-element.99), channel_id=1, source_target_pairs={{0,1},{1,2},{2,3},{3,4},{4,5},{5,6},{6,7},{7,8},{8,9},{9,10},{10,1... | collective-permute-start | bytes 417800 | tf_op jit(solution)/shard_map/ppermute | solution.py:383
  19.6 2.2 %relay_2.1 = (bf16[6,128,128]{2,1,0:T(8,128)(2,1)S(1)}, bf16[6,128,128]{2,1,0:T(8,128)(2,1)S(1)}, bf16[6,128,128]{2,1,0:T(8,128)(2,1)S(1)}, bf16[6,128,128]{2,1,...) custom-call(s32[1]{0:T(128)} %bitcast.me_ref, ...), custom_call_target="tpu_custom_call" | custom-call | tf_op jit(solution)/shard_map/relay_2/pallas_call | solution.py:369
  21.8 2.1 %collective-permute-start.7 = (bf16[6,128,128]{2,1,0:T(8,128)(2,1)S(1)}, bf16[6,128,128]{2,1,0:T(8,128)(2,1)S(1)}, u32[]{:S(2)}, u32[]{:S(2)}) collective-permute-start(bf16[6,128,128]{2,1,0:T(8,128)(2,1)S(1)} %get-tuple-element.106), channel_id=1, source_target_pairs={{0,64},{32,96},{64,0},{96,32},{1,65},{33,97},{65,1},{97,33},{2,66}... | collective-permute-start | bytes 589832 | tf_op jit(solution)/shard_map/ppermute | solution.py:388
  23.9 1.2 %weights_1.1 = (f32[33,128,128]{2,1,0:T(8,128)S(1)}, f32[32,128]{1,0:T(8,128)S(1)}) custom-call(s32[4,8,128]{2,1,0:T(8,128)S(1)} %get-tuple-element.92.ids_ref, s32[6,2,8]{2,1,0:T(2,128)S(1)} %bitcast.21, bf16[6,128,128]{2,1,0:T(8,128)(2,1)S(1)} %get-tuple-element.93.near_ref, bf16[6,128,128]{2,1,0:T(8,128)(2,1)S(1)} %collective-permute-done.4.far_ref), custom_call_target="tpu_custom_call" | custom-call | tf_op jit(solution)/shard_map/weights_1/pallas_call | solution.py:356
  28.7 1.1 %collective-permute-start.9 = (bf16[272,256]{1,0:T(8,128)(2,1)S(1)}, bf16[272,256]{1,0:T(8,128)(2,1)S(1)}, u32[]{:S(2)}, u32[]{:S(2)}) collective-permute-start(bf16[272,256]{1,0:T(8,128)(2,1)S(1)} %get-tuple-element.111), channel_id=1, source_target_pairs={{0,1},{1,2},{2,3},{3,4},{4,5},{5,6},{6,7},{7,8},{8,9},{9,10},{10,1... | collective-permute-start | bytes 417800 | tf_op jit(solution)/shard_map/ppermute | solution.py:383
  30.5 1.6 %collective-permute-start.10 = (bf16[6,128,128]{2,1,0:T(8,128)(2,1)S(1)}, bf16[6,128,128]{2,1,0:T(8,128)(2,1)S(1)}, u32[]{:S(2)}, u32[]{:S(2)}) collective-permute-start(bf16[6,128,128]{2,1,0:T(8,128)(2,1)S(1)} %get-tuple-element.118), channel_id=1, source_target_pairs={{0,64},{32,96},{64,0},{96,32},{1,65},{33,97},{65,1},{97,33},{2,66}... | collective-permute-start | bytes 589832 | tf_op jit(solution)/shard_map/ppermute | solution.py:388
  32.1 1.2 %weights_2.1 = (f32[33,128,128]{2,1,0:T(8,128)S(1)}, f32[32,128]{1,0:T(8,128)S(1)}) custom-call(s32[4,8,128]{2,1,0:T(8,128)S(1)} %get-tuple-element.92.ids_ref, s32[6,2,8]{2,1,0:T(2,128)S(1)} %bitcast.22, bf16[6,128,128]{2,1,0:T(8,128)(2,1)S(1)} %get-tuple-element.104.near_ref, bf16[6,128,128]{2,1,0:T(8,128)(2,1)S(1)} %collective-permute-done.7.far_ref), custom_call_target="tpu_custom_call" | custom-call | tf_op jit(solution)/shard_map/weights_2/pallas_call | solution.py:356
  33.3 3.8 %collective-permute-done.8.refs_0_.refs_2_ = bf16[272,256]{1,0:T(8,128)(2,1)S(1)} collective-permute-done((bf16[272,256]{1,0:T(8,128)(2,1)S(1)}, bf16[272,256]{1,0:T(8,128)(2,1)S(1)}, u32[]{:S(2)}, u32[]{:S(2)}) %collective-permute-start.8) | collective-permute-done | bytes 139296 | tf_op jit(solution)/shard_map/ppermute | solution.py:383
  40.5 2.2 %collective-permute-start.13 = (bf16[6,128,128]{2,1,0:T(8,128)(2,1)S(1)}, bf16[6,128,128]{2,1,0:T(8,128)(2,1)S(1)}, u32[]{:S(2)}, u32[]{:S(2)}) collective-permute-start(bf16[6,128,128]{2,1,0:T(8,128)(2,1)S(1)} %get-tuple-element.130), channel_id=1, source_target_pairs={{0,64},{32,96},{64,0},{96,32},{1,65},{33,97},{65,1},{97,33},{2,66}... | collective-permute-start | bytes 589832 | tf_op jit(solution)/shard_map/ppermute | solution.py:388
  42.8 1.2 %weights_3.1 = (f32[33,128,128]{2,1,0:T(8,128)S(1)}, f32[32,128]{1,0:T(8,128)S(1)}) custom-call(s32[4,8,128]{2,1,0:T(8,128)S(1)} %get-tuple-element.92.ids_ref, s32[6,2,8]{2,1,0:T(2,128)S(1)} %bitcast.23, bf16[6,128,128]{2,1,0:T(8,128)(2,1)S(1)} %get-tuple-element.116.near_ref, bf16[6,128,128]{2,1,0:T(8,128)(2,1)S(1)} %collective-permute-done.10.far_ref), custom_call_target="tpu_custom_call" | custom-call | tf_op jit(solution)/shard_map/weights_3/pallas_call | solution.py:356
  44.0 4.5 %collective-permute-done.11.refs_0_.refs_2_ = bf16[272,256]{1,0:T(8,128)(2,1)S(1)} collective-permute-done((bf16[272,256]{1,0:T(8,128)(2,1)S(1)}, bf16[272,256]{1,0:T(8,128)(2,1)S(1)}, u32[]{:S(2)}, u32[]{:S(2)}) %collective-permute-start.11) | collective-permute-done | bytes 139296 | tf_op jit(solution)/shard_map/ppermute | solution.py:383
  51.5 2.2 %collective-permute-start.16 = (bf16[6,128,128]{2,1,0:T(8,128)(2,1)S(1)}, bf16[6,128,128]{2,1,0:T(8,128)(2,1)S(1)}, u32[]{:S(2)}, u32[]{:S(2)}) collective-permute-start(bf16[6,128,128]{2,1,0:T(8,128)(2,1)S(1)} %get-tuple-element.142), channel_id=1, source_target_pairs={{0,64},{32,96},{64,0},{96,32},{1,65},{33,97},{65,1},{97,33},{2,66}... | collective-permute-start | bytes 589832 | tf_op jit(solution)/shard_map/ppermute | solution.py:388
  53.7 1.2 %weights_4.1 = (f32[33,128,128]{2,1,0:T(8,128)S(1)}, f32[32,128]{1,0:T(8,128)S(1)}) custom-call(s32[4,8,128]{2,1,0:T(8,128)S(1)} %get-tuple-element.92.ids_ref, s32[6,2,8]{2,1,0:T(2,128)S(1)} %bitcast.24, bf16[6,128,128]{2,1,0:T(8,128)(2,1)S(1)} %get-tuple-element.128.near_ref, bf16[6,128,128]{2,1,0:T(8,128)(2,1)S(1)} %collective-permute-done.13.far_ref), custom_call_target="tpu_custom_call" | custom-call | tf_op jit(solution)/shard_map/weights_4/pallas_call | solution.py:356
  54.9 3.7 %collective-permute-done.14.refs_0_.refs_2_ = bf16[272,256]{1,0:T(8,128)(2,1)S(1)} collective-permute-done((bf16[272,256]{1,0:T(8,128)(2,1)S(1)}, bf16[272,256]{1,0:T(8,128)(2,1)S(1)}, u32[]{:S(2)}, u32[]{:S(2)}) %collective-permute-start.14) | collective-permute-done | bytes 139296 | tf_op jit(solution)/shard_map/ppermute | solution.py:383
  61.7 1.1 %collective-permute-done.16.far_ref = bf16[6,128,128]{2,1,0:T(8,128)(2,1)S(1)} collective-permute-done((bf16[6,128,128]{2,1,0:T(8,128)(2,1)S(1)}, bf16[6,128,128]{2,1,0:T(8,128)(2,1)S(1)}, u32[]{:S(2)}, u32[]{:S(2)}) %collective-permute-start.16) | collective-permute-done | bytes 196640 | tf_op jit(solution)/shard_map/ppermute | solution.py:388
  62.8 1.2 %weights_5.1 = (f32[33,128,128]{2,1,0:T(8,128)S(1)}, f32[32,128]{1,0:T(8,128)S(1)}) custom-call(s32[4,8,128]{2,1,0:T(8,128)S(1)} %get-tuple-element.92.ids_ref, s32[6,2,8]{2,1,0:T(2,128)S(1)} %bitcast.25, bf16[6,128,128]{2,1,0:T(8,128)(2,1)S(1)} %get-tuple-element.140.near_ref, bf16[6,128,128]{2,1,0:T(8,128)(2,1)S(1)} %collective-permute-done.16.far_ref), custom_call_target="tpu_custom_call" | custom-call | tf_op jit(solution)/shard_map/weights_5/pallas_call | solution.py:356
  64.0 6.3 %collective-permute-done.17.refs_0_ = bf16[272,256]{1,0:T(8,128)(2,1)S(1)} collective-permute-done((bf16[272,256]{1,0:T(8,128)(2,1)S(1)}, bf16[272,256]{1,0:T(8,128)(2,1)S(1)}, u32[]{:S(2)}, u32[]{:S(2)}) %collective-permute-start.17) | collective-permute-done | bytes 139296 | tf_op jit(solution)/shard_map/ppermute | solution.py:383
  71.0 1.1 %collective-permute-done.18.refs_1_ = bf16[272,256]{1,0:T(8,128)(2,1)S(1)} collective-permute-done((bf16[272,256]{1,0:T(8,128)(2,1)S(1)}, bf16[272,256]{1,0:T(8,128)(2,1)S(1)}, u32[]{:S(2)}, u32[]{:S(2)}) %collective-permute-start.18) | collective-permute-done | bytes 139296 | tf_op jit(solution)/shard_map/ppermute | solution.py:383
  72.1 2.1 %final.1 = (f32[1024,256]{1,0:T(8,128)}, f32[8,128]{1,0:T(8,128)}, f32[512,256]{1,0:T(8,128)}, f32[4,128]{1,0:T(4,128)}) custom-call(bf16[1024,256]{1,0:T(8,128)(2,1)S(1)} %get-tuple-element.139.v_ref, f32[33,128,128]{2,1,0:T(8,128)S(1)} %get-tuple-element.143.w_ref, f32[32,128]{1,0:T(8,128)S(1)} %get-tuple-element.144.q_ref, ...), custom_call_target="tpu_custom_call" | custom-call | tf_op jit(solution)/shard_map/final/pallas_call | solution.py:331
  (55 shorter events, 19.8 us)
Async XLA Ops:
  2.5 5.6 %collective-permute-start.1 = (bf16[4,6,3,128,128]{4,3,2,1,0:T(8,128)(2,1)S(1)}, bf16[4,6,3,128,128]{4,3,2,1,0:T(8,128)(2,1)S(1)}, u32[]{:S(2)}, u32[]{:S(2)}) collective-permute-start(bf16[4,6,3,128,128]{4,3,2,1,0:T(8,128)(2,1)S(1)} %bitcast.17), channel_id=1, source_target_pairs={{0,32},{32,0},{64,96},{96,64},{1,33},{33,1},{65,97},{97,65},{2,34}... | collective-permute-start | bytes 7077896 | tf_op jit(solution)/shard_map/ppermute | solution.py:388
  2.6 10.6 %collective-permute-start.2 = (bf16[400,128]{1,0:T(8,128)(2,1)}, bf16[400,128]{1,0:T(8,128)(2,1)S(1)}, u32[]{:S(2)}, u32[]{:S(2)}) collective-permute-start(bf16[400,128]{1,0:T(8,128)(2,1)} %get-tuple-element.82), channel_id=1, source_target_pairs={{0,64},{32,96},{64,0},{96,32},{1,65},{33,97},{65,1},{97,33},{2,66}... | collective-permute-start | bytes 307208 | tf_op jit(solution)/shard_map/ppermute | solution.py:388
  6.6 6.6 %collective-permute-start.3 = (bf16[400,128]{1,0:T(8,128)(2,1)}, bf16[400,128]{1,0:T(8,128)(2,1)S(1)}, u32[]{:S(2)}, u32[]{:S(2)}) collective-permute-start(bf16[400,128]{1,0:T(8,128)(2,1)} %get-tuple-element.86), channel_id=1, source_target_pairs={{0,96},{32,64},{64,32},{96,0},{1,97},{33,65},{65,33},{97,1},{2,98}... | collective-permute-start | bytes 307208 | tf_op jit(solution)/shard_map/ppermute | solution.py:388
  6.7 5.6 %copy-start.3 = (s32[1,1,6,8,2]{3,4,2,1,0:T(2,128)S(1)}, s32[1,1,6,8,2]{3,4,2,1,0:T(2,128)}, u32[]{:S(2)}) copy-start(s32[1,1,6,8,2]{3,4,2,1,0:T(2,128)} %param.17) | copy-start | bytes 1156
  6.7 5.6 %copy-start.4 = (s32[8,128]{1,0:T(8,128)S(1)}, s32[8,128]{1,0:T(8,128)}, u32[]{:S(2)}) copy-start(s32[8,128]{1,0:T(8,128)} %get-tuple-element.80.own_ref) | copy-start | bytes 12292
  6.7 1.4 %collective-permute-start = (s32[8,128]{1,0:T(8,128)}, s32[8,128]{1,0:T(8,128)S(1)}, u32[]{:S(2)}, u32[]{:S(2)}) collective-permute-start(s32[8,128]{1,0:T(8,128)} %get-tuple-element.81), channel_id=1, source_target_pairs={{0,32},{32,0},{64,96},{96,64},{1,33},{33,1},{65,97},{97,65},{2,34}... | collective-permute-start | bytes 12296 | tf_op jit(solution)/shard_map/ppermute | solution.py:388
  8.9 5.2 %copy-start.1 = (f32[1024,256]{1,0:T(8,128)S(1)}, f32[1024,256]{1,0:T(8,128)}, u32[]{:S(2)}) copy-start(f32[1024,256]{1,0:T(8,128)} %refs_3_.1) | copy-start | bytes 3145732
  8.9 5.2 %copy-start.2 = (f32[512,256]{1,0:T(8,128)S(1)}, f32[512,256]{1,0:T(8,128)}, u32[]{:S(2)}) copy-start(f32[512,256]{1,0:T(8,128)} %refs_2_.1) | copy-start | bytes 1572868
  8.9 5.2 %copy-start.5 = (f32[512]{0:T(512)S(1)}, f32[512]{0:T(512)}, u32[]{:S(2)}) copy-start(f32[512]{0:T(512)} %param.12) | copy-start | bytes 6148
  8.9 15.0 %collective-permute-start.4 = (bf16[6,128,128]{2,1,0:T(8,128)(2,1)S(1)}, bf16[6,128,128]{2,1,0:T(8,128)(2,1)S(1)}, u32[]{:S(2)}, u32[]{:S(2)}) collective-permute-start(bf16[6,128,128]{2,1,0:T(8,128)(2,1)S(1)} %get-tuple-element.94), channel_id=1, source_target_pairs={{0,64},{32,96},{64,0},{96,32},{1,65},{33,97},{65,1},{97,33},{2,66}... | collective-permute-start | bytes 589832 | tf_op jit(solution)/shard_map/ppermute | solution.py:388
  14.9 10.9 %collective-permute-start.5 = (bf16[272,256]{1,0:T(8,128)(2,1)S(1)}, bf16[272,256]{1,0:T(8,128)(2,1)S(1)}, u32[]{:S(2)}, u32[]{:S(2)}) collective-permute-start(bf16[272,256]{1,0:T(8,128)(2,1)S(1)} %get-tuple-element.97), channel_id=1, source_target_pairs={{0,1},{1,2},{2,3},{3,4},{4,5},{5,6},{6,7},{7,8},{8,9},{9,10},{10,1... | collective-permute-start | bytes 417800 | tf_op jit(solution)/shard_map/ppermute | solution.py:383
  16.8 11.2 %collective-permute-start.6 = (bf16[272,256]{1,0:T(8,128)(2,1)S(1)}, bf16[272,256]{1,0:T(8,128)(2,1)S(1)}, u32[]{:S(2)}, u32[]{:S(2)}) collective-permute-start(bf16[272,256]{1,0:T(8,128)(2,1)S(1)} %get-tuple-element.99), channel_id=1, source_target_pairs={{0,1},{1,2},{2,3},{3,4},{4,5},{5,6},{6,7},{7,8},{8,9},{9,10},{10,1... | collective-permute-start | bytes 417800 | tf_op jit(solution)/shard_map/ppermute | solution.py:383
  21.8 10.3 %collective-permute-start.7 = (bf16[6,128,128]{2,1,0:T(8,128)(2,1)S(1)}, bf16[6,128,128]{2,1,0:T(8,128)(2,1)S(1)}, u32[]{:S(2)}, u32[]{:S(2)}) collective-permute-start(bf16[6,128,128]{2,1,0:T(8,128)(2,1)S(1)} %get-tuple-element.106), channel_id=1, source_target_pairs={{0,64},{32,96},{64,0},{96,32},{1,65},{33,97},{65,1},{97,33},{2,66}... | collective-permute-start | bytes 589832 | tf_op jit(solution)/shard_map/ppermute | solution.py:388
  26.5 10.6 %collective-permute-start.8 = (bf16[272,256]{1,0:T(8,128)(2,1)S(1)}, bf16[272,256]{1,0:T(8,128)(2,1)S(1)}, u32[]{:S(2)}, u32[]{:S(2)}) collective-permute-start(bf16[272,256]{1,0:T(8,128)(2,1)S(1)} %get-tuple-element.109), channel_id=1, source_target_pairs={{0,1},{1,2},{2,3},{3,4},{4,5},{5,6},{6,7},{7,8},{8,9},{9,10},{10,1... | collective-permute-start | bytes 417800 | tf_op jit(solution)/shard_map/ppermute | solution.py:383
  28.7 10.2 %collective-permute-start.9 = (bf16[272,256]{1,0:T(8,128)(2,1)S(1)}, bf16[272,256]{1,0:T(8,128)(2,1)S(1)}, u32[]{:S(2)}, u32[]{:S(2)}) collective-permute-start(bf16[272,256]{1,0:T(8,128)(2,1)S(1)} %get-tuple-element.111), channel_id=1, source_target_pairs={{0,1},{1,2},{2,3},{3,4},{4,5},{5,6},{6,7},{7,8},{8,9},{9,10},{10,1... | collective-permute-start | bytes 417800 | tf_op jit(solution)/shard_map/ppermute | solution.py:383
  30.5 12.2 %collective-permute-start.10 = (bf16[6,128,128]{2,1,0:T(8,128)(2,1)S(1)}, bf16[6,128,128]{2,1,0:T(8,128)(2,1)S(1)}, u32[]{:S(2)}, u32[]{:S(2)}) collective-permute-start(bf16[6,128,128]{2,1,0:T(8,128)(2,1)S(1)} %get-tuple-element.118), channel_id=1, source_target_pairs={{0,64},{32,96},{64,0},{96,32},{1,65},{33,97},{65,1},{97,33},{2,66}... | collective-permute-start | bytes 589832 | tf_op jit(solution)/shard_map/ppermute | solution.py:388
  37.9 10.6 %collective-permute-start.11 = (bf16[272,256]{1,0:T(8,128)(2,1)S(1)}, bf16[272,256]{1,0:T(8,128)(2,1)S(1)}, u32[]{:S(2)}, u32[]{:S(2)}) collective-permute-start(bf16[272,256]{1,0:T(8,128)(2,1)S(1)} %get-tuple-element.121), channel_id=1, source_target_pairs={{0,1},{1,2},{2,3},{3,4},{4,5},{5,6},{6,7},{7,8},{8,9},{9,10},{10,1... | collective-permute-start | bytes 417800 | tf_op jit(solution)/shard_map/ppermute | solution.py:383
  39.7 10.2 %collective-permute-start.12 = (bf16[272,256]{1,0:T(8,128)(2,1)S(1)}, bf16[272,256]{1,0:T(8,128)(2,1)S(1)}, u32[]{:S(2)}, u32[]{:S(2)}) collective-permute-start(bf16[272,256]{1,0:T(8,128)(2,1)S(1)} %get-tuple-element.123), channel_id=1, source_target_pairs={{0,1},{1,2},{2,3},{3,4},{4,5},{5,6},{6,7},{7,8},{8,9},{9,10},{10,1... | collective-permute-start | bytes 417800 | tf_op jit(solution)/shard_map/ppermute | solution.py:383
  40.5 13.2 %collective-permute-start.13 = (bf16[6,128,128]{2,1,0:T(8,128)(2,1)S(1)}, bf16[6,128,128]{2,1,0:T(8,128)(2,1)S(1)}, u32[]{:S(2)}, u32[]{:S(2)}) collective-permute-start(bf16[6,128,128]{2,1,0:T(8,128)(2,1)S(1)} %get-tuple-element.130), channel_id=1, source_target_pairs={{0,64},{32,96},{64,0},{96,32},{1,65},{33,97},{65,1},{97,33},{2,66}... | collective-permute-start | bytes 589832 | tf_op jit(solution)/shard_map/ppermute | solution.py:388
  49.3 9.3 %collective-permute-start.14 = (bf16[272,256]{1,0:T(8,128)(2,1)S(1)}, bf16[272,256]{1,0:T(8,128)(2,1)S(1)}, u32[]{:S(2)}, u32[]{:S(2)}) collective-permute-start(bf16[272,256]{1,0:T(8,128)(2,1)S(1)} %get-tuple-element.133), channel_id=1, source_target_pairs={{0,1},{1,2},{2,3},{3,4},{4,5},{5,6},{6,7},{7,8},{8,9},{9,10},{10,1... | collective-permute-start | bytes 417800 | tf_op jit(solution)/shard_map/ppermute | solution.py:383
  50.7 9.3 %collective-permute-start.15 = (bf16[272,256]{1,0:T(8,128)(2,1)S(1)}, bf16[272,256]{1,0:T(8,128)(2,1)S(1)}, u32[]{:S(2)}, u32[]{:S(2)}) collective-permute-start(bf16[272,256]{1,0:T(8,128)(2,1)S(1)} %get-tuple-element.135), channel_id=1, source_target_pairs={{0,1},{1,2},{2,3},{3,4},{4,5},{5,6},{6,7},{7,8},{8,9},{9,10},{10,1... | collective-permute-start | bytes 417800 | tf_op jit(solution)/shard_map/ppermute | solution.py:383
  51.5 11.3 %collective-permute-start.16 = (bf16[6,128,128]{2,1,0:T(8,128)(2,1)S(1)}, bf16[6,128,128]{2,1,0:T(8,128)(2,1)S(1)}, u32[]{:S(2)}, u32[]{:S(2)}) collective-permute-start(bf16[6,128,128]{2,1,0:T(8,128)(2,1)S(1)} %get-tuple-element.142), channel_id=1, source_target_pairs={{0,64},{32,96},{64,0},{96,32},{1,65},{33,97},{65,1},{97,33},{2,66}... | collective-permute-start | bytes 589832 | tf_op jit(solution)/shard_map/ppermute | solution.py:388
  59.4 10.8 %collective-permute-start.17 = (bf16[272,256]{1,0:T(8,128)(2,1)S(1)}, bf16[272,256]{1,0:T(8,128)(2,1)S(1)}, u32[]{:S(2)}, u32[]{:S(2)}) collective-permute-start(bf16[272,256]{1,0:T(8,128)(2,1)S(1)} %get-tuple-element.145), channel_id=1, source_target_pairs={{0,1},{1,2},{2,3},{3,4},{4,5},{5,6},{6,7},{7,8},{8,9},{9,10},{10,1... | collective-permute-start | bytes 417800 | tf_op jit(solution)/shard_map/ppermute | solution.py:383
  60.9 11.3 %collective-permute-start.18 = (bf16[272,256]{1,0:T(8,128)(2,1)S(1)}, bf16[272,256]{1,0:T(8,128)(2,1)S(1)}, u32[]{:S(2)}, u32[]{:S(2)}) collective-permute-start(bf16[272,256]{1,0:T(8,128)(2,1)S(1)} %get-tuple-element.146), channel_id=1, source_target_pairs={{0,1},{1,2},{2,3},{3,4},{4,5},{5,6},{6,7},{7,8},{8,9},{9,10},{10,1... | collective-permute-start | bytes 417800 | tf_op jit(solution)/shard_map/ppermute | solution.py:383
  (2 other events, 5.8 us)

commit v4 on v3

--- a/solution.py
+++ b/solution.py
@@ -170,8 +170,7 @@
         new_rows, new_state = adagrad(eye, v32_ref[rows, :], vs_ref[r : r + 1, :], dot(pt, c_bf, TN))
         v_new[rows, :] = new_rows
         vs_new[r : r + 1, :] = new_state
-        if r % 2:
-            store(v_new.at[pl.ds((r - 1) * TILE, 2 * TILE)], vout_ref.at[pl.ds((r - 1) * TILE, 2 * TILE)])
+        store(v_new.at[pl.ds(r * TILE, TILE)], vout_ref.at[pl.ds(r * TILE, TILE)])
     store(vs_new, vsout_ref)
     for copy in stores:
         copy.wait()
@@ -202,7 +201,7 @@
     )
 
 
-def first_weights_kernel(own_ref, one_ref, part_ref, two_ref, three_ref, out_ref, ids_ref, scalars, sem):
+def first_weights_kernel(own_ref, one_ref, part_ref, two_ref, three_ref, out_ref, ids_ref, scalars, turned, sem):
     msgs = two_ref, three_ref
     cap = (two_ref.shape[0] - TAIL) // TILE
     for at, msg in enumerate(msgs):
@@ -211,15 +210,12 @@
     copy.start()
     ids_ref[0] = own_ref[...]
     ids_ref[1] = one_ref[...]
+    places = [(at, slot) for at in range(2) for slot in range(cap)]
+    for k, (at, slot) in enumerate(places):
+        turned[k] = 0.5 * msgs[at][slot * TILE : (slot + 1) * TILE, :].astype(F32).T
     copy.wait()
-    add_tiles(
-        out_ref,
-        [
-            (scalars[at, slot, 0], msg[slot * TILE : (slot + 1) * TILE, :])
-            for at, msg in enumerate(msgs)
-            for slot in range(cap)
-        ],
-    )
+    for k, (at, slot) in enumerate(places):
+        out_ref[scalars[at, slot, 0]] += turned[k]
 
 
 def weights_kernel(stop, ids_ref, neg_ref, near_ref, far_ref, out_ref, q_ref):
@@ -344,7 +340,7 @@
             pltpu.VMEM((tiles, TILE), F32),
             pltpu.VMEM(v.shape, F32),
             pltpu.VMEM(vs.shape, F32),
-            pltpu.SemaphoreType.DMA((n + 2 + v.shape[0] // (2 * TILE),)),
+            pltpu.SemaphoreType.DMA((n + 2 + v.shape[0] // TILE,)),
         ],
         compiler_params=params(),
         cost_estimate=FREE,
@@ -442,7 +438,11 @@
         out_shape=[shape(PAIRS + 1, TILE, TILE, dtype=F32), shape(groups, ID_ROWS, TILE, dtype=jnp.int32)],
         in_specs=[VM] * 5,
         out_specs=[VM] * 2,
-        scratch_shapes=[pltpu.SMEM((2, ID_ROWS, TILE), jnp.int32), pltpu.SemaphoreType.DMA],
+        scratch_shapes=[
+            pltpu.SMEM((2, ID_ROWS, TILE), jnp.int32),
+            pltpu.VMEM((2 * cap, TILE, TILE), F32),
+            pltpu.SemaphoreType.DMA,
+        ],
         input_output_aliases={2: 0},
         compiler_params=params(),
         cost_estimate=FREE,

time: 74.6 us -> 74.5 us (level)
  transfers between devices with their start and end apart: 19 -> 19, of which waited for: 12 -> 12; matrix products, arithmetic and copies ran while one was open for 0% -> 0% of each run, Pallas kernels for 31% -> 30%
where the time goes in v4:
time: 74.5 us; the launch traced here: 74.4 us
  Pallas kernels  26.6 us (36%)
  waiting for transfers between devices  25.7 us (34%)
  starting transfers between devices  20.9 us (28%)
  between operations  1.12 us (2%)
    ppermute x10, waiting for transfers between devices, shifted(): lax.ppermute(value, axis, [(i, (i + by) % peers) for i in range(peers)])  23.3 us
    ppermute x9, starting transfers between devices, swapped(): return lax.ppermute(value, 'group', [(i, i ^ by) for i in range(peers)])  15.8 us
    pallas_call x11, Pallas kernels, context_call(): pl.pallas_call(functools.partial(context_kernel, first, last, chunk * hei...  8.58 us
    pallas_call x5, Pallas kernels, weights_call(): pl.pallas_call(functools.partial(weights_kernel, stop), out_shape=[shape(...  5.83 us
    ppermute x10, starting transfers between devices, shifted(): lax.ppermute(value, axis, [(i, (i + by) % peers) for i in range(peers)])  5.14 us
    pallas_call x5, Pallas kernels, vertex_call(): pl.pallas_call(functools.partial(vertex_kernel, len(pts), len(cs) == 1),...  3.5 us
    pallas_call x2, Pallas kernels, relay_call(): pl.pallas_call(functools.partial(relay_kernel, wanted), out_shape=[shape(...  3.02 us
    ppermute x9, waiting for transfers between devices, swapped(): return lax.ppermute(value, 'group', [(i, i ^ by) for i in range(peers)])  2.37 us
  transfers between devices with their start and end apart: 19, of which 12 were waited for; matrix products, arithmetic and copies ran while one was open for 0% of the time, Pallas kernels for 30%

profile of v4, /device:TPU:0, one launch (start us, length us, event | category | flops | bytes accessed | tf_op | source)
XLA Modules:
  0.0 74.4 jit_solution(18127643789327113095)
XLA Ops:
  0.6 1.8 %pack.1 = (s32[8,128]{1,0:T(8,128)}, s32[8,128]{1,0:T(8,128)}, bf16[400,128]{1,0:T(8,128)(2,1)}, bf16[400,128]{1,0:T(8,128)(2,1)}) custom-call(s32[1]{0:T(128)} %bitcast.me_ref, bf16[4,6,3,128,128]{4,3,2,1,0:T(8,128)(2,1)} %bitcast.16, s32[3,4,6]{2,1,0:T(4,128)} %bitcast.29, s32[3,4,6]{2,1,0:T(4,128)} %bitcast.30, s32[4,6]{1,0:T(4,128)} %bitcast.31), custom_call_target="tpu_custom_call" | custom-call | tf_op jit(solution)/shard_map/pack/pallas_call | solution.py:400
  2.6 4.0 %collective-permute-start.2 = (bf16[400,128]{1,0:T(8,128)(2,1)}, bf16[400,128]{1,0:T(8,128)(2,1)S(1)}, u32[]{:S(2)}, u32[]{:S(2)}) collective-permute-start(bf16[400,128]{1,0:T(8,128)(2,1)} %get-tuple-element.82), channel_id=1, source_target_pairs={{0,64},{32,96},{64,0},{96,32},{1,65},{33,97},{65,1},{97,33},{2,66}... | collective-permute-start | bytes 307208 | tf_op jit(solution)/shard_map/ppermute | solution.py:384
  6.8 1.2 %collective-permute-done.after_ref.one_ref = s32[8,128]{1,0:T(8,128)S(1)} collective-permute-done((s32[8,128]{1,0:T(8,128)}, s32[8,128]{1,0:T(8,128)S(1)}, u32[]{:S(2)}, u32[]{:S(2)}) %collective-permute-start) | collective-permute-done | bytes 4128 | tf_op jit(solution)/shard_map/ppermute | solution.py:384
  8.9 3.3 %collective-permute-start.4 = (bf16[6,128,128]{2,1,0:T(8,128)(2,1)S(1)}, bf16[6,128,128]{2,1,0:T(8,128)(2,1)S(1)}, u32[]{:S(2)}, u32[]{:S(2)}) collective-permute-start(bf16[6,128,128]{2,1,0:T(8,128)(2,1)S(1)} %get-tuple-element.94), channel_id=1, source_target_pairs={{0,64},{32,96},{64,0},{96,32},{1,65},{33,97},{65,1},{97,33},{2,66}... | collective-permute-start | bytes 589832 | tf_op jit(solution)/shard_map/ppermute | solution.py:384
  14.8 1.1 %collective-permute-start.5 = (bf16[272,256]{1,0:T(8,128)(2,1)S(1)}, bf16[272,256]{1,0:T(8,128)(2,1)S(1)}, u32[]{:S(2)}, u32[]{:S(2)}) collective-permute-start(bf16[272,256]{1,0:T(8,128)(2,1)S(1)} %get-tuple-element.97), channel_id=1, source_target_pairs={{0,1},{1,2},{2,3},{3,4},{4,5},{5,6},{6,7},{7,8},{8,9},{9,10},{10,1... | collective-permute-start | bytes 417800 | tf_op jit(solution)/shard_map/ppermute | solution.py:379
  16.7 2.1 %collective-permute-start.6 = (bf16[272,256]{1,0:T(8,128)(2,1)S(1)}, bf16[272,256]{1,0:T(8,128)(2,1)S(1)}, u32[]{:S(2)}, u32[]{:S(2)}) collective-permute-start(bf16[272,256]{1,0:T(8,128)(2,1)S(1)} %get-tuple-element.99), channel_id=1, source_target_pairs={{0,1},{1,2},{2,3},{3,4},{4,5},{5,6},{6,7},{7,8},{8,9},{9,10},{10,1... | collective-permute-start | bytes 417800 | tf_op jit(solution)/shard_map/ppermute | solution.py:379
  19.5 2.2 %relay_2.1 = (bf16[6,128,128]{2,1,0:T(8,128)(2,1)S(1)}, bf16[6,128,128]{2,1,0:T(8,128)(2,1)S(1)}, bf16[6,128,128]{2,1,0:T(8,128)(2,1)S(1)}, bf16[6,128,128]{2,1,...) custom-call(s32[1]{0:T(128)} %bitcast.me_ref, ...), custom_call_target="tpu_custom_call" | custom-call | tf_op jit(solution)/shard_map/relay_2/pallas_call | solution.py:365
  21.7 2.1 %collective-permute-start.7 = (bf16[6,128,128]{2,1,0:T(8,128)(2,1)S(1)}, bf16[6,128,128]{2,1,0:T(8,128)(2,1)S(1)}, u32[]{:S(2)}, u32[]{:S(2)}) collective-permute-start(bf16[6,128,128]{2,1,0:T(8,128)(2,1)S(1)} %get-tuple-element.106), channel_id=1, source_target_pairs={{0,64},{32,96},{64,0},{96,32},{1,65},{33,97},{65,1},{97,33},{2,66}... | collective-permute-start | bytes 589832 | tf_op jit(solution)/shard_map/ppermute | solution.py:384
  23.8 1.2 %weights_1.1 = (f32[33,128,128]{2,1,0:T(8,128)S(1)}, f32[32,128]{1,0:T(8,128)S(1)}) custom-call(s32[4,8,128]{2,1,0:T(8,128)S(1)} %get-tuple-element.92.ids_ref, s32[6,2,8]{2,1,0:T(2,128)S(1)} %bitcast.21, bf16[6,128,128]{2,1,0:T(8,128)(2,1)S(1)} %get-tuple-element.93.near_ref, bf16[6,128,128]{2,1,0:T(8,128)(2,1)S(1)} %collective-permute-done.4.far_ref), custom_call_target="tpu_custom_call" | custom-call | tf_op jit(solution)/shard_map/weights_1/pallas_call | solution.py:352
  28.7 1.1 %collective-permute-start.9 = (bf16[272,256]{1,0:T(8,128)(2,1)S(1)}, bf16[272,256]{1,0:T(8,128)(2,1)S(1)}, u32[]{:S(2)}, u32[]{:S(2)}) collective-permute-start(bf16[272,256]{1,0:T(8,128)(2,1)S(1)} %get-tuple-element.111), channel_id=1, source_target_pairs={{0,1},{1,2},{2,3},{3,4},{4,5},{5,6},{6,7},{7,8},{8,9},{9,10},{10,1... | collective-permute-start | bytes 417800 | tf_op jit(solution)/shard_map/ppermute | solution.py:379
  30.5 1.6 %collective-permute-start.10 = (bf16[6,128,128]{2,1,0:T(8,128)(2,1)S(1)}, bf16[6,128,128]{2,1,0:T(8,128)(2,1)S(1)}, u32[]{:S(2)}, u32[]{:S(2)}) collective-permute-start(bf16[6,128,128]{2,1,0:T(8,128)(2,1)S(1)} %get-tuple-element.118), channel_id=1, source_target_pairs={{0,64},{32,96},{64,0},{96,32},{1,65},{33,97},{65,1},{97,33},{2,66}... | collective-permute-start | bytes 589832 | tf_op jit(solution)/shard_map/ppermute | solution.py:384
  32.1 1.2 %weights_2.1 = (f32[33,128,128]{2,1,0:T(8,128)S(1)}, f32[32,128]{1,0:T(8,128)S(1)}) custom-call(s32[4,8,128]{2,1,0:T(8,128)S(1)} %get-tuple-element.92.ids_ref, s32[6,2,8]{2,1,0:T(2,128)S(1)} %bitcast.22, bf16[6,128,128]{2,1,0:T(8,128)(2,1)S(1)} %get-tuple-element.104.near_ref, bf16[6,128,128]{2,1,0:T(8,128)(2,1)S(1)} %collective-permute-done.7.far_ref), custom_call_target="tpu_custom_call" | custom-call | tf_op jit(solution)/shard_map/weights_2/pallas_call | solution.py:352
  33.2 3.8 %collective-permute-done.8.refs_0_.refs_2_ = bf16[272,256]{1,0:T(8,128)(2,1)S(1)} collective-permute-done((bf16[272,256]{1,0:T(8,128)(2,1)S(1)}, bf16[272,256]{1,0:T(8,128)(2,1)S(1)}, u32[]{:S(2)}, u32[]{:S(2)}) %collective-permute-start.8) | collective-permute-done | bytes 139296 | tf_op jit(solution)/shard_map/ppermute | solution.py:379
  40.5 2.2 %collective-permute-start.13 = (bf16[6,128,128]{2,1,0:T(8,128)(2,1)S(1)}, bf16[6,128,128]{2,1,0:T(8,128)(2,1)S(1)}, u32[]{:S(2)}, u32[]{:S(2)}) collective-permute-start(bf16[6,128,128]{2,1,0:T(8,128)(2,1)S(1)} %get-tuple-element.130), channel_id=1, source_target_pairs={{0,64},{32,96},{64,0},{96,32},{1,65},{33,97},{65,1},{97,33},{2,66}... | collective-permute-start | bytes 589832 | tf_op jit(solution)/shard_map/ppermute | solution.py:384
  42.7 1.2 %weights_3.1 = (f32[33,128,128]{2,1,0:T(8,128)S(1)}, f32[32,128]{1,0:T(8,128)S(1)}) custom-call(s32[4,8,128]{2,1,0:T(8,128)S(1)} %get-tuple-element.92.ids_ref, s32[6,2,8]{2,1,0:T(2,128)S(1)} %bitcast.23, bf16[6,128,128]{2,1,0:T(8,128)(2,1)S(1)} %get-tuple-element.116.near_ref, bf16[6,128,128]{2,1,0:T(8,128)(2,1)S(1)} %collective-permute-done.10.far_ref), custom_call_target="tpu_custom_call" | custom-call | tf_op jit(solution)/shard_map/weights_3/pallas_call | solution.py:352
  43.9 4.5 %collective-permute-done.11.refs_0_.refs_2_ = bf16[272,256]{1,0:T(8,128)(2,1)S(1)} collective-permute-done((bf16[272,256]{1,0:T(8,128)(2,1)S(1)}, bf16[272,256]{1,0:T(8,128)(2,1)S(1)}, u32[]{:S(2)}, u32[]{:S(2)}) %collective-permute-start.11) | collective-permute-done | bytes 139296 | tf_op jit(solution)/shard_map/ppermute | solution.py:379
  51.4 2.2 %collective-permute-start.16 = (bf16[6,128,128]{2,1,0:T(8,128)(2,1)S(1)}, bf16[6,128,128]{2,1,0:T(8,128)(2,1)S(1)}, u32[]{:S(2)}, u32[]{:S(2)}) collective-permute-start(bf16[6,128,128]{2,1,0:T(8,128)(2,1)S(1)} %get-tuple-element.142), channel_id=1, source_target_pairs={{0,64},{32,96},{64,0},{96,32},{1,65},{33,97},{65,1},{97,33},{2,66}... | collective-permute-start | bytes 589832 | tf_op jit(solution)/shard_map/ppermute | solution.py:384
  53.6 1.2 %weights_4.1 = (f32[33,128,128]{2,1,0:T(8,128)S(1)}, f32[32,128]{1,0:T(8,128)S(1)}) custom-call(s32[4,8,128]{2,1,0:T(8,128)S(1)} %get-tuple-element.92.ids_ref, s32[6,2,8]{2,1,0:T(2,128)S(1)} %bitcast.24, bf16[6,128,128]{2,1,0:T(8,128)(2,1)S(1)} %get-tuple-element.128.near_ref, bf16[6,128,128]{2,1,0:T(8,128)(2,1)S(1)} %collective-permute-done.13.far_ref), custom_call_target="tpu_custom_call" | custom-call | tf_op jit(solution)/shard_map/weights_4/pallas_call | solution.py:352
  54.8 3.7 %collective-permute-done.14.refs_0_.refs_2_ = bf16[272,256]{1,0:T(8,128)(2,1)S(1)} collective-permute-done((bf16[272,256]{1,0:T(8,128)(2,1)S(1)}, bf16[272,256]{1,0:T(8,128)(2,1)S(1)}, u32[]{:S(2)}, u32[]{:S(2)}) %collective-permute-start.14) | collective-permute-done | bytes 139296 | tf_op jit(solution)/shard_map/ppermute | solution.py:379
  61.6 1.1 %collective-permute-done.16.far_ref = bf16[6,128,128]{2,1,0:T(8,128)(2,1)S(1)} collective-permute-done((bf16[6,128,128]{2,1,0:T(8,128)(2,1)S(1)}, bf16[6,128,128]{2,1,0:T(8,128)(2,1)S(1)}, u32[]{:S(2)}, u32[]{:S(2)}) %collective-permute-start.16) | collective-permute-done | bytes 196640 | tf_op jit(solution)/shard_map/ppermute | solution.py:384
  62.7 1.2 %weights_5.1 = (f32[33,128,128]{2,1,0:T(8,128)S(1)}, f32[32,128]{1,0:T(8,128)S(1)}) custom-call(s32[4,8,128]{2,1,0:T(8,128)S(1)} %get-tuple-element.92.ids_ref, s32[6,2,8]{2,1,0:T(2,128)S(1)} %bitcast.25, bf16[6,128,128]{2,1,0:T(8,128)(2,1)S(1)} %get-tuple-element.140.near_ref, bf16[6,128,128]{2,1,0:T(8,128)(2,1)S(1)} %collective-permute-done.16.far_ref), custom_call_target="tpu_custom_call" | custom-call | tf_op jit(solution)/shard_map/weights_5/pallas_call | solution.py:352
  63.9 6.3 %collective-permute-done.17.refs_0_ = bf16[272,256]{1,0:T(8,128)(2,1)S(1)} collective-permute-done((bf16[272,256]{1,0:T(8,128)(2,1)S(1)}, bf16[272,256]{1,0:T(8,128)(2,1)S(1)}, u32[]{:S(2)}, u32[]{:S(2)}) %collective-permute-start.17) | collective-permute-done | bytes 139296 | tf_op jit(solution)/shard_map/ppermute | solution.py:379
  70.9 1.1 %collective-permute-done.18.refs_1_ = bf16[272,256]{1,0:T(8,128)(2,1)S(1)} collective-permute-done((bf16[272,256]{1,0:T(8,128)(2,1)S(1)}, bf16[272,256]{1,0:T(8,128)(2,1)S(1)}, u32[]{:S(2)}, u32[]{:S(2)}) %collective-permute-start.18) | collective-permute-done | bytes 139296 | tf_op jit(solution)/shard_map/ppermute | solution.py:379
  72.1 2.1 %final.1 = (f32[1024,256]{1,0:T(8,128)}, f32[8,128]{1,0:T(8,128)}, f32[512,256]{1,0:T(8,128)}, f32[4,128]{1,0:T(4,128)}) custom-call(bf16[1024,256]{1,0:T(8,128)(2,1)S(1)} %get-tuple-element.139.v_ref, f32[33,128,128]{2,1,0:T(8,128)S(1)} %get-tuple-element.143.w_ref, f32[32,128]{1,0:T(8,128)S(1)} %get-tuple-element.144.q_ref, ...), custom_call_target="tpu_custom_call" | custom-call | tf_op jit(solution)/shard_map/final/pallas_call | solution.py:327
  (55 shorter events, 19.7 us)
Async XLA Ops:
  2.5 5.6 %collective-permute-start.1 = (bf16[4,6,3,128,128]{4,3,2,1,0:T(8,128)(2,1)S(1)}, bf16[4,6,3,128,128]{4,3,2,1,0:T(8,128)(2,1)S(1)}, u32[]{:S(2)}, u32[]{:S(2)}) collective-permute-start(bf16[4,6,3,128,128]{4,3,2,1,0:T(8,128)(2,1)S(1)} %bitcast.17), channel_id=1, source_target_pairs={{0,32},{32,0},{64,96},{96,64},{1,33},{33,1},{65,97},{97,65},{2,34}... | collective-permute-start | bytes 7077896 | tf_op jit(solution)/shard_map/ppermute | solution.py:384
  2.6 10.6 %collective-permute-start.2 = (bf16[400,128]{1,0:T(8,128)(2,1)}, bf16[400,128]{1,0:T(8,128)(2,1)S(1)}, u32[]{:S(2)}, u32[]{:S(2)}) collective-permute-start(bf16[400,128]{1,0:T(8,128)(2,1)} %get-tuple-element.82), channel_id=1, source_target_pairs={{0,64},{32,96},{64,0},{96,32},{1,65},{33,97},{65,1},{97,33},{2,66}... | collective-permute-start | bytes 307208 | tf_op jit(solution)/shard_map/ppermute | solution.py:384
  6.6 6.6 %collective-permute-start.3 = (bf16[400,128]{1,0:T(8,128)(2,1)}, bf16[400,128]{1,0:T(8,128)(2,1)S(1)}, u32[]{:S(2)}, u32[]{:S(2)}) collective-permute-start(bf16[400,128]{1,0:T(8,128)(2,1)} %get-tuple-element.86), channel_id=1, source_target_pairs={{0,96},{32,64},{64,32},{96,0},{1,97},{33,65},{65,33},{97,1},{2,98}... | collective-permute-start | bytes 307208 | tf_op jit(solution)/shard_map/ppermute | solution.py:384
  6.7 5.6 %copy-start.3 = (s32[1,1,6,8,2]{3,4,2,1,0:T(2,128)S(1)}, s32[1,1,6,8,2]{3,4,2,1,0:T(2,128)}, u32[]{:S(2)}) copy-start(s32[1,1,6,8,2]{3,4,2,1,0:T(2,128)} %param.17) | copy-start | bytes 1156
  6.7 5.6 %copy-start.4 = (s32[8,128]{1,0:T(8,128)S(1)}, s32[8,128]{1,0:T(8,128)}, u32[]{:S(2)}) copy-start(s32[8,128]{1,0:T(8,128)} %get-tuple-element.80.own_ref) | copy-start | bytes 12292
  6.7 1.4 %collective-permute-start = (s32[8,128]{1,0:T(8,128)}, s32[8,128]{1,0:T(8,128)S(1)}, u32[]{:S(2)}, u32[]{:S(2)}) collective-permute-start(s32[8,128]{1,0:T(8,128)} %get-tuple-element.81), channel_id=1, source_target_pairs={{0,32},{32,0},{64,96},{96,64},{1,33},{33,1},{65,97},{97,65},{2,34}... | collective-permute-start | bytes 12296 | tf_op jit(solution)/shard_map/ppermute | solution.py:384
  8.9 5.1 %copy-start.1 = (f32[1024,256]{1,0:T(8,128)S(1)}, f32[1024,256]{1,0:T(8,128)}, u32[]{:S(2)}) copy-start(f32[1024,256]{1,0:T(8,128)} %refs_3_.1) | copy-start | bytes 3145732
  8.9 5.1 %copy-start.2 = (f32[512,256]{1,0:T(8,128)S(1)}, f32[512,256]{1,0:T(8,128)}, u32[]{:S(2)}) copy-start(f32[512,256]{1,0:T(8,128)} %refs_2_.1) | copy-start | bytes 1572868
  8.9 5.1 %copy-start.5 = (f32[512]{0:T(512)S(1)}, f32[512]{0:T(512)}, u32[]{:S(2)}) copy-start(f32[512]{0:T(512)} %param.12) | copy-start | bytes 6148
  8.9 14.9 %collective-permute-start.4 = (bf16[6,128,128]{2,1,0:T(8,128)(2,1)S(1)}, bf16[6,128,128]{2,1,0:T(8,128)(2,1)S(1)}, u32[]{:S(2)}, u32[]{:S(2)}) collective-permute-start(bf16[6,128,128]{2,1,0:T(8,128)(2,1)S(1)} %get-tuple-element.94), channel_id=1, source_target_pairs={{0,64},{32,96},{64,0},{96,32},{1,65},{33,97},{65,1},{97,33},{2,66}... | collective-permute-start | bytes 589832 | tf_op jit(solution)/shard_map/ppermute | solution.py:384
  14.8 10.9 %collective-permute-start.5 = (bf16[272,256]{1,0:T(8,128)(2,1)S(1)}, bf16[272,256]{1,0:T(8,128)(2,1)S(1)}, u32[]{:S(2)}, u32[]{:S(2)}) collective-permute-start(bf16[272,256]{1,0:T(8,128)(2,1)S(1)} %get-tuple-element.97), channel_id=1, source_target_pairs={{0,1},{1,2},{2,3},{3,4},{4,5},{5,6},{6,7},{7,8},{8,9},{9,10},{10,1... | collective-permute-start | bytes 417800 | tf_op jit(solution)/shard_map/ppermute | solution.py:379
  16.7 11.2 %collective-permute-start.6 = (bf16[272,256]{1,0:T(8,128)(2,1)S(1)}, bf16[272,256]{1,0:T(8,128)(2,1)S(1)}, u32[]{:S(2)}, u32[]{:S(2)}) collective-permute-start(bf16[272,256]{1,0:T(8,128)(2,1)S(1)} %get-tuple-element.99), channel_id=1, source_target_pairs={{0,1},{1,2},{2,3},{3,4},{4,5},{5,6},{6,7},{7,8},{8,9},{9,10},{10,1... | collective-permute-start | bytes 417800 | tf_op jit(solution)/shard_map/ppermute | solution.py:379
  21.7 10.3 %collective-permute-start.7 = (bf16[6,128,128]{2,1,0:T(8,128)(2,1)S(1)}, bf16[6,128,128]{2,1,0:T(8,128)(2,1)S(1)}, u32[]{:S(2)}, u32[]{:S(2)}) collective-permute-start(bf16[6,128,128]{2,1,0:T(8,128)(2,1)S(1)} %get-tuple-element.106), channel_id=1, source_target_pairs={{0,64},{32,96},{64,0},{96,32},{1,65},{33,97},{65,1},{97,33},{2,66}... | collective-permute-start | bytes 589832 | tf_op jit(solution)/shard_map/ppermute | solution.py:384
  26.5 10.6 %collective-permute-start.8 = (bf16[272,256]{1,0:T(8,128)(2,1)S(1)}, bf16[272,256]{1,0:T(8,128)(2,1)S(1)}, u32[]{:S(2)}, u32[]{:S(2)}) collective-permute-start(bf16[272,256]{1,0:T(8,128)(2,1)S(1)} %get-tuple-element.109), channel_id=1, source_target_pairs={{0,1},{1,2},{2,3},{3,4},{4,5},{5,6},{6,7},{7,8},{8,9},{9,10},{10,1... | collective-permute-start | bytes 417800 | tf_op jit(solution)/shard_map/ppermute | solution.py:379
  28.7 10.2 %collective-permute-start.9 = (bf16[272,256]{1,0:T(8,128)(2,1)S(1)}, bf16[272,256]{1,0:T(8,128)(2,1)S(1)}, u32[]{:S(2)}, u32[]{:S(2)}) collective-permute-start(bf16[272,256]{1,0:T(8,128)(2,1)S(1)} %get-tuple-element.111), channel_id=1, source_target_pairs={{0,1},{1,2},{2,3},{3,4},{4,5},{5,6},{6,7},{7,8},{8,9},{9,10},{10,1... | collective-permute-start | bytes 417800 | tf_op jit(solution)/shard_map/ppermute | solution.py:379
  30.5 12.2 %collective-permute-start.10 = (bf16[6,128,128]{2,1,0:T(8,128)(2,1)S(1)}, bf16[6,128,128]{2,1,0:T(8,128)(2,1)S(1)}, u32[]{:S(2)}, u32[]{:S(2)}) collective-permute-start(bf16[6,128,128]{2,1,0:T(8,128)(2,1)S(1)} %get-tuple-element.118), channel_id=1, source_target_pairs={{0,64},{32,96},{64,0},{96,32},{1,65},{33,97},{65,1},{97,33},{2,66}... | collective-permute-start | bytes 589832 | tf_op jit(solution)/shard_map/ppermute | solution.py:384
  37.9 10.5 %collective-permute-start.11 = (bf16[272,256]{1,0:T(8,128)(2,1)S(1)}, bf16[272,256]{1,0:T(8,128)(2,1)S(1)}, u32[]{:S(2)}, u32[]{:S(2)}) collective-permute-start(bf16[272,256]{1,0:T(8,128)(2,1)S(1)} %get-tuple-element.121), channel_id=1, source_target_pairs={{0,1},{1,2},{2,3},{3,4},{4,5},{5,6},{6,7},{7,8},{8,9},{9,10},{10,1... | collective-permute-start | bytes 417800 | tf_op jit(solution)/shard_map/ppermute | solution.py:379
  39.7 10.2 %collective-permute-start.12 = (bf16[272,256]{1,0:T(8,128)(2,1)S(1)}, bf16[272,256]{1,0:T(8,128)(2,1)S(1)}, u32[]{:S(2)}, u32[]{:S(2)}) collective-permute-start(bf16[272,256]{1,0:T(8,128)(2,1)S(1)} %get-tuple-element.123), channel_id=1, source_target_pairs={{0,1},{1,2},{2,3},{3,4},{4,5},{5,6},{6,7},{7,8},{8,9},{9,10},{10,1... | collective-permute-start | bytes 417800 | tf_op jit(solution)/shard_map/ppermute | solution.py:379
  40.5 13.2 %collective-permute-start.13 = (bf16[6,128,128]{2,1,0:T(8,128)(2,1)S(1)}, bf16[6,128,128]{2,1,0:T(8,128)(2,1)S(1)}, u32[]{:S(2)}, u32[]{:S(2)}) collective-permute-start(bf16[6,128,128]{2,1,0:T(8,128)(2,1)S(1)} %get-tuple-element.130), channel_id=1, source_target_pairs={{0,64},{32,96},{64,0},{96,32},{1,65},{33,97},{65,1},{97,33},{2,66}... | collective-permute-start | bytes 589832 | tf_op jit(solution)/shard_map/ppermute | solution.py:384
  49.2 9.3 %collective-permute-start.14 = (bf16[272,256]{1,0:T(8,128)(2,1)S(1)}, bf16[272,256]{1,0:T(8,128)(2,1)S(1)}, u32[]{:S(2)}, u32[]{:S(2)}) collective-permute-start(bf16[272,256]{1,0:T(8,128)(2,1)S(1)} %get-tuple-element.133), channel_id=1, source_target_pairs={{0,1},{1,2},{2,3},{3,4},{4,5},{5,6},{6,7},{7,8},{8,9},{9,10},{10,1... | collective-permute-start | bytes 417800 | tf_op jit(solution)/shard_map/ppermute | solution.py:379
  50.7 9.3 %collective-permute-start.15 = (bf16[272,256]{1,0:T(8,128)(2,1)S(1)}, bf16[272,256]{1,0:T(8,128)(2,1)S(1)}, u32[]{:S(2)}, u32[]{:S(2)}) collective-permute-start(bf16[272,256]{1,0:T(8,128)(2,1)S(1)} %get-tuple-element.135), channel_id=1, source_target_pairs={{0,1},{1,2},{2,3},{3,4},{4,5},{5,6},{6,7},{7,8},{8,9},{9,10},{10,1... | collective-permute-start | bytes 417800 | tf_op jit(solution)/shard_map/ppermute | solution.py:379
  51.4 11.3 %collective-permute-start.16 = (bf16[6,128,128]{2,1,0:T(8,128)(2,1)S(1)}, bf16[6,128,128]{2,1,0:T(8,128)(2,1)S(1)}, u32[]{:S(2)}, u32[]{:S(2)}) collective-permute-start(bf16[6,128,128]{2,1,0:T(8,128)(2,1)S(1)} %get-tuple-element.142), channel_id=1, source_target_pairs={{0,64},{32,96},{64,0},{96,32},{1,65},{33,97},{65,1},{97,33},{2,66}... | collective-permute-start | bytes 589832 | tf_op jit(solution)/shard_map/ppermute | solution.py:384
  59.3 10.8 %collective-permute-start.17 = (bf16[272,256]{1,0:T(8,128)(2,1)S(1)}, bf16[272,256]{1,0:T(8,128)(2,1)S(1)}, u32[]{:S(2)}, u32[]{:S(2)}) collective-permute-start(bf16[272,256]{1,0:T(8,128)(2,1)S(1)} %get-tuple-element.145), channel_id=1, source_target_pairs={{0,1},{1,2},{2,3},{3,4},{4,5},{5,6},{6,7},{7,8},{8,9},{9,10},{10,1... | collective-permute-start | bytes 417800 | tf_op jit(solution)/shard_map/ppermute | solution.py:379
  60.8 11.3 %collective-permute-start.18 = (bf16[272,256]{1,0:T(8,128)(2,1)S(1)}, bf16[272,256]{1,0:T(8,128)(2,1)S(1)}, u32[]{:S(2)}, u32[]{:S(2)}) collective-permute-start(bf16[272,256]{1,0:T(8,128)(2,1)S(1)} %get-tuple-element.146), channel_id=1, source_target_pairs={{0,1},{1,2},{2,3},{3,4},{4,5},{5,6},{6,7},{7,8},{8,9},{9,10},{10,1... | collective-permute-start | bytes 417800 | tf_op jit(solution)/shard_map/ppermute | solution.py:379
  (2 other events, 5.8 us)
